TPU v7x, 256 devices: a whole 4x4x8 slice. The times are simulated.
256 devices in a mesh: seq: 64 (over z_lo, x, y), tp: 4 (over z_hi, core).
Axes of the slice: x: 4, y: 4, z: 8 (z_hi: 2, z_lo: 4; z = z_hi * 4 + z_lo), core: 2. Of those that a mesh axis runs over, the one named last changes fastest.
Arguments:
- byte_states: bfloat16 [16384, 1024], P('seq'), may hold values from -6 to 6
- enc_gain: bfloat16 [1024], replicated, may hold values from 0.25 to 1.75
- enc_qkv: bfloat16 [3, 1024, 1024], P(None, None, 'tp')
- enc_proj_out: bfloat16 [1024, 1024], P('tp'), may hold values from -0.1875 to 0.1875
- starts: int32 [64, 64], P('seq'), may hold values from 0 to 16384, as said below
- counts: int32 [64], P('seq'), may hold values from 32 to 64, as said below
- lift: bfloat16 [1024, 4096], P(None, 'tp')
- cross_kv: bfloat16 [2, 1024, 4096], P(None, None, 'tp')
- latent_gain: bfloat16 [4096], replicated, may hold values from 0.25 to 1.75
- lat_qkv: bfloat16 [3, 4096, 2048], P(None, 'seq', 'tp')
- lat_proj_out: bfloat16 [2048, 4096], P('tp', 'seq'), may hold values from -0.75 to 0.75
Outputs:
- byte_out: bfloat16 [16384, 1024], P('seq')
- latent_out: bfloat16 [4096, 4096], P('seq', 'tp')
Inputs may be any that keep to these rules, and one draw needn't show every extreme that they name: `starts`: row s lists in increasing order the first byte (counted over all 16384 bytes) of each patch beginning in bytes s * 256 to (s + 1) * 256 - 1, then 16384 in unused places. Byte 0 begins a patch; every row's first patch begins fewer than 8 bytes into its block, and in some row exactly 7 bytes in. counts[s] is the number of patches listed in row s of starts; some row holds 64.
All inputs are finite; a program needn't handle non-finite values.
Results may differ from a plain program's by a relative error of at most 0.018.
Values may be sent and summed in bfloat16 or wider, within the bound.
No kernel may reach another device: no remote copies, remote signals or barrier semaphores. Data moves between devices by JAX's collectives and lax.ppermute only.
A program may use at most 128 MiB of HBM per device.

v0:
```python
import math

import jax
import jax.numpy as jnp
from jax import lax
from jax.experimental import pallas as pl
from jax.experimental.pallas import tpu as pltpu
from jax.sharding import Mesh
from jax.sharding import PartitionSpec as P

EH = 64
HD = 128
WIN = 512
SPILL = 8
EDGE = 16
ZL, RX, RY, ZH, CO = ("z_lo", "ring_x", "ring_y", "z_hi", "core")
SEQ = (ZL, RX, RY)
TP = (ZH, CO)
ROWS = (RX, RY)
COLUMN = (ZL, ZH, CO)

epsilon = 1e-05
rope_base = 500000.0
far_position = 1 << 30
bf16 = jnp.bfloat16
f32 = jnp.float32
i32 = jnp.int32
NT = (((1,), (1,)), ((), ()))


def shifted(value, axis, steps):
    count = lax.axis_size(axis)
    leading, last = (max(0, -steps), min(count, count - steps))
    return lax.ppermute(value, axis, [(source, source + steps) for source in range(leading, last)])


def exchanged(pieces, axis):
    return lax.all_to_all(pieces, axis, split_axis=0, concat_axis=0, tiled=True)


def swapped(value, axis):
    return lax.ppermute(value, axis, [(0, 1), (1, 0)])


def gathered(value, axis):
    return exchanged(jnp.broadcast_to(value, (lax.axis_size(axis), *value.shape)), axis)


def around_ring(value, axis):
    count = lax.axis_size(axis)
    return [value] + [
        lax.ppermute(value, axis, [((i + k) % count, i) for i in range(count)])
        for k in range(1, count)
    ]


def near_ring(value, axis):
    count = lax.axis_size(axis)

    def moved(part, step):
        return lax.ppermute(part, axis, [(i, (i + step) % count) for i in range(count)])

    up, down = (moved(value, 1), moved(value, -1))
    half = value.shape[0] // 2
    return [
        (value, 0, 0),
        (up, count - 1, 0),
        (down, 1, 0),
        (moved(up[:half], 1), 2, 0),
        (moved(down[half:], -1), 2, half),
    ]


def around_column(value):
    low, high = (lax.axis_size(ZL), lax.axis_size(ZH))
    count = low * high

    def moved(part, step):
        named = lambda z: z % count % low * high + z % count // low
        return lax.ppermute(part, (ZL, ZH), [(named(z), named(z + step)) for z in range(count)])

    pieces = [(value, 0, 0)]
    up = down = value
    for step in range(1, count // 2):
        up, down = (moved(up, 1), moved(down, -1))
        pieces += [(up, count - step, 0), (down, step, 0)]
    half = value.shape[0] // 2
    pieces += [(moved(up[:half], 1), count // 2, 0), (moved(down[half:], -1), count // 2, half)]
    return pieces


def on_chip(kernel, outs, scratch=(), limit=48, **extra):
    return pl.pallas_call(
        kernel,
        out_shape=outs,
        scratch_shapes=list(scratch),
        compiler_params=pltpu.CompilerParams(vmem_limit_bytes=limit << 20),
        cost_estimate=pl.CostEstimate(flops=1 << 20, transcendentals=0, bytes_accessed=1 << 20),
        **extra,
    )


def blank(shape, dtype=bf16):
    return jax.ShapeDtypeStruct(shape, dtype)


def encoder_heads(states, gain, weights):
    rows, width = states.shape
    share, _, inner = weights.shape

    def kernel(states_ref, gain_ref, weights_ref, query_ref, keys_values_ref):
        values = states_ref[...].astype(f32)
        factor = lax.rsqrt(jnp.mean(values * values, axis=-1, keepdims=True) + epsilon)
        normed = (values * factor * gain_ref[...].astype(f32)).astype(bf16)
        for i in range(1, share):
            keys_values_ref[:, (i - 1) * inner : i * inner] = jnp.dot(
                normed, weights_ref[i], preferred_element_type=f32
            ).astype(bf16)
        query_ref[...] = jnp.dot(normed, weights_ref[0], preferred_element_type=f32).astype(bf16)

    return on_chip(kernel, [blank((rows, inner)), blank((rows, (share - 1) * inner))])(
        states, gain.reshape(1, width), weights
    )


def encoder_attention(own_q, more_q, far, near, own, more, anchor):
    rows, width = own_q.shape
    total = rows + EDGE
    spans = WIN + total
    padded = -(-spans // 128) * 128

    def kernel(anchor_ref, q_ref, mq_ref, far_ref, near_ref, own_ref, more_ref, out_ref, held):
        at = 0
        for part in (far_ref, near_ref, own_ref, more_ref):
            held[at : at + part.shape[0], :] = part[...]
            at += part.shape[0]
        held[at:, :] = jnp.zeros((padded - at, 2 * width), bf16)
        queries = jnp.concatenate([q_ref[...], mq_ref[...]], axis=0)
        row = lax.broadcasted_iota(i32, (total, padded), 0)
        column = lax.broadcasted_iota(i32, (total, padded), 1)
        allowed = (
            (column - WIN <= row) & (column > row) & (column >= WIN - anchor_ref[0])
        )
        lane = lax.broadcasted_iota(i32, (total, HD), 1)
        for pair in range(width // HD):
            span = slice(pair * HD, (pair + 1) * HD)
            keys = held[:, span]
            values = held[:, width + pair * HD : width + (pair + 1) * HD]
            both = queries[:, span]
            done = None
            for side in range(HD // EH):
                mine = (lane >= side * EH) & (lane < (side + 1) * EH)
                query = jnp.where(mine, both, jnp.zeros_like(both))
                scores = lax.dot_general(query, keys, NT, preferred_element_type=f32)
                scores = jnp.where(allowed, scores * (1.0 / math.sqrt(EH)), -1e30)
                largest = jnp.max(scores, axis=-1, keepdims=True)
                raised = jnp.where(allowed, jnp.exp(scores - largest), 0.0)
                weights = (raised / jnp.maximum(jnp.sum(raised, axis=-1, keepdims=True), 1e-30))
                result = jnp.dot(weights.astype(bf16), values, preferred_element_type=f32)
                done = result if done is None else jnp.where(mine, result, done)
            out_ref[:, span] = done.astype(bf16)

    whole = pl.BlockSpec(memory_space=pltpu.VMEM)
    return on_chip(
        kernel,
        blank((total, width)),
        [pltpu.VMEM((padded, 2 * width), bf16)],
        in_specs=[pl.BlockSpec(memory_space=pltpu.SMEM)] + [whole] * 6,
        out_specs=whole,
    )(anchor.reshape(1), own_q, more_q, far, near, own, more)


def encoder_output(states, edge, attended, parts):
    rows, width = states.shape

    def kernel(states_ref, edge_ref, attended_ref, *refs):
        *part_refs, out_ref = refs
        here = lax.axis_index(TP)
        total = jnp.zeros((rows + EDGE, width), f32)
        for (_, turn, start), part in zip(parts, part_refs):
            deep = part.shape[0]
            piece = attended_ref[lax.bitwise_xor(here, turn), :, start : start + deep]
            total += jnp.dot(piece, part[...], preferred_element_type=f32)
        out_ref[:rows, :] = (states_ref[...].astype(f32) + total[:rows]).astype(bf16)
        out_ref[rows:, :] = (edge_ref[...].astype(f32) + total[rows:]).astype(bf16)

    return on_chip(kernel, blank((rows + EDGE, width)))(
        states, edge, attended, *(part for part, *_ in parts)
    )


def patch_block(extended, bounds, lift, cross_kv):
    spans = extended.shape[0]
    slots = bounds.shape[0]
    width = lift.shape[1]

    def kernel(extended_ref, bounds_ref, lift_ref, cross_ref, out_ref):
        column = lax.broadcasted_iota(i32, (slots, spans), 1)
        first, after, seen, used = (bounds_ref[:, k : k + 1] for k in range(4))
        rows = extended_ref[...]
        inside = (column >= first) & (column < after)
        allowed = (column >= first) & (column < seen)
        member = jnp.where(inside, 1.0, 0.0).astype(bf16)
        lengths = jnp.maximum(after - first, 1).astype(f32)
        pooled = (jnp.dot(member, rows, preferred_element_type=f32) / lengths).astype(bf16)
        lifted = jnp.dot(pooled, lift_ref[...], preferred_element_type=f32)
        query = lifted.astype(bf16)
        keys = jnp.dot(rows, cross_ref[0], preferred_element_type=f32).astype(bf16)
        values = jnp.dot(rows, cross_ref[1], preferred_element_type=f32).astype(bf16)
        for head in range(width // HD):
            span = slice(head * HD, (head + 1) * HD)
            scores = lax.dot_general(
                query[:, span], keys[:, span], NT, preferred_element_type=f32
            ) * (1.0 / math.sqrt(HD))
            scores = jnp.where(allowed, scores, -1e30)
            largest = jnp.max(scores, axis=-1, keepdims=True)
            raised = jnp.where(allowed, jnp.exp(scores - largest), 0.0)
            weights = (raised / jnp.sum(raised, axis=-1, keepdims=True)).astype(bf16)
            crossed = jnp.dot(weights, values[:, span], preferred_element_type=f32)
            total = jnp.where(used > 0, lifted[:, span] + crossed, 0.0)
            out_ref[:, span] = total.astype(bf16)

    return on_chip(kernel, blank((slots, width)))(extended, bounds, lift, cross_kv)


def placed_rows(pieces):
    rows, width = pieces[0][0].shape
    low, high = (lax.axis_size(ZL), lax.axis_size(ZH))

    def kernel(*refs):
        *parts, out_ref = refs
        here = lax.axis_index(ZH) * low + lax.axis_index(ZL)
        for part, (_, distance, shift) in zip(parts, pieces):
            z = lax.bitwise_and(here + distance, low * high - 1)
            across = lax.bitwise_and(z, low - 1) * rows + shift
            down = lax.shift_right_logical(z, low.bit_length() - 1) * width
            out_ref[
                pl.ds(pl.multiple_of(across, 16), part.shape[0]),
                pl.ds(pl.multiple_of(down, 128), width),
            ] = part[...]

    return on_chip(kernel, blank((low * rows, high * width)))(*(part for part, *_ in pieces))


def placed_weights(gathered_weights, first, columns, share, depth, step):
    groups = gathered_weights.shape[0]

    def kernel(weights_ref, out_ref):
        core = lax.axis_index(CO)
        for g in range(groups):
            for side in range(2):
                for high in range(columns // 2):
                    t = 2 * high + lax.bitwise_xor(core, side)
                    for i in range(share):
                        start = pl.multiple_of(first + t * step + i * depth, 16)
                        out_ref[
                            side, high, g * depth : (g + 1) * depth, i * HD : (i + 1) * HD
                        ] = weights_ref[g, pl.ds(start, depth), :]

    return on_chip(kernel, blank((2, columns // 2, groups * depth, share * HD)))(
        gathered_weights
    )


def latent_heads(own_rows, other_rows, weights, cosine, sine):
    rows, width = own_rows.shape
    full = 2 * width

    def kernel(own_ref, other_ref, weights_ref, cosine_ref, sine_ref, q_ref, k_ref, v_ref):
        squares = jnp.zeros((rows, 1), f32)
        total = jnp.zeros((rows, 3 * HD), f32)
        half = width // 2
        for side, part in enumerate((own_ref, other_ref)):
            for high in range(2):
                values = part[:, high * half : (high + 1) * half]
                wide = values.astype(f32)
                squares += jnp.sum(wide * wide, axis=1, keepdims=True)
                total += jnp.dot(values, weights_ref[side, high], preferred_element_type=f32)
        total = total * lax.rsqrt(squares / full + epsilon)
        for which, out_ref in enumerate((q_ref, k_ref)):
            value = total[:, which * HD : (which + 1) * HD]
            turned = value * cosine_ref[...] + pltpu.roll(value, HD // 2, 1) * sine_ref[...]
            out_ref[...] = turned.astype(bf16)
        v_ref[...] = total[:, 2 * HD :].astype(bf16)

    return on_chip(kernel, [blank((rows, HD))] * 3)(
        own_rows, other_rows, weights, cosine, sine
    )


def latent_attention(queries, keys, values, position, key_pos):
    rows = queries.shape[0]
    n_x, n_y = (len(keys), len(values))

    def kernel(*refs):
        q_ref, pos_ref, key_pos_ref = refs[:3]
        key_refs, value_refs = (refs[3 : 3 + n_x], refs[3 + n_x : 3 + n_x + n_y])
        out_ref, held = refs[3 + n_x + n_y :]
        query = q_ref[...]
        position = pos_ref[...]
        top = jnp.full((rows, rows), -1e30, f32)
        for x in range(n_x):
            for y in range(n_y):
                scores = lax.dot_general(
                    query, key_refs[x][y], NT, preferred_element_type=f32
                ) * (1.0 / math.sqrt(HD))
                allowed = key_pos_ref[x * n_y + y : x * n_y + y + 1, :] <= position
                scores = jnp.where(allowed, scores, -1e30)
                held[x * n_y + y] = scores
                top = jnp.maximum(top, scores)
        largest = jnp.max(top, axis=-1, keepdims=True)
        total = jnp.zeros((rows, rows), f32)
        weighted = jnp.zeros((rows, HD), f32)
        for x in range(n_x):
            for y in range(n_y):
                raised = jnp.exp(held[x * n_y + y] - largest)
                total += raised
                weighted += jnp.dot(
                    raised.astype(bf16), value_refs[y][x], preferred_element_type=f32
                )
        out_ref[...] = (weighted / jnp.sum(total, axis=-1, keepdims=True)).astype(bf16)

    return on_chip(
        kernel, blank((rows, HD)), [pltpu.VMEM((n_x * n_y, rows, rows), f32)]
    )(queries, position, key_pos, *keys, *values)


def partial_outputs(heads, weights):
    columns, rows, _ = heads.shape
    groups = weights.shape[0]
    slots = rows // columns
    cut = slots

    def kernel(heads_ref, weights_ref, *out_refs):
        here = lax.axis_index(TP)
        flat = [
            weights_ref[:, zl * cut : (zl + 1) * cut, :].reshape(groups * cut, HD)
            for zl in range(columns)
        ]
        for k, out_ref in enumerate(out_refs):
            start = lax.bitwise_and(here + k, columns - 1) * slots
            span = pl.ds(pl.multiple_of(start, slots), slots)
            total = jnp.zeros((slots, groups * cut), f32)
            for zl in range(columns):
                total += lax.dot_general(
                    heads_ref[zl, span, :], flat[zl], NT, preferred_element_type=f32
                )
            out_ref[...] = total.astype(bf16)

    block = (groups, columns * cut, HD)
    return on_chip(
        kernel,
        [blank((slots, groups * cut))] * columns,
        grid=(1,),
        in_specs=[
            pl.BlockSpec(heads.shape, lambda i: (0, 0, 0)),
            pl.BlockSpec(block, lambda i: (0, 0, 0)),
        ],
        out_specs=[pl.BlockSpec((slots, groups * cut), lambda i: (0, 0))] * columns,
    )(heads, weights)


def summed_outputs(pieces, patches, counts):
    def kernel(count_ref, patches_ref, *refs):
        *piece_refs, out_ref = refs
        total = patches_ref[...].astype(f32)
        for piece in piece_refs:
            total += piece[...].astype(f32)
        used = lax.broadcasted_iota(i32, total.shape, 0) < count_ref[0]
        out_ref[...] = jnp.where(used, total, 0.0).astype(bf16)

    whole = pl.BlockSpec(memory_space=pltpu.VMEM)
    return on_chip(
        kernel,
        blank(patches.shape),
        in_specs=[pl.BlockSpec(memory_space=pltpu.SMEM)] + [whole] * (1 + len(pieces)),
        out_specs=whole,
    )(counts, patches, *pieces)


def shards(
    byte_states,
    enc_gain,
    enc_qkv,
    enc_proj_out,
    starts,
    counts,
    lift,
    cross_kv,
    latent_gain,
    lat_qkv,
    lat_proj_out,
):
    byte_rows, byte_width = byte_states.shape
    slots = starts.shape[1]
    columns = lax.axis_size(ZL)
    tensor = lax.axis_size(TP)
    groups = lax.axis_size(ROWS)
    block = lax.axis_index(SEQ)
    anchor = block * byte_rows
    local_starts = starts[0]
    patch_count = counts[0]
    slot_ids = jnp.arange(slots, dtype=i32)
    in_use = slot_ids < patch_count

    own_q, own_kv = encoder_heads(byte_states, enc_gain, enc_qkv)
    far_kv = shifted(own_kv, SEQ, 2)
    near_kv = shifted(own_kv, SEQ, 1)

    first_local = (local_starts[0] - anchor).astype(bf16)
    edge = jnp.concatenate(
        [
            byte_states[:SPILL],
            jnp.broadcast_to(first_local, (EDGE - SPILL, byte_width)),
        ],
        axis=0,
    )
    edge = shifted(edge, SEQ, -1)

    share, depth, inner = lat_qkv.shape
    own_gain = lax.dynamic_slice_in_dim(latent_gain, block * depth, depth).astype(f32)
    scaled = (lat_qkv.astype(f32) * own_gain[:, None]).astype(bf16).reshape(share * depth, inner)
    mark = jnp.broadcast_to(counts.astype(bf16), (EDGE, HD))
    step = share * depth + EDGE
    by_head = jnp.concatenate(
        [part for k in range(columns) for part in (scaled[:, k * HD : (k + 1) * HD], mark)], axis=0
    ).reshape(columns, step, HD)
    by_head = exchanged(by_head, ZL).reshape(columns * step, HD)
    out_part = lat_proj_out.T
    cut = out_part.shape[0]
    out_part = [out_part[:, k * HD : (k + 1) * HD] for k in range(columns)]
    by_head = jnp.concatenate(out_part + [by_head], axis=0)

    half = enc_proj_out.shape[0] // 2
    high_a, high_b = (swapped(enc_proj_out[at : at + half], ZH) for at in (0, half))
    out_side = swapped(enc_proj_out, CO)

    near_kv, by_head, edge, out_side = lax.optimization_barrier(
        (near_kv, by_head, edge, out_side)
    )
    far_kv, high_a = lax.optimization_barrier((far_kv, high_a))
    by_head = gathered(by_head, ROWS)
    next_first = edge[SPILL, 0].astype(i32)
    more_q, more_kv = encoder_heads(edge, enc_gain, enc_qkv)
    attended = encoder_attention(own_q, more_q, far_kv, near_kv, own_kv, more_kv, anchor)
    both_a = swapped(high_a, CO)
    attended, high_b, both_a = lax.optimization_barrier((attended, high_b, both_a))
    both_b = swapped(high_b, CO)
    attended = lax.all_gather(attended, TP)
    extended = encoder_output(
        byte_states,
        edge,
        attended,
        (
            (enc_proj_out, 0, 0),
            (out_side, 1, 0),
            (high_a, 2, 0),
            (both_a, 3, 0),
            (high_b, 2, half),
            (both_b, 3, half),
        ),
    )
    encoded = extended[:byte_rows]

    following = jnp.concatenate([local_starts[1:], jnp.zeros((1,), i32)])
    patch_end = jnp.where(slot_ids + 1 < patch_count, following, anchor + byte_rows + next_first)
    first, after = (jnp.where(in_use, end - anchor, 0) for end in (local_starts, patch_end))
    used = in_use.astype(i32)
    bounds = jnp.stack([first, after, jnp.where(in_use, after, 1), used], axis=1)
    patches = patch_block(extended, bounds, lift, cross_kv)
    grid = (*(lax.axis_size(name) for name in ROWS), columns)
    here = tuple(lax.axis_index(name) for name in ROWS)
    all_counts = jnp.stack(
        [by_head[:, columns * cut + (k + 1) * step - 1, 0] for k in range(columns)], axis=1
    )
    all_counts = all_counts.astype(i32).reshape(*grid)
    all_counts = lax.dynamic_slice(jnp.tile(all_counts, (2, 2, 1)), (*here, 0), grid)
    order = sum(
        stride
        * lax.bitwise_and(lax.broadcasted_iota(i32, grid, dim) + start, grid[dim] - 1)
        for dim, stride, start in ((0, grid[1], here[0]), (1, 1, here[1]), (2, groups, 0))
    ).reshape(-1)
    flat_counts = all_counts.reshape(-1)
    offsets = jnp.sum(jnp.where(order[None, :] < order[:, None], flat_counts[None, :], 0), axis=1)
    position = (offsets[:columns, None] + slot_ids[None, :]).reshape(-1)
    key_pos = jnp.where(
        slot_ids[None, :] < flat_counts[:, None], offsets[:, None] + slot_ids[None, :], far_position
    ).reshape(groups, columns * slots)
    halfway = HD // 2
    frequency = jnp.power(rope_base, -2.0 * jnp.arange(halfway, dtype=f32) / HD)
    angles = position.astype(f32)[:, None] * frequency[None, :]
    cosine, sine = (jnp.cos(angles), jnp.sin(angles))
    cosine = jnp.concatenate([cosine, cosine], axis=1)
    sine = jnp.concatenate([-sine, sine], axis=1)
    latent_in = placed_weights(by_head, columns * cut, columns, share, depth, step)

    own_rows = placed_rows(around_column(patches))
    own_rows, latent_in = lax.optimization_barrier((own_rows, latent_in))
    other_rows = swapped(own_rows, CO)
    queries, keys, values = latent_heads(own_rows, other_rows, latent_in, cosine, sine)
    keys = around_ring(jnp.stack(around_ring(keys, RY)), RX)
    values = around_ring(jnp.stack(around_ring(values, RX)), RY)
    heads = latent_attention(queries, keys, values, position[:, None], key_pos)

    partial = partial_outputs(lax.all_gather(heads, ZL), by_head)
    partial = [
        lax.ppermute(
            piece,
            COLUMN,
            [
                (a * tensor + b, (b + k) % columns * tensor + a)
                for a in range(columns)
                for b in range(tensor)
            ],
        )
        for k, piece in enumerate(partial)
    ]
    latent = summed_outputs(partial, patches, counts)
    return (encoded, latent)


def solution(mesh):
    finer = Mesh(mesh.devices.reshape(4, 4, 4, 2, 2), (*SEQ, *TP))
    in_specs = (
        P(SEQ, None),
        P(),
        P(None, None, TP),
        P(TP, None),
        P(SEQ, None),
        P(SEQ),
        P(None, TP),
        P(None, None, TP),
        P(),
        P(None, SEQ, TP),
        P(TP, SEQ),
    )
    out_specs = (P(SEQ, None), P(SEQ, TP))
    return jax.shard_map(
        shards, mesh=finer, in_specs=in_specs, out_specs=out_specs, check_vma=False
    )
```

profile of v0, /device:TPU:1, one launch (start us, length us, event | category | flops | bytes accessed | tf_op | source)
XLA Modules:
  0.0 261.3 jit_solution(864997536471612869)
XLA Ops:
  8.0 6.4 %all-to-all-start = ((bf16[4,208,128]{2,1,0:T(8,128)(2,1)}), bf16[4,208,128]{2,1,0:T(8,128)(2,1)S(1)}, u32[]{:S(2)}, u32[]{:S(2)}) async-start(bf16[4,208,128]{2,1,0:T(8,128)(2,1)} %bitcast.3), calls=%async_computation | async-start | bytes 425984 | tf_op jit(solution)/shard_map/all_to_all | solution.py:38
  22.4 4.0 %collective-permute-start = (bf16[256,512]{1,0:T(8,128)(2,1)}, bf16[256,512]{1,0:T(8,128)(2,1)S(1)}, u32[]{:S(2)}, u32[]{:S(2)}) collective-permute-start(bf16[256,512]{1,0:T(8,128)(2,1)} %get-tuple-element.24.own_ref), channel_id=1, source_target_pairs={{0,4},{4,8},{8,12},{12,16},{16,20},{20,24},{24,28},{28,32},{32,36}... | collective-permute-start | bytes 786440 | tf_op jit(solution)/shard_map/ppermute | solution.py:34
  31.7 3.0 %broadcast_in_dim.47 = bf16[16,1088,128]{2,1,0:T(8,128)(2,1)} broadcast(bf16[1088,128]{1,0:T(8,128)(2,1)S(1)} %constant_dynamic-update-slice_fusion.4), dimensions={1,2} | broadcast | bytes 4734976 | tf_op jit(solution)/shard_map/broadcast_in_dim | solution.py:46
  34.7 10.7 %all-to-all-start.1 = ((bf16[16,1088,128]{2,1,0:T(8,128)(2,1)}), bf16[16,1088,128]{2,1,0:T(8,128)(2,1)}, u32[]{:S(2)}, u32[]{:S(2)}) async-start(bf16[16,1088,128]{2,1,0:T(8,128)(2,1)} %broadcast_in_dim.47), calls=%async_computation.1 | async-start | bytes 8912896 | tf_op jit(solution)/shard_map/all_to_all | solution.py:38
  45.4 4.9 %collective-permute-start.3 = (bf16[256,512]{1,0:T(8,128)(2,1)}, bf16[256,512]{1,0:T(8,128)(2,1)S(1)}, u32[]{:S(2)}, u32[]{:S(2)}) collective-permute-start(bf16[256,512]{1,0:T(8,128)(2,1)} %get-tuple-element.24.own_ref), channel_id=1, source_target_pairs={{0,8},{4,12},{8,16},{12,20},{16,24},{20,28},{24,32},{28,36},{32,40... | collective-permute-start | bytes 786440 | tf_op jit(solution)/shard_map/ppermute | solution.py:34
  51.1 5.0 %collective-permute-start.4 = (bf16[128,1024]{1,0:T(8,128)(2,1)S(1)}, bf16[128,1024]{1,0:T(8,128)(2,1)S(1)}, u32[]{:S(2)}, u32[]{:S(2)}) collective-permute-start(bf16[128,1024]{1,0:T(8,128)(2,1)S(1)} %get-tuple-element.53), channel_id=1, source_target_pairs={{0,2},{2,0},{1,3},{3,1},{4,6},{6,4},{5,7},{7,5},{8,10},{10,8},{9,1... | collective-permute-start | bytes 786440 | tf_op jit(solution)/shard_map/ppermute | solution.py:42
  56.4 44.3 %collective-permute-done.3.far_ref = bf16[256,512]{1,0:T(8,128)(2,1)S(1)} collective-permute-done((bf16[256,512]{1,0:T(8,128)(2,1)}, bf16[256,512]{1,0:T(8,128)(2,1)S(1)}, u32[]{:S(2)}, u32[]{:S(2)}) %collective-permute-start.3) | collective-permute-done | bytes 262176 | tf_op jit(solution)/shard_map/ppermute | solution.py:34
  101.5 5.2 %collective-permute-start.6 = (bf16[128,1024]{1,0:T(8,128)(2,1)S(1)}, bf16[128,1024]{1,0:T(8,128)(2,1)}, u32[]{:S(2)}, u32[]{:S(2)}) collective-permute-start(bf16[128,1024]{1,0:T(8,128)(2,1)S(1)} %collective-permute-done.4.refs_2_), channel_id=1, source_target_pairs={{0,1},{1,0},{2,3},{3,2},{4,5},{5,4},{6,7},{7,6},{8,9},{9,8},{10,11... | collective-permute-start | bytes 786440 | tf_op jit(solution)/shard_map/ppermute | solution.py:42
  111.0 3.0 %shard_map.124 = bf16[272,256]{1,0:T(8,128)(2,1)S(1)} custom-call(s32[1]{0:T(128)} %bitcast.6.anchor_ref, bf16[256,256]{1,0:T(8,128)(2,1)S(1)} %copy-done.13, bf16[16,256]{1,0:T(8,128)(2,1)S(1)} %get-tuple-element.27.mq_ref, bf16[256,512]{1,0:T(8,128)(2,1)S(1)} %copy-done.11, bf16[256,512]{1,0:T(8,128)(2,1)S(1)} %copy-done.9, ...), custom_call_target="tpu_custom_call" | custom-call | flops 1048576 | bytes 1048576 | tf_op jit(solution)/shard_map/pallas_call | solution.py:164
  114.3 12.0 %all-gather = bf16[1088,256]{1,0:T(8,128)(2,1)S(1)} all-gather(bf16[272,256]{1,0:T(8,128)(2,1)S(1)} %shard_map.124), channel_id=2, replica_groups=mesh['z_lo'=4,'ring_x'=4,'ring_y'=4,'z_hi'=2,'core'=2] {'z_hi','core'}, dimensions={0}, use_global_device_ids=true | all-gather | bytes 696320 | tf_op jit(solution)/shard_map/all_gather | solution.py:449
  128.4 6.8 %shard_map.126.refs_0_.patches_ref = bf16[64,1024]{1,0:T(8,128)(2,1)S(1)} custom-call(bf16[272,1024]{1,0:T(8,128)(2,1)S(1)} %shard_map.125.extended_ref, s32[64,4]{1,0:T(8,128)S(1)} %copy.26.bounds_ref, bf16[1024,1024]{1,0:T(8,128)(2,1)S(1)} %copy-done.7, bf16[2,1024,1024]{2,1,0:T(8,128)(2,1)} %cross_ref.1), custom_call_target="tpu_custom_call" | custom-call | flops 1048576 | bytes 1048576 | tf_op jit(solution)/shard_map/pallas_call | solution.py:223
  136.0 5.5 %collective-permute-start.8 = (bf16[64,1024]{1,0:T(8,128)(2,1)S(1)}, bf16[64,1024]{1,0:T(8,128)(2,1)S(1)}, u32[]{:S(2)}, u32[]{:S(2)}) collective-permute-start(bf16[64,1024]{1,0:T(8,128)(2,1)S(1)} %shard_map.126.refs_0_.patches_ref), channel_id=1, source_target_pairs={{0,64},{64,128},{128,192},{192,2},{2,66},{66,130},{130,194},{194,0... | collective-permute-start | bytes 393224 | tf_op jit(solution)/shard_map/ppermute | solution.py:80
  141.5 4.5 %collective-permute-start.9 = (bf16[64,1024]{1,0:T(8,128)(2,1)S(1)}, bf16[64,1024]{1,0:T(8,128)(2,1)S(1)}, u32[]{:S(2)}, u32[]{:S(2)}) collective-permute-start(bf16[64,1024]{1,0:T(8,128)(2,1)S(1)} %shard_map.126.refs_0_.patches_ref), channel_id=1, source_target_pairs={{0,194},{64,0},{128,64},{192,128},{2,192},{66,2},{130,66},{194,130... | collective-permute-start | bytes 393224 | tf_op jit(solution)/shard_map/ppermute | solution.py:80
  146.0 3.7 %collective-permute-done.8.refs_1_ = bf16[64,1024]{1,0:T(8,128)(2,1)S(1)} collective-permute-done((bf16[64,1024]{1,0:T(8,128)(2,1)S(1)}, bf16[64,1024]{1,0:T(8,128)(2,1)S(1)}, u32[]{:S(2)}, u32[]{:S(2)}) %collective-permute-start.8) | collective-permute-done | bytes 131104 | tf_op jit(solution)/shard_map/ppermute | solution.py:80
  149.7 2.7 %collective-permute-start.11 = (bf16[64,1024]{1,0:T(8,128)(2,1)S(1)}, bf16[64,1024]{1,0:T(8,128)(2,1)S(1)}, u32[]{:S(2)}, u32[]{:S(2)}) collective-permute-start(bf16[64,1024]{1,0:T(8,128)(2,1)S(1)} %collective-permute-done.9.refs_2_), channel_id=1, source_target_pairs={{0,194},{64,0},{128,64},{192,128},{2,192},{66,2},{130,66},{194,130... | collective-permute-start | bytes 393224 | tf_op jit(solution)/shard_map/ppermute | solution.py:80
  152.4 2.8 %collective-permute-done.10.refs_3_ = bf16[64,1024]{1,0:T(8,128)(2,1)S(1)} collective-permute-done((bf16[64,1024]{1,0:T(8,128)(2,1)S(1)}, bf16[64,1024]{1,0:T(8,128)(2,1)S(1)}, u32[]{:S(2)}, u32[]{:S(2)}) %collective-permute-start.10) | collective-permute-done | bytes 131104 | tf_op jit(solution)/shard_map/ppermute | solution.py:80
  155.2 2.7 %collective-permute-start.13 = (bf16[64,1024]{1,0:T(8,128)(2,1)S(1)}, bf16[64,1024]{1,0:T(8,128)(2,1)S(1)}, u32[]{:S(2)}, u32[]{:S(2)}) collective-permute-start(bf16[64,1024]{1,0:T(8,128)(2,1)S(1)} %collective-permute-done.11.refs_4_), channel_id=1, source_target_pairs={{0,194},{64,0},{128,64},{192,128},{2,192},{66,2},{130,66},{194,130... | collective-permute-start | bytes 393224 | tf_op jit(solution)/shard_map/ppermute | solution.py:80
  160.3 2.7 %collective-permute-start.15 = (bf16[32,1024]{1,0:T(8,128)(2,1)S(1)}, bf16[32,1024]{1,0:T(8,128)(2,1)S(1)}, u32[]{:S(2)}, u32[]{:S(2)}) collective-permute-start(bf16[32,1024]{1,0:T(8,128)(2,1)S(1)} %slice.101), channel_id=1, source_target_pairs={{0,194},{64,0},{128,64},{192,128},{2,192},{66,2},{130,66},{194,130... | collective-permute-start | bytes 196616 | tf_op jit(solution)/shard_map/ppermute | solution.py:80
  165.6 2.8 %shard_map.128.weights_ref = bf16[2,2,1024,384]{3,2,1,0:T(8,128)(2,1)S(1)} custom-call(bf16[16,1088,128]{2,1,0:T(8,128)(2,1)} %all-to-all-done.1.weights_ref), custom_call_target="tpu_custom_call" | custom-call | flops 1048576 | bytes 1048576 | tf_op jit(solution)/shard_map/pallas_call | solution.py:260
  168.4 4.0 %collective-permute-start.16 = (bf16[256,2048]{1,0:T(8,128)(2,1)}, bf16[256,2048]{1,0:T(8,128)(2,1)}, u32[]{:S(2)}, u32[]{:S(2)}) collective-permute-start(bf16[256,2048]{1,0:T(8,128)(2,1)} %shard_map.127.own_ref), channel_id=1, source_target_pairs={{0,1},{1,0},{2,3},{3,2},{4,5},{5,4},{6,7},{7,6},{8,9},{9,8},{10,11... | collective-permute-start | bytes 3145736 | tf_op jit(solution)/shard_map/ppermute | solution.py:42
  175.3 3.0 %shard_map.129 = (bf16[256,128]{1,0:T(8,128)(2,1)S(1)}, bf16[256,128]{1,0:T(8,128)(2,1)S(1)}, bf16[256,128]{1,0:T(8,128)(2,1)S(1)}) custom-call(bf16[256,2048]{1,0:T(8,128)(2,1)} %shard_map.127.own_ref, bf16[256,2048]{1,0:T(8,128)(2,1)} %collective-permute-done.16.other_ref, bf16[2,2,1024,384]{3,2,1,0:T(8,128)(2,1)S(1)} %shard_map.128.weights_ref, ...), custom_call_target="tpu_custom_call" | custom-call | flops 1048576 | bytes 1048576 | tf_op jit(solution)/shard_map/pallas_call | solution.py:286
  178.3 4.9 %collective-permute-start.23 = (bf16[256,128]{1,0:T(8,128)(2,1)S(1)}, bf16[256,128]{1,0:T(8,128)(2,1)S(1)}, u32[]{:S(2)}, u32[]{:S(2)}) collective-permute-start(bf16[256,128]{1,0:T(8,128)(2,1)S(1)} %get-tuple-element.41), channel_id=1, source_target_pairs={{16,0},{32,16},{48,32},{0,48},{17,1},{33,17},{49,33},{1,49},{18,2}... | collective-permute-start | bytes 196616 | tf_op jit(solution)/shard_map/ppermute | solution.py:52
  183.9 2.1 collective-permute-done.23
  189.8 3.1 %collective-permute-start.18 = (bf16[256,128]{1,0:T(8,128)(2,1)S(1)}, bf16[256,128]{1,0:T(8,128)(2,1)S(1)}, u32[]{:S(2)}, u32[]{:S(2)}) collective-permute-start(bf16[256,128]{1,0:T(8,128)(2,1)S(1)} %get-tuple-element.40), channel_id=1, source_target_pairs={{8,0},{12,4},{0,8},{4,12},{9,1},{13,5},{1,9},{5,13},{10,2},{14,6},... | collective-permute-start | bytes 196616 | tf_op jit(solution)/shard_map/ppermute | solution.py:52
  194.9 3.4 %collective-permute-done.17 = bf16[256,128]{1,0:T(8,128)(2,1)S(1)} collective-permute-done((bf16[256,128]{1,0:T(8,128)(2,1)S(1)}, bf16[256,128]{1,0:T(8,128)(2,1)S(1)}, u32[]{:S(2)}, u32[]{:S(2)}) %collective-permute-start.17) | collective-permute-done | bytes 65568 | tf_op jit(solution)/shard_map/ppermute | solution.py:52
  198.2 7.9 %collective-permute-start.28 = (bf16[4,256,128]{2,1,0:T(8,128)(2,1)S(1)}, bf16[4,256,128]{2,1,0:T(8,128)(2,1)S(1)}, u32[]{:S(2)}, u32[]{:S(2)}) collective-permute-start(bf16[4,256,128]{2,1,0:T(8,128)(2,1)S(1)} %pad_maximum_fusion.1.refs_7_), channel_id=1, source_target_pairs={{12,0},{0,4},{4,8},{8,12},{13,1},{1,5},{5,9},{9,13},{14,2},{2,6},{... | collective-permute-start | bytes 786440 | tf_op jit(solution)/shard_map/ppermute | solution.py:52
  213.5 8.0 %collective-permute-done.22.refs_6_ = bf16[4,256,128]{2,1,0:T(8,128)(2,1)S(1)} collective-permute-done((bf16[4,256,128]{2,1,0:T(8,128)(2,1)S(1)}, bf16[4,256,128]{2,1,0:T(8,128)(2,1)S(1)}, u32[]{:S(2)}, u32[]{:S(2)}) %collective-permute-start.22) | collective-permute-done | bytes 262176 | tf_op jit(solution)/shard_map/ppermute | solution.py:52
  223.6 13.6 %all-gather.1 = bf16[1024,128]{1,0:T(8,128)(2,1)S(1)} all-gather(bf16[256,128]{1,0:T(8,128)(2,1)S(1)} %shard_map.130), channel_id=3, replica_groups=mesh['z_lo'=4,'ring_x'=4,'ring_y'=4,'z_hi'=2,'core'=2] {'z_lo'}, dimensions={0}, use_global_device_ids=true | all-gather | bytes 327680 | tf_op jit(solution)/shard_map/all_gather | solution.py:505
  237.2 2.8 %shard_map.131 = (bf16[64,1024]{1,0:T(8,128)(2,1)S(1)}, bf16[64,1024]{1,0:T(8,128)(2,1)S(1)}, bf16[64,1024]{1,0:T(8,128)(2,1)S(1)}, bf16[64,1024]{1,0:T(8,128)(2,1)S(1)}) custom-call(bf16[4,256,128]{2,1,0:T(8,128)(2,1)S(1)} %bitcast.32, bf16[16,1088,128]{2,1,0:T(8,128)(2,1)} %all-to-all-done.1.weights_ref), custom_call_target="tpu_custom_call" | custom-call | flops 1048576 | bytes 1048576 | tf_op jit(solution)/shard_map/pallas_call | solution.py:351
  240.0 6.5 %collective-permute-start.29 = (bf16[64,1024]{1,0:T(8,128)(2,1)S(1)}, bf16[64,1024]{1,0:T(8,128)(2,1)S(1)}, u32[]{:S(2)}, u32[]{:S(2)}) collective-permute-start(bf16[64,1024]{1,0:T(8,128)(2,1)S(1)} %get-tuple-element.42), channel_id=1, source_target_pairs={{0,0},{1,64},{2,128},{3,192},{64,1},{65,65},{66,129},{67,193},{128... | collective-permute-start | bytes 393224 | tf_op jit(solution)/shard_map/ppermute | solution.py:507
  249.4 8.2 %collective-permute-done.30.refs_1_ = bf16[64,1024]{1,0:T(8,128)(2,1)S(1)} collective-permute-done((bf16[64,1024]{1,0:T(8,128)(2,1)S(1)}, bf16[64,1024]{1,0:T(8,128)(2,1)S(1)}, u32[]{:S(2)}, u32[]{:S(2)}) %collective-permute-start.30) | collective-permute-done | bytes 131104 | tf_op jit(solution)/shard_map/ppermute | solution.py:507
  257.6 3.0 %collective-permute-done.31.refs_2_ = bf16[64,1024]{1,0:T(8,128)(2,1)S(1)} collective-permute-done((bf16[64,1024]{1,0:T(8,128)(2,1)S(1)}, bf16[64,1024]{1,0:T(8,128)(2,1)S(1)}, u32[]{:S(2)}, u32[]{:S(2)}) %collective-permute-start.31) | collective-permute-done | bytes 131104 | tf_op jit(solution)/shard_map/ppermute | solution.py:507
  (144 shorter events, 55.3 us)
Async XLA Ops:
  8.0 22.9 %all-to-all-start = ((bf16[4,208,128]{2,1,0:T(8,128)(2,1)}), bf16[4,208,128]{2,1,0:T(8,128)(2,1)S(1)}, u32[]{:S(2)}, u32[]{:S(2)}) async-start(bf16[4,208,128]{2,1,0:T(8,128)(2,1)} %bitcast.3), calls=%async_computation | async-start | bytes 425984 | tf_op jit(solution)/shard_map/all_to_all | solution.py:38
  15.9 15.0 %collective-permute-start.1 = (bf16[16,1024]{1,0:T(8,128)(2,1)S(1)}, bf16[16,1024]{1,0:T(8,128)(2,1)S(1)}, u32[]{:S(2)}, u32[]{:S(2)}) collective-permute-start(bf16[16,1024]{1,0:T(8,128)(2,1)S(1)} %slice_select_fusion), channel_id=1, source_target_pairs={{4,0},{8,4},{12,8},{16,12},{20,16},{24,20},{28,24},{32,28},{36,32}... | collective-permute-start | bytes 98312 | tf_op jit(solution)/shard_map/ppermute | solution.py:34
  22.4 8.6 %collective-permute-start = (bf16[256,512]{1,0:T(8,128)(2,1)}, bf16[256,512]{1,0:T(8,128)(2,1)S(1)}, u32[]{:S(2)}, u32[]{:S(2)}) collective-permute-start(bf16[256,512]{1,0:T(8,128)(2,1)} %get-tuple-element.24.own_ref), channel_id=1, source_target_pairs={{0,4},{4,8},{8,12},{12,16},{16,20},{20,24},{24,28},{28,32},{32,36}... | collective-permute-start | bytes 786440 | tf_op jit(solution)/shard_map/ppermute | solution.py:34
  26.4 5.3 %collective-permute-start.2 = (bf16[256,1024]{1,0:T(8,128)(2,1)}, bf16[256,1024]{1,0:T(8,128)(2,1)S(1)}, u32[]{:S(2)}, u32[]{:S(2)}) collective-permute-start(bf16[256,1024]{1,0:T(8,128)(2,1)} %refs_0_.1), channel_id=1, source_target_pairs={{0,1},{1,0},{2,3},{3,2},{4,5},{5,4},{6,7},{7,6},{8,9},{9,8},{10,11... | collective-permute-start | bytes 1572872 | tf_op jit(solution)/shard_map/ppermute | solution.py:42
  34.7 130.9 %all-to-all-start.1 = ((bf16[16,1088,128]{2,1,0:T(8,128)(2,1)}), bf16[16,1088,128]{2,1,0:T(8,128)(2,1)}, u32[]{:S(2)}, u32[]{:S(2)}) async-start(bf16[16,1088,128]{2,1,0:T(8,128)(2,1)} %broadcast_in_dim.47), calls=%async_computation.1 | async-start | bytes 8912896 | tf_op jit(solution)/shard_map/all_to_all | solution.py:38
  45.4 55.4 %collective-permute-start.3 = (bf16[256,512]{1,0:T(8,128)(2,1)}, bf16[256,512]{1,0:T(8,128)(2,1)S(1)}, u32[]{:S(2)}, u32[]{:S(2)}) collective-permute-start(bf16[256,512]{1,0:T(8,128)(2,1)} %get-tuple-element.24.own_ref), channel_id=1, source_target_pairs={{0,8},{4,12},{8,16},{12,20},{16,24},{20,28},{24,32},{28,36},{32,40... | collective-permute-start | bytes 786440 | tf_op jit(solution)/shard_map/ppermute | solution.py:34
  51.1 50.4 %collective-permute-start.4 = (bf16[128,1024]{1,0:T(8,128)(2,1)S(1)}, bf16[128,1024]{1,0:T(8,128)(2,1)S(1)}, u32[]{:S(2)}, u32[]{:S(2)}) collective-permute-start(bf16[128,1024]{1,0:T(8,128)(2,1)S(1)} %get-tuple-element.53), channel_id=1, source_target_pairs={{0,2},{2,0},{1,3},{3,1},{4,6},{6,4},{5,7},{7,5},{8,10},{10,8},{9,1... | collective-permute-start | bytes 786440 | tf_op jit(solution)/shard_map/ppermute | solution.py:42
  56.0 58.0 %collective-permute-start.5 = (bf16[128,1024]{1,0:T(8,128)(2,1)}, bf16[128,1024]{1,0:T(8,128)(2,1)}, u32[]{:S(2)}, u32[]{:S(2)}) collective-permute-start(bf16[128,1024]{1,0:T(8,128)(2,1)} %get-tuple-element.52), channel_id=1, source_target_pairs={{0,2},{2,0},{1,3},{3,1},{4,6},{6,4},{5,7},{7,5},{8,10},{10,8},{9,1... | collective-permute-start | bytes 786440 | tf_op jit(solution)/shard_map/ppermute | solution.py:42
  101.5 12.5 %collective-permute-start.6 = (bf16[128,1024]{1,0:T(8,128)(2,1)S(1)}, bf16[128,1024]{1,0:T(8,128)(2,1)}, u32[]{:S(2)}, u32[]{:S(2)}) collective-permute-start(bf16[128,1024]{1,0:T(8,128)(2,1)S(1)} %collective-permute-done.4.refs_2_), channel_id=1, source_target_pairs={{0,1},{1,0},{2,3},{3,2},{4,5},{5,4},{6,7},{7,6},{8,9},{9,8},{10,11... | collective-permute-start | bytes 786440 | tf_op jit(solution)/shard_map/ppermute | solution.py:42
  114.0 12.4 %collective-permute-start.7 = (bf16[128,1024]{1,0:T(8,128)(2,1)}, bf16[128,1024]{1,0:T(8,128)(2,1)S(1)}, u32[]{:S(2)}, u32[]{:S(2)}) collective-permute-start(bf16[128,1024]{1,0:T(8,128)(2,1)} %collective-permute-done.5.refs_4_), channel_id=1, source_target_pairs={{0,1},{1,0},{2,3},{3,2},{4,5},{5,4},{6,7},{7,6},{8,9},{9,8},{10,11... | collective-permute-start | bytes 786440 | tf_op jit(solution)/shard_map/ppermute | solution.py:42
  136.0 13.7 %collective-permute-start.8 = (bf16[64,1024]{1,0:T(8,128)(2,1)S(1)}, bf16[64,1024]{1,0:T(8,128)(2,1)S(1)}, u32[]{:S(2)}, u32[]{:S(2)}) collective-permute-start(bf16[64,1024]{1,0:T(8,128)(2,1)S(1)} %shard_map.126.refs_0_.patches_ref), channel_id=1, source_target_pairs={{0,64},{64,128},{128,192},{192,2},{2,66},{66,130},{130,194},{194,0... | collective-permute-start | bytes 393224 | tf_op jit(solution)/shard_map/ppermute | solution.py:80
  141.5 8.2 %collective-permute-start.9 = (bf16[64,1024]{1,0:T(8,128)(2,1)S(1)}, bf16[64,1024]{1,0:T(8,128)(2,1)S(1)}, u32[]{:S(2)}, u32[]{:S(2)}) collective-permute-start(bf16[64,1024]{1,0:T(8,128)(2,1)S(1)} %shard_map.126.refs_0_.patches_ref), channel_id=1, source_target_pairs={{0,194},{64,0},{128,64},{192,128},{2,192},{66,2},{130,66},{194,130... | collective-permute-start | bytes 393224 | tf_op jit(solution)/shard_map/ppermute | solution.py:80
  149.7 5.5 %collective-permute-start.10 = (bf16[64,1024]{1,0:T(8,128)(2,1)S(1)}, bf16[64,1024]{1,0:T(8,128)(2,1)S(1)}, u32[]{:S(2)}, u32[]{:S(2)}) collective-permute-start(bf16[64,1024]{1,0:T(8,128)(2,1)S(1)} %collective-permute-done.8.refs_1_), channel_id=1, source_target_pairs={{0,64},{64,128},{128,192},{192,2},{2,66},{66,130},{130,194},{194,0... | collective-permute-start | bytes 393224 | tf_op jit(solution)/shard_map/ppermute | solution.py:80
  149.7 5.5 %collective-permute-start.11 = (bf16[64,1024]{1,0:T(8,128)(2,1)S(1)}, bf16[64,1024]{1,0:T(8,128)(2,1)S(1)}, u32[]{:S(2)}, u32[]{:S(2)}) collective-permute-start(bf16[64,1024]{1,0:T(8,128)(2,1)S(1)} %collective-permute-done.9.refs_2_), channel_id=1, source_target_pairs={{0,194},{64,0},{128,64},{192,128},{2,192},{66,2},{130,66},{194,130... | collective-permute-start | bytes 393224 | tf_op jit(solution)/shard_map/ppermute | solution.py:80
  155.2 5.0 %collective-permute-start.12 = (bf16[64,1024]{1,0:T(8,128)(2,1)S(1)}, bf16[64,1024]{1,0:T(8,128)(2,1)S(1)}, u32[]{:S(2)}, u32[]{:S(2)}) collective-permute-start(bf16[64,1024]{1,0:T(8,128)(2,1)S(1)} %collective-permute-done.10.refs_3_), channel_id=1, source_target_pairs={{0,64},{64,128},{128,192},{192,2},{2,66},{66,130},{130,194},{194,0... | collective-permute-start | bytes 393224 | tf_op jit(solution)/shard_map/ppermute | solution.py:80
  155.2 5.0 %collective-permute-start.13 = (bf16[64,1024]{1,0:T(8,128)(2,1)S(1)}, bf16[64,1024]{1,0:T(8,128)(2,1)S(1)}, u32[]{:S(2)}, u32[]{:S(2)}) collective-permute-start(bf16[64,1024]{1,0:T(8,128)(2,1)S(1)} %collective-permute-done.11.refs_4_), channel_id=1, source_target_pairs={{0,194},{64,0},{128,64},{192,128},{2,192},{66,2},{130,66},{194,130... | collective-permute-start | bytes 393224 | tf_op jit(solution)/shard_map/ppermute | solution.py:80
  168.4 6.9 %collective-permute-start.16 = (bf16[256,2048]{1,0:T(8,128)(2,1)}, bf16[256,2048]{1,0:T(8,128)(2,1)}, u32[]{:S(2)}, u32[]{:S(2)}) collective-permute-start(bf16[256,2048]{1,0:T(8,128)(2,1)} %shard_map.127.own_ref), channel_id=1, source_target_pairs={{0,1},{1,0},{2,3},{3,2},{4,5},{5,4},{6,7},{7,6},{8,9},{9,8},{10,11... | collective-permute-start | bytes 3145736 | tf_op jit(solution)/shard_map/ppermute | solution.py:42
  178.3 7.7 %collective-permute-start.23 = (bf16[256,128]{1,0:T(8,128)(2,1)S(1)}, bf16[256,128]{1,0:T(8,128)(2,1)S(1)}, u32[]{:S(2)}, u32[]{:S(2)}) collective-permute-start(bf16[256,128]{1,0:T(8,128)(2,1)S(1)} %get-tuple-element.41), channel_id=1, source_target_pairs={{16,0},{32,16},{48,32},{0,48},{17,1},{33,17},{49,33},{1,49},{18,2}... | collective-permute-start | bytes 196616 | tf_op jit(solution)/shard_map/ppermute | solution.py:52
  183.2 6.4 %collective-permute-start.25 = (bf16[256,128]{1,0:T(8,128)(2,1)S(1)}, bf16[256,128]{1,0:T(8,128)(2,1)S(1)}, u32[]{:S(2)}, u32[]{:S(2)}) collective-permute-start(bf16[256,128]{1,0:T(8,128)(2,1)S(1)} %get-tuple-element.41), channel_id=1, source_target_pairs={{48,0},{0,16},{16,32},{32,48},{49,1},{1,17},{17,33},{33,49},{50,2}... | collective-permute-start | bytes 196616 | tf_op jit(solution)/shard_map/ppermute | solution.py:52
  189.7 16.7 %collective-permute-start.26 = (bf16[4,256,128]{2,1,0:T(8,128)(2,1)S(1)}, bf16[4,256,128]{2,1,0:T(8,128)(2,1)S(1)}, u32[]{:S(2)}, u32[]{:S(2)}) collective-permute-start(bf16[4,256,128]{2,1,0:T(8,128)(2,1)S(1)} %pad_maximum_fusion.1.refs_7_), channel_id=1, source_target_pairs={{4,0},{8,4},{12,8},{0,12},{5,1},{9,5},{13,9},{1,13},{6,2},{10,6},{... | collective-permute-start | bytes 786440 | tf_op jit(solution)/shard_map/ppermute | solution.py:52
  189.7 8.5 %collective-permute-start.17 = (bf16[256,128]{1,0:T(8,128)(2,1)S(1)}, bf16[256,128]{1,0:T(8,128)(2,1)S(1)}, u32[]{:S(2)}, u32[]{:S(2)}) collective-permute-start(bf16[256,128]{1,0:T(8,128)(2,1)S(1)} %get-tuple-element.40), channel_id=1, source_target_pairs={{4,0},{8,4},{12,8},{0,12},{5,1},{9,5},{13,9},{1,13},{6,2},{10,6},{... | collective-permute-start | bytes 196616 | tf_op jit(solution)/shard_map/ppermute | solution.py:52
  189.8 16.3 %collective-permute-start.18 = (bf16[256,128]{1,0:T(8,128)(2,1)S(1)}, bf16[256,128]{1,0:T(8,128)(2,1)S(1)}, u32[]{:S(2)}, u32[]{:S(2)}) collective-permute-start(bf16[256,128]{1,0:T(8,128)(2,1)S(1)} %get-tuple-element.40), channel_id=1, source_target_pairs={{8,0},{12,4},{0,8},{4,12},{9,1},{13,5},{1,9},{5,13},{10,2},{14,6},... | collective-permute-start | bytes 196616 | tf_op jit(solution)/shard_map/ppermute | solution.py:52
  193.0 13.2 %collective-permute-start.19 = (bf16[256,128]{1,0:T(8,128)(2,1)S(1)}, bf16[256,128]{1,0:T(8,128)(2,1)S(1)}, u32[]{:S(2)}, u32[]{:S(2)}) collective-permute-start(bf16[256,128]{1,0:T(8,128)(2,1)S(1)} %get-tuple-element.40), channel_id=1, source_target_pairs={{12,0},{0,4},{4,8},{8,12},{13,1},{1,5},{5,9},{9,13},{14,2},{2,6},{... | collective-permute-start | bytes 196616 | tf_op jit(solution)/shard_map/ppermute | solution.py:52
  193.3 15.1 %collective-permute-start.27 = (bf16[4,256,128]{2,1,0:T(8,128)(2,1)S(1)}, bf16[4,256,128]{2,1,0:T(8,128)(2,1)S(1)}, u32[]{:S(2)}, u32[]{:S(2)}) collective-permute-start(bf16[4,256,128]{2,1,0:T(8,128)(2,1)S(1)} %pad_maximum_fusion.1.refs_7_), channel_id=1, source_target_pairs={{8,0},{12,4},{0,8},{4,12},{9,1},{13,5},{1,9},{5,13},{10,2},{14,6},... | collective-permute-start | bytes 786440 | tf_op jit(solution)/shard_map/ppermute | solution.py:52
  198.2 11.9 %collective-permute-start.28 = (bf16[4,256,128]{2,1,0:T(8,128)(2,1)S(1)}, bf16[4,256,128]{2,1,0:T(8,128)(2,1)S(1)}, u32[]{:S(2)}, u32[]{:S(2)}) collective-permute-start(bf16[4,256,128]{2,1,0:T(8,128)(2,1)S(1)} %pad_maximum_fusion.1.refs_7_), channel_id=1, source_target_pairs={{12,0},{0,4},{4,8},{8,12},{13,1},{1,5},{5,9},{9,13},{14,2},{2,6},{... | collective-permute-start | bytes 786440 | tf_op jit(solution)/shard_map/ppermute | solution.py:52
  206.2 6.0 %collective-permute-start.20 = (bf16[4,256,128]{2,1,0:T(8,128)(2,1)S(1)}, bf16[4,256,128]{2,1,0:T(8,128)(2,1)S(1)}, u32[]{:S(2)}, u32[]{:S(2)}) collective-permute-start(bf16[4,256,128]{2,1,0:T(8,128)(2,1)S(1)} %pad_maximum_fusion.refs_3_), channel_id=1, source_target_pairs={{16,0},{32,16},{48,32},{0,48},{17,1},{33,17},{49,33},{1,49},{18,2}... | collective-permute-start | bytes 786440 | tf_op jit(solution)/shard_map/ppermute | solution.py:52
  206.3 7.2 %collective-permute-start.21 = (bf16[4,256,128]{2,1,0:T(8,128)(2,1)S(1)}, bf16[4,256,128]{2,1,0:T(8,128)(2,1)S(1)}, u32[]{:S(2)}, u32[]{:S(2)}) collective-permute-start(bf16[4,256,128]{2,1,0:T(8,128)(2,1)S(1)} %pad_maximum_fusion.refs_3_), channel_id=1, source_target_pairs={{32,0},{48,16},{0,32},{16,48},{33,1},{49,17},{1,33},{17,49},{34,2}... | collective-permute-start | bytes 786440 | tf_op jit(solution)/shard_map/ppermute | solution.py:52
  206.4 15.1 %collective-permute-start.22 = (bf16[4,256,128]{2,1,0:T(8,128)(2,1)S(1)}, bf16[4,256,128]{2,1,0:T(8,128)(2,1)S(1)}, u32[]{:S(2)}, u32[]{:S(2)}) collective-permute-start(bf16[4,256,128]{2,1,0:T(8,128)(2,1)S(1)} %pad_maximum_fusion.refs_3_), channel_id=1, source_target_pairs={{48,0},{0,16},{16,32},{32,48},{49,1},{1,17},{17,33},{33,49},{50,2}... | collective-permute-start | bytes 786440 | tf_op jit(solution)/shard_map/ppermute | solution.py:52
  240.0 9.4 %collective-permute-start.29 = (bf16[64,1024]{1,0:T(8,128)(2,1)S(1)}, bf16[64,1024]{1,0:T(8,128)(2,1)S(1)}, u32[]{:S(2)}, u32[]{:S(2)}) collective-permute-start(bf16[64,1024]{1,0:T(8,128)(2,1)S(1)} %get-tuple-element.42), channel_id=1, source_target_pairs={{0,0},{1,64},{2,128},{3,192},{64,1},{65,65},{66,129},{67,193},{128... | collective-permute-start | bytes 393224 | tf_op jit(solution)/shard_map/ppermute | solution.py:507
  246.5 11.1 %collective-permute-start.30 = (bf16[64,1024]{1,0:T(8,128)(2,1)S(1)}, bf16[64,1024]{1,0:T(8,128)(2,1)S(1)}, u32[]{:S(2)}, u32[]{:S(2)}) collective-permute-start(bf16[64,1024]{1,0:T(8,128)(2,1)S(1)} %get-tuple-element.43), channel_id=1, source_target_pairs={{0,64},{1,128},{2,192},{3,0},{64,65},{65,129},{66,193},{67,1},{128... | collective-permute-start | bytes 393224 | tf_op jit(solution)/shard_map/ppermute | solution.py:507
  247.4 13.1 %collective-permute-start.31 = (bf16[64,1024]{1,0:T(8,128)(2,1)S(1)}, bf16[64,1024]{1,0:T(8,128)(2,1)S(1)}, u32[]{:S(2)}, u32[]{:S(2)}) collective-permute-start(bf16[64,1024]{1,0:T(8,128)(2,1)S(1)} %get-tuple-element.44), channel_id=1, source_target_pairs={{0,128},{1,192},{2,0},{3,64},{64,129},{65,193},{66,1},{67,65},{128... | collective-permute-start | bytes 393224 | tf_op jit(solution)/shard_map/ppermute | solution.py:507
  248.5 12.1 %collective-permute-start.32 = (bf16[64,1024]{1,0:T(8,128)(2,1)S(1)}, bf16[64,1024]{1,0:T(8,128)(2,1)S(1)}, u32[]{:S(2)}, u32[]{:S(2)}) collective-permute-start(bf16[64,1024]{1,0:T(8,128)(2,1)S(1)} %get-tuple-element.45), channel_id=1, source_target_pairs={{0,192},{1,0},{2,64},{3,128},{64,193},{65,1},{66,65},{67,129},{128... | collective-permute-start | bytes 393224 | tf_op jit(solution)/shard_map/ppermute | solution.py:507
  (18 other events, 336.2 us)
where the time goes:
time: 265 us; the launch traced here: 261 us
  starting transfers between devices  90.4 us (34%)
  waiting for transfers between devices  88 us (33%)
  Pallas kernels  26 us (10%)
  blocking collectives  25.6 us (10%)
  local copies, waits for them, and re-layouts  24.5 us (9%)
  other arithmetic  3.91 us (1%)
  between operations  2.9 us (1%)
    ppermute x3, waiting for transfers between devices, shifted(): lax.ppermute(value, axis, [(source, source + steps) for source in range(l...  44.4 us
    ppermute x12, waiting for transfers between devices, around_ring(): lax.ppermute(value, axis, [((i + k) % count, i) for i in range(count)])  22.2 us
    ppermute x12, starting transfers between devices, around_ring(): lax.ppermute(value, axis, [((i + k) % count, i) for i in range(count)])  20.2 us
    ppermute x8, starting transfers between devices, moved(): lax.ppermute(part, (ZL, ZH), [(named(z), named(z + step)) for z in range(...  18.1 us
    all_to_all x2, starting transfers between devices, exchanged(): return lax.all_to_all(pieces, axis, split_axis=0, concat_axis=0, tiled=True)  17.2 us
    ppermute x6, starting transfers between devices, swapped(): return lax.ppermute(value, axis, [(0, 1), (1, 0)])  16.3 us
    unnamed x41, local copies, waits for them, and re-layouts  15.3 us
    all_gather x1, blocking collectives, shards(): partial = partial_outputs(lax.all_gather(heads, ZL), by_head)  13.6 us
  transfers between devices with their start and end apart: 35, of which 16 were waited for; matrix products, arithmetic and copies ran while one was open for 4% of the time, Pallas kernels for 6%

commit v1 on v0

--- a/solution.py
+++ b/solution.py
@@ -242,6 +242,59 @@
     return on_chip(kernel, blank((low * rows, high * width)))(*(part for part, *_ in pieces))
 
 
+def head_weights(lat_qkv, gains, counts):
+    share, depth, inner = lat_qkv.shape
+    step = share * depth + EDGE
+    heads = inner // HD
+
+    def kernel(count_ref, weights_ref, gains_ref, out_ref):
+        block = lax.axis_index(SEQ)
+        gains = gains_ref[...].astype(f32)
+        mine = lax.broadcasted_iota(i32, gains.shape, 0) == block
+        row = jnp.sum(jnp.where(mine, gains, 0.0), axis=0, keepdims=True)
+        square = (depth, depth)
+        same = lax.broadcasted_iota(i32, square, 0) == lax.broadcasted_iota(i32, square, 1)
+        column = jnp.sum(jnp.where(same, row, 0.0), axis=1, keepdims=True)
+        mark = jnp.full((EDGE, HD), count_ref[0].astype(f32)).astype(bf16)
+        for i in range(share):
+            scaled = (weights_ref[i].astype(f32) * column).astype(bf16)
+            for k in range(heads):
+                out_ref[k, i * depth : (i + 1) * depth, :] = scaled[:, k * HD : (k + 1) * HD]
+        for k in range(heads):
+            out_ref[k, share * depth :, :] = mark
+
+    whole = pl.BlockSpec(memory_space=pltpu.VMEM)
+    return on_chip(
+        kernel,
+        blank((heads, step, HD)),
+        in_specs=[pl.BlockSpec(memory_space=pltpu.SMEM), whole, whole],
+        out_specs=whole,
+    )(counts, lat_qkv, gains)
+
+
+def copied_weights(out_part, by_head, copies):
+    cut, deep = out_part.shape
+    heads, step, _ = by_head.shape
+    total = heads * (cut + step)
+
+    def kernel(out_part_ref, by_head_ref, out_ref):
+        for k in range(heads):
+            out_ref[0, k * cut : (k + 1) * cut, :] = out_part_ref[:, k * HD : (k + 1) * HD]
+            start = heads * cut + k * step
+            out_ref[0, start : start + step, :] = by_head_ref[k]
+
+    return on_chip(
+        kernel,
+        blank((copies, total, HD)),
+        grid=(copies,),
+        in_specs=[
+            pl.BlockSpec(out_part.shape, lambda i: (0, 0)),
+            pl.BlockSpec(by_head.shape, lambda i: (0, 0, 0)),
+        ],
+        out_specs=pl.BlockSpec((1, total, HD), lambda i: (i, 0, 0)),
+    )(out_part, by_head)
+
+
 def placed_weights(gathered_weights, first, columns, share, depth, step):
     groups = gathered_weights.shape[0]
 
@@ -404,8 +457,8 @@
     in_use = slot_ids < patch_count
 
     own_q, own_kv = encoder_heads(byte_states, enc_gain, enc_qkv)
-    far_kv = shifted(own_kv, SEQ, 2)
     near_kv = shifted(own_kv, SEQ, 1)
+    far_kv = shifted(near_kv, SEQ, 1)
 
     first_local = (local_starts[0] - anchor).astype(bf16)
     edge = jnp.concatenate(
@@ -418,28 +471,19 @@
     edge = shifted(edge, SEQ, -1)
 
     share, depth, inner = lat_qkv.shape
-    own_gain = lax.dynamic_slice_in_dim(latent_gain, block * depth, depth).astype(f32)
-    scaled = (lat_qkv.astype(f32) * own_gain[:, None]).astype(bf16).reshape(share * depth, inner)
-    mark = jnp.broadcast_to(counts.astype(bf16), (EDGE, HD))
     step = share * depth + EDGE
-    by_head = jnp.concatenate(
-        [part for k in range(columns) for part in (scaled[:, k * HD : (k + 1) * HD], mark)], axis=0
-    ).reshape(columns, step, HD)
-    by_head = exchanged(by_head, ZL).reshape(columns * step, HD)
-    out_part = lat_proj_out.T
-    cut = out_part.shape[0]
-    out_part = [out_part[:, k * HD : (k + 1) * HD] for k in range(columns)]
-    by_head = jnp.concatenate(out_part + [by_head], axis=0)
+    by_head = head_weights(lat_qkv, latent_gain.reshape(-1, depth), counts)
+    by_head = exchanged(by_head, ZL)
+    cut = lat_proj_out.shape[1]
 
     half = enc_proj_out.shape[0] // 2
     high_a, high_b = (swapped(enc_proj_out[at : at + half], ZH) for at in (0, half))
     out_side = swapped(enc_proj_out, CO)
 
-    near_kv, by_head, edge, out_side = lax.optimization_barrier(
-        (near_kv, by_head, edge, out_side)
-    )
-    far_kv, high_a = lax.optimization_barrier((far_kv, high_a))
-    by_head = gathered(by_head, ROWS)
+    near_kv, far_kv, by_head, edge, out_side, high_a = lax.optimization_barrier(
+        (near_kv, far_kv, by_head, edge, out_side, high_a)
+    )
+    by_head = exchanged(copied_weights(lat_proj_out.T, by_head, groups), ROWS)
     next_first = edge[SPILL, 0].astype(i32)
     more_q, more_kv = encoder_heads(edge, enc_gain, enc_qkv)
     attended = encoder_attention(own_q, more_q, far_kv, near_kv, own_kv, more_kv, anchor)

time: 265 us -> 217 us (0.82)
  the two profiles are of different devices: /device:TPU:1 before, /device:TPU:38 now
where the time goes in v1:
time: 217 us; the launch traced here: 216 us
  starting transfers between devices  77.9 us (36%)
  waiting for transfers between devices  62.7 us (29%)
  Pallas kernels  25.7 us (12%)
  blocking collectives  24.1 us (11%)
  local copies, waits for them, and re-layouts  20.4 us (9%)
  between operations  2.95 us (1%)
    ppermute x12, waiting for transfers between devices, around_ring(): lax.ppermute(value, axis, [((i + k) % count, i) for i in range(count)])  24.1 us
    all_to_all x2, starting transfers between devices, exchanged(): return lax.all_to_all(pieces, axis, split_axis=0, concat_axis=0, tiled=True)  20.3 us
    ppermute x12, starting transfers between devices, around_ring(): lax.ppermute(value, axis, [((i + k) % count, i) for i in range(count)])  16.7 us
    ppermute x8, waiting for transfers between devices, moved(): lax.ppermute(part, (ZL, ZH), [(named(z), named(z + step)) for z in range(...  13.6 us
    unnamed x40, local copies, waits for them, and re-layouts  12.9 us
    all_gather x1, blocking collectives, shards(): partial = partial_outputs(lax.all_gather(heads, ZL), by_head)  12.4 us
    ppermute x8, starting transfers between devices, moved(): lax.ppermute(part, (ZL, ZH), [(named(z), named(z + step)) for z in range(...  12.3 us
    all_gather x1, blocking collectives, shards(): attended = lax.all_gather(attended, TP)  11.7 us
  transfers between devices with their start and end apart: 35, of which 22 were waited for; matrix products, arithmetic and copies ran while one was open for 4% of the time, Pallas kernels for 6%

profile of v1, /device:TPU:38, one launch (start us, length us, event | category | flops | bytes accessed | tf_op | source)
XLA Modules:
  0.0 215.9 jit_solution(15685120712334443753)
XLA Ops:
  5.1 3.5 %collective-permute-start = (bf16[256,512]{1,0:T(8,128)(2,1)S(1)}, bf16[256,512]{1,0:T(8,128)(2,1)S(1)}, u32[]{:S(2)}, u32[]{:S(2)}) collective-permute-start(bf16[256,512]{1,0:T(8,128)(2,1)S(1)} %get-tuple-element.24.own_ref), channel_id=1, source_target_pairs={{0,4},{4,8},{8,12},{12,16},{16,20},{20,24},{24,28},{28,32},{32,36}... | collective-permute-start | bytes 786440 | tf_op jit(solution)/shard_map/ppermute | solution.py:34
  11.9 6.0 %all-to-all-start = ((bf16[4,208,128]{2,1,0:T(8,128)(2,1)}), bf16[4,208,128]{2,1,0:T(8,128)(2,1)S(1)}, u32[]{:S(2)}, u32[]{:S(2)}) async-start(bf16[4,208,128]{2,1,0:T(8,128)(2,1)} %shard_map.123), calls=%async_computation | async-start | bytes 425984 | tf_op jit(solution)/shard_map/all_to_all | solution.py:38
  19.6 4.7 %collective-permute-start.4 = (bf16[128,1024]{1,0:T(8,128)(2,1)S(1)}, bf16[128,1024]{1,0:T(8,128)(2,1)S(1)}, u32[]{:S(2)}, u32[]{:S(2)}) collective-permute-start(bf16[128,1024]{1,0:T(8,128)(2,1)S(1)} %get-tuple-element.53), channel_id=1, source_target_pairs={{0,2},{2,0},{1,3},{3,1},{4,6},{6,4},{5,7},{7,5},{8,10},{10,8},{9,1... | collective-permute-start | bytes 786440 | tf_op jit(solution)/shard_map/ppermute | solution.py:42
  24.3 3.5 %collective-permute-start.1 = (bf16[256,512]{1,0:T(8,128)(2,1)S(1)}, bf16[256,512]{1,0:T(8,128)(2,1)S(1)}, u32[]{:S(2)}, u32[]{:S(2)}) collective-permute-start(bf16[256,512]{1,0:T(8,128)(2,1)S(1)} %collective-permute-done.near_ref), channel_id=1, source_target_pairs={{0,4},{4,8},{8,12},{12,16},{16,20},{20,24},{24,28},{28,32},{32,36}... | collective-permute-start | bytes 786440 | tf_op jit(solution)/shard_map/ppermute | solution.py:34
  29.9 4.5 %collective-permute-start.2 = (bf16[16,1024]{1,0:T(8,128)(2,1)S(1)}, bf16[16,1024]{1,0:T(8,128)(2,1)S(1)}, u32[]{:S(2)}, u32[]{:S(2)}) collective-permute-start(bf16[16,1024]{1,0:T(8,128)(2,1)S(1)} %slice_select_fusion), channel_id=1, source_target_pairs={{4,0},{8,4},{12,8},{16,12},{20,16},{24,20},{28,24},{32,28},{36,32}... | collective-permute-start | bytes 98312 | tf_op jit(solution)/shard_map/ppermute | solution.py:34
  41.0 14.3 %all-to-all-start.1 = ((bf16[16,1088,128]{2,1,0:T(8,128)(2,1)}), bf16[16,1088,128]{2,1,0:T(8,128)(2,1)}, u32[]{:S(2)}, u32[]{:S(2)}) async-start(bf16[16,1088,128]{2,1,0:T(8,128)(2,1)} %copy-done), calls=%async_computation.1 | async-start | bytes 8912896 | tf_op jit(solution)/shard_map/all_to_all | solution.py:38
  55.3 2.2 %collective-permute-start.5 = (bf16[128,1024]{1,0:T(8,128)(2,1)}, bf16[128,1024]{1,0:T(8,128)(2,1)}, u32[]{:S(2)}, u32[]{:S(2)}) collective-permute-start(bf16[128,1024]{1,0:T(8,128)(2,1)} %get-tuple-element.52), channel_id=1, source_target_pairs={{0,2},{2,0},{1,3},{3,1},{4,6},{6,4},{5,7},{7,5},{8,10},{10,8},{9,1... | collective-permute-start | bytes 786440 | tf_op jit(solution)/shard_map/ppermute | solution.py:42
  65.0 3.9 %collective-permute-done.5.refs_4_ = bf16[128,1024]{1,0:T(8,128)(2,1)} collective-permute-done((bf16[128,1024]{1,0:T(8,128)(2,1)}, bf16[128,1024]{1,0:T(8,128)(2,1)}, u32[]{:S(2)}, u32[]{:S(2)}) %collective-permute-start.5) | collective-permute-done | bytes 262176 | tf_op jit(solution)/shard_map/ppermute | solution.py:42
  69.0 11.7 %all-gather = bf16[1088,256]{1,0:T(8,128)(2,1)S(1)} all-gather(bf16[272,256]{1,0:T(8,128)(2,1)S(1)} %shard_map.125), channel_id=2, replica_groups=mesh['z_lo'=4,'ring_x'=4,'ring_y'=4,'z_hi'=2,'core'=2] {'z_hi','core'}, dimensions={0}, use_global_device_ids=true | all-gather | bytes 696320 | tf_op jit(solution)/shard_map/all_gather | solution.py:493
  82.8 6.8 %shard_map.127.refs_0_.patches_ref = bf16[64,1024]{1,0:T(8,128)(2,1)S(1)} custom-call(bf16[272,1024]{1,0:T(8,128)(2,1)S(1)} %shard_map.126.extended_ref, s32[64,4]{1,0:T(8,128)S(1)} %copy.26.bounds_ref, bf16[1024,1024]{1,0:T(8,128)(2,1)S(1)} %copy-done.8, bf16[2,1024,1024]{2,1,0:T(8,128)(2,1)} %cross_ref.1), custom_call_target="tpu_custom_call" | custom-call | flops 1048576 | bytes 1048576 | tf_op jit(solution)/shard_map/pallas_call | solution.py:223
  92.4 3.7 %collective-permute-done.8.refs_1_ = bf16[64,1024]{1,0:T(8,128)(2,1)S(1)} collective-permute-done((bf16[64,1024]{1,0:T(8,128)(2,1)S(1)}, bf16[64,1024]{1,0:T(8,128)(2,1)S(1)}, u32[]{:S(2)}, u32[]{:S(2)}) %collective-permute-start.8) | collective-permute-done | bytes 131104 | tf_op jit(solution)/shard_map/ppermute | solution.py:80
  96.1 4.8 %collective-permute-start.10 = (bf16[64,1024]{1,0:T(8,128)(2,1)S(1)}, bf16[64,1024]{1,0:T(8,128)(2,1)S(1)}, u32[]{:S(2)}, u32[]{:S(2)}) collective-permute-start(bf16[64,1024]{1,0:T(8,128)(2,1)S(1)} %collective-permute-done.8.refs_1_), channel_id=1, source_target_pairs={{0,64},{64,128},{128,192},{192,2},{2,66},{66,130},{130,194},{194,0... | collective-permute-start | bytes 393224 | tf_op jit(solution)/shard_map/ppermute | solution.py:80
  101.5 3.5 %collective-permute-done.10.refs_3_ = bf16[64,1024]{1,0:T(8,128)(2,1)S(1)} collective-permute-done((bf16[64,1024]{1,0:T(8,128)(2,1)S(1)}, bf16[64,1024]{1,0:T(8,128)(2,1)S(1)}, u32[]{:S(2)}, u32[]{:S(2)}) %collective-permute-start.10) | collective-permute-done | bytes 131104 | tf_op jit(solution)/shard_map/ppermute | solution.py:80
  108.2 2.7 %collective-permute-done.12.refs_5_ = bf16[64,1024]{1,0:T(8,128)(2,1)S(1)} collective-permute-done((bf16[64,1024]{1,0:T(8,128)(2,1)S(1)}, bf16[64,1024]{1,0:T(8,128)(2,1)S(1)}, u32[]{:S(2)}, u32[]{:S(2)}) %collective-permute-start.12) | collective-permute-done | bytes 131104 | tf_op jit(solution)/shard_map/ppermute | solution.py:80
  111.4 2.9 %collective-permute-start.15 = (bf16[32,1024]{1,0:T(8,128)(2,1)S(1)}, bf16[32,1024]{1,0:T(8,128)(2,1)S(1)}, u32[]{:S(2)}, u32[]{:S(2)}) collective-permute-start(bf16[32,1024]{1,0:T(8,128)(2,1)S(1)} %slice.61), channel_id=1, source_target_pairs={{0,194},{64,0},{128,64},{192,128},{2,192},{66,2},{130,66},{194,130... | collective-permute-start | bytes 196616 | tf_op jit(solution)/shard_map/ppermute | solution.py:80
  117.7 7.2 %all-to-all-done.1.weights_ref = bf16[16,1088,128]{2,1,0:T(8,128)(2,1)} async-done(((bf16[16,1088,128]{2,1,0:T(8,128)(2,1)}), bf16[16,1088,128]{2,1,0:T(8,128)(2,1)}, u32[]{:S(2)}, u32[]{:S(2)}) %all-to-all-start.1) | async-done | bytes 4456480 | tf_op jit(solution)/shard_map/all_to_all | solution.py:38
  124.9 2.8 %shard_map.130.weights_ref = bf16[2,2,1024,384]{3,2,1,0:T(8,128)(2,1)S(1)} custom-call(bf16[16,1088,128]{2,1,0:T(8,128)(2,1)} %all-to-all-done.1.weights_ref), custom_call_target="tpu_custom_call" | custom-call | flops 1048576 | bytes 1048576 | tf_op jit(solution)/shard_map/pallas_call | solution.py:313
  130.8 3.0 %shard_map.131 = (bf16[256,128]{1,0:T(8,128)(2,1)S(1)}, bf16[256,128]{1,0:T(8,128)(2,1)S(1)}, bf16[256,128]{1,0:T(8,128)(2,1)S(1)}) custom-call(bf16[256,2048]{1,0:T(8,128)(2,1)} %shard_map.128.own_ref, bf16[256,2048]{1,0:T(8,128)(2,1)} %collective-permute-done.16.other_ref, bf16[2,2,1024,384]{3,2,1,0:T(8,128)(2,1)S(1)} %shard_map.130.weights_ref, ...), custom_call_target="tpu_custom_call" | custom-call | flops 1048576 | bytes 1048576 | tf_op jit(solution)/shard_map/pallas_call | solution.py:339
  134.0 3.1 %collective-permute-start.17 = (bf16[256,128]{1,0:T(8,128)(2,1)S(1)}, bf16[256,128]{1,0:T(8,128)(2,1)S(1)}, u32[]{:S(2)}, u32[]{:S(2)}) collective-permute-start(bf16[256,128]{1,0:T(8,128)(2,1)S(1)} %get-tuple-element.40), channel_id=1, source_target_pairs={{4,0},{8,4},{12,8},{0,12},{5,1},{9,5},{13,9},{1,13},{6,2},{10,6},{... | collective-permute-start | bytes 196616 | tf_op jit(solution)/shard_map/ppermute | solution.py:52
  137.1 3.8 %collective-permute-done.19 = bf16[256,128]{1,0:T(8,128)(2,1)S(1)} collective-permute-done((bf16[256,128]{1,0:T(8,128)(2,1)S(1)}, bf16[256,128]{1,0:T(8,128)(2,1)S(1)}, u32[]{:S(2)}, u32[]{:S(2)}) %collective-permute-start.19) | collective-permute-done | bytes 65568 | tf_op jit(solution)/shard_map/ppermute | solution.py:52
  141.5 3.4 %collective-permute-start.20 = (bf16[4,256,128]{2,1,0:T(8,128)(2,1)S(1)}, bf16[4,256,128]{2,1,0:T(8,128)(2,1)S(1)}, u32[]{:S(2)}, u32[]{:S(2)}) collective-permute-start(bf16[4,256,128]{2,1,0:T(8,128)(2,1)S(1)} %pad_maximum_fusion.refs_3_), channel_id=1, source_target_pairs={{16,0},{32,16},{48,32},{0,48},{17,1},{33,17},{49,33},{1,49},{18,2}... | collective-permute-start | bytes 786440 | tf_op jit(solution)/shard_map/ppermute | solution.py:52
  147.1 4.0 %collective-permute-start.21 = (bf16[4,256,128]{2,1,0:T(8,128)(2,1)S(1)}, bf16[4,256,128]{2,1,0:T(8,128)(2,1)S(1)}, u32[]{:S(2)}, u32[]{:S(2)}) collective-permute-start(bf16[4,256,128]{2,1,0:T(8,128)(2,1)S(1)} %pad_maximum_fusion.refs_3_), channel_id=1, source_target_pairs={{32,0},{48,16},{0,32},{16,48},{33,1},{49,17},{1,33},{17,49},{34,2}... | collective-permute-start | bytes 786440 | tf_op jit(solution)/shard_map/ppermute | solution.py:52
  153.1 5.7 %collective-permute-done.23 = bf16[256,128]{1,0:T(8,128)(2,1)S(1)} collective-permute-done((bf16[256,128]{1,0:T(8,128)(2,1)S(1)}, bf16[256,128]{1,0:T(8,128)(2,1)S(1)}, u32[]{:S(2)}, u32[]{:S(2)}) %collective-permute-start.23) | collective-permute-done | bytes 65568 | tf_op jit(solution)/shard_map/ppermute | solution.py:52
  158.8 2.9 %collective-permute-start.26 = (bf16[4,256,128]{2,1,0:T(8,128)(2,1)S(1)}, bf16[4,256,128]{2,1,0:T(8,128)(2,1)S(1)}, u32[]{:S(2)}, u32[]{:S(2)}) collective-permute-start(bf16[4,256,128]{2,1,0:T(8,128)(2,1)S(1)} %pad_maximum_fusion.1.refs_7_), channel_id=1, source_target_pairs={{4,0},{8,4},{12,8},{0,12},{5,1},{9,5},{13,9},{1,13},{6,2},{10,6},{... | collective-permute-start | bytes 786440 | tf_op jit(solution)/shard_map/ppermute | solution.py:52
  163.3 8.6 %collective-permute-done.26.refs_8_ = bf16[4,256,128]{2,1,0:T(8,128)(2,1)S(1)} collective-permute-done((bf16[4,256,128]{2,1,0:T(8,128)(2,1)S(1)}, bf16[4,256,128]{2,1,0:T(8,128)(2,1)S(1)}, u32[]{:S(2)}, u32[]{:S(2)}) %collective-permute-start.26) | collective-permute-done | bytes 262176 | tf_op jit(solution)/shard_map/ppermute | solution.py:52
  172.4 2.9 %collective-permute-done.28.refs_10_ = bf16[4,256,128]{2,1,0:T(8,128)(2,1)S(1)} collective-permute-done((bf16[4,256,128]{2,1,0:T(8,128)(2,1)S(1)}, bf16[4,256,128]{2,1,0:T(8,128)(2,1)S(1)}, u32[]{:S(2)}, u32[]{:S(2)}) %collective-permute-start.28) | collective-permute-done | bytes 262176 | tf_op jit(solution)/shard_map/ppermute | solution.py:52
  177.4 12.4 %all-gather.1 = bf16[1024,128]{1,0:T(8,128)(2,1)S(1)} all-gather(bf16[256,128]{1,0:T(8,128)(2,1)S(1)} %shard_map.132), channel_id=3, replica_groups=mesh['z_lo'=4,'ring_x'=4,'ring_y'=4,'z_hi'=2,'core'=2] {'z_lo'}, dimensions={0}, use_global_device_ids=true | all-gather | bytes 327680 | tf_op jit(solution)/shard_map/all_gather | solution.py:549
  189.9 2.8 %shard_map.133 = (bf16[64,1024]{1,0:T(8,128)(2,1)S(1)}, bf16[64,1024]{1,0:T(8,128)(2,1)S(1)}, bf16[64,1024]{1,0:T(8,128)(2,1)S(1)}, bf16[64,1024]{1,0:T(8,128)(2,1)S(1)}) custom-call(bf16[4,256,128]{2,1,0:T(8,128)(2,1)S(1)} %bitcast.29, bf16[16,1088,128]{2,1,0:T(8,128)(2,1)} %all-to-all-done.1.weights_ref), custom_call_target="tpu_custom_call" | custom-call | flops 1048576 | bytes 1048576 | tf_op jit(solution)/shard_map/pallas_call | solution.py:404
  194.7 4.0 %collective-permute-start.31 = (bf16[64,1024]{1,0:T(8,128)(2,1)S(1)}, bf16[64,1024]{1,0:T(8,128)(2,1)S(1)}, u32[]{:S(2)}, u32[]{:S(2)}) collective-permute-start(bf16[64,1024]{1,0:T(8,128)(2,1)S(1)} %get-tuple-element.44), channel_id=1, source_target_pairs={{0,128},{1,192},{2,0},{3,64},{64,129},{65,193},{66,1},{67,65},{128... | collective-permute-start | bytes 393224 | tf_op jit(solution)/shard_map/ppermute | solution.py:551
  198.7 4.1 %collective-permute-start.32 = (bf16[64,1024]{1,0:T(8,128)(2,1)S(1)}, bf16[64,1024]{1,0:T(8,128)(2,1)S(1)}, u32[]{:S(2)}, u32[]{:S(2)}) collective-permute-start(bf16[64,1024]{1,0:T(8,128)(2,1)S(1)} %get-tuple-element.45), channel_id=1, source_target_pairs={{0,192},{1,0},{2,64},{3,128},{64,193},{65,1},{66,65},{67,129},{128... | collective-permute-start | bytes 393224 | tf_op jit(solution)/shard_map/ppermute | solution.py:551
  203.6 8.2 %collective-permute-done.31.refs_2_ = bf16[64,1024]{1,0:T(8,128)(2,1)S(1)} collective-permute-done((bf16[64,1024]{1,0:T(8,128)(2,1)S(1)}, bf16[64,1024]{1,0:T(8,128)(2,1)S(1)}, u32[]{:S(2)}, u32[]{:S(2)}) %collective-permute-start.31) | collective-permute-done | bytes 131104 | tf_op jit(solution)/shard_map/ppermute | solution.py:551
  211.8 3.4 %collective-permute-done.32.refs_3_ = bf16[64,1024]{1,0:T(8,128)(2,1)S(1)} collective-permute-done((bf16[64,1024]{1,0:T(8,128)(2,1)S(1)}, bf16[64,1024]{1,0:T(8,128)(2,1)S(1)}, u32[]{:S(2)}, u32[]{:S(2)}) %collective-permute-start.32) | collective-permute-done | bytes 131104 | tf_op jit(solution)/shard_map/ppermute | solution.py:551
  (142 shorter events, 52.4 us)
Async XLA Ops:
  5.1 19.2 %collective-permute-start = (bf16[256,512]{1,0:T(8,128)(2,1)S(1)}, bf16[256,512]{1,0:T(8,128)(2,1)S(1)}, u32[]{:S(2)}, u32[]{:S(2)}) collective-permute-start(bf16[256,512]{1,0:T(8,128)(2,1)S(1)} %get-tuple-element.24.own_ref), channel_id=1, source_target_pairs={{0,4},{4,8},{8,12},{12,16},{16,20},{20,24},{24,28},{28,32},{32,36}... | collective-permute-start | bytes 786440 | tf_op jit(solution)/shard_map/ppermute | solution.py:34
  8.6 28.9 %collective-permute-start.3 = (bf16[256,1024]{1,0:T(8,128)(2,1)}, bf16[256,1024]{1,0:T(8,128)(2,1)S(1)}, u32[]{:S(2)}, u32[]{:S(2)}) collective-permute-start(bf16[256,1024]{1,0:T(8,128)(2,1)} %refs_0_.1), channel_id=1, source_target_pairs={{0,1},{1,0},{2,3},{3,2},{4,5},{5,4},{6,7},{7,6},{8,9},{9,8},{10,11... | collective-permute-start | bytes 1572872 | tf_op jit(solution)/shard_map/ppermute | solution.py:42
  11.9 24.9 %all-to-all-start = ((bf16[4,208,128]{2,1,0:T(8,128)(2,1)}), bf16[4,208,128]{2,1,0:T(8,128)(2,1)S(1)}, u32[]{:S(2)}, u32[]{:S(2)}) async-start(bf16[4,208,128]{2,1,0:T(8,128)(2,1)} %shard_map.123), calls=%async_computation | async-start | bytes 425984 | tf_op jit(solution)/shard_map/all_to_all | solution.py:38
  19.6 17.1 %collective-permute-start.4 = (bf16[128,1024]{1,0:T(8,128)(2,1)S(1)}, bf16[128,1024]{1,0:T(8,128)(2,1)S(1)}, u32[]{:S(2)}, u32[]{:S(2)}) collective-permute-start(bf16[128,1024]{1,0:T(8,128)(2,1)S(1)} %get-tuple-element.53), channel_id=1, source_target_pairs={{0,2},{2,0},{1,3},{3,1},{4,6},{6,4},{5,7},{7,5},{8,10},{10,8},{9,1... | collective-permute-start | bytes 786440 | tf_op jit(solution)/shard_map/ppermute | solution.py:42
  24.3 12.5 %collective-permute-start.1 = (bf16[256,512]{1,0:T(8,128)(2,1)S(1)}, bf16[256,512]{1,0:T(8,128)(2,1)S(1)}, u32[]{:S(2)}, u32[]{:S(2)}) collective-permute-start(bf16[256,512]{1,0:T(8,128)(2,1)S(1)} %collective-permute-done.near_ref), channel_id=1, source_target_pairs={{0,4},{4,8},{8,12},{12,16},{16,20},{20,24},{24,28},{28,32},{32,36}... | collective-permute-start | bytes 786440 | tf_op jit(solution)/shard_map/ppermute | solution.py:34
  29.9 6.0 %collective-permute-start.2 = (bf16[16,1024]{1,0:T(8,128)(2,1)S(1)}, bf16[16,1024]{1,0:T(8,128)(2,1)S(1)}, u32[]{:S(2)}, u32[]{:S(2)}) collective-permute-start(bf16[16,1024]{1,0:T(8,128)(2,1)S(1)} %slice_select_fusion), channel_id=1, source_target_pairs={{4,0},{8,4},{12,8},{16,12},{20,16},{24,20},{28,24},{32,28},{36,32}... | collective-permute-start | bytes 98312 | tf_op jit(solution)/shard_map/ppermute | solution.py:34
  41.0 83.8 %all-to-all-start.1 = ((bf16[16,1088,128]{2,1,0:T(8,128)(2,1)}), bf16[16,1088,128]{2,1,0:T(8,128)(2,1)}, u32[]{:S(2)}, u32[]{:S(2)}) async-start(bf16[16,1088,128]{2,1,0:T(8,128)(2,1)} %copy-done), calls=%async_computation.1 | async-start | bytes 8912896 | tf_op jit(solution)/shard_map/all_to_all | solution.py:38
  55.3 13.6 %collective-permute-start.5 = (bf16[128,1024]{1,0:T(8,128)(2,1)}, bf16[128,1024]{1,0:T(8,128)(2,1)}, u32[]{:S(2)}, u32[]{:S(2)}) collective-permute-start(bf16[128,1024]{1,0:T(8,128)(2,1)} %get-tuple-element.52), channel_id=1, source_target_pairs={{0,2},{2,0},{1,3},{3,1},{4,6},{6,4},{5,7},{7,5},{8,10},{10,8},{9,1... | collective-permute-start | bytes 786440 | tf_op jit(solution)/shard_map/ppermute | solution.py:42
  57.5 11.4 %collective-permute-start.6 = (bf16[128,1024]{1,0:T(8,128)(2,1)S(1)}, bf16[128,1024]{1,0:T(8,128)(2,1)}, u32[]{:S(2)}, u32[]{:S(2)}) collective-permute-start(bf16[128,1024]{1,0:T(8,128)(2,1)S(1)} %collective-permute-done.4.refs_2_), channel_id=1, source_target_pairs={{0,1},{1,0},{2,3},{3,2},{4,5},{5,4},{6,7},{7,6},{8,9},{9,8},{10,11... | collective-permute-start | bytes 786440 | tf_op jit(solution)/shard_map/ppermute | solution.py:42
  68.9 11.8 %collective-permute-start.7 = (bf16[128,1024]{1,0:T(8,128)(2,1)}, bf16[128,1024]{1,0:T(8,128)(2,1)S(1)}, u32[]{:S(2)}, u32[]{:S(2)}) collective-permute-start(bf16[128,1024]{1,0:T(8,128)(2,1)} %collective-permute-done.5.refs_4_), channel_id=1, source_target_pairs={{0,1},{1,0},{2,3},{3,2},{4,5},{5,4},{6,7},{7,6},{8,9},{9,8},{10,11... | collective-permute-start | bytes 786440 | tf_op jit(solution)/shard_map/ppermute | solution.py:42
  90.4 5.8 %collective-permute-start.8 = (bf16[64,1024]{1,0:T(8,128)(2,1)S(1)}, bf16[64,1024]{1,0:T(8,128)(2,1)S(1)}, u32[]{:S(2)}, u32[]{:S(2)}) collective-permute-start(bf16[64,1024]{1,0:T(8,128)(2,1)S(1)} %shard_map.127.refs_0_.patches_ref), channel_id=1, source_target_pairs={{0,64},{64,128},{128,192},{192,2},{2,66},{66,130},{130,194},{194,0... | collective-permute-start | bytes 393224 | tf_op jit(solution)/shard_map/ppermute | solution.py:80
  92.0 9.4 %collective-permute-start.9 = (bf16[64,1024]{1,0:T(8,128)(2,1)S(1)}, bf16[64,1024]{1,0:T(8,128)(2,1)S(1)}, u32[]{:S(2)}, u32[]{:S(2)}) collective-permute-start(bf16[64,1024]{1,0:T(8,128)(2,1)S(1)} %shard_map.127.refs_0_.patches_ref), channel_id=1, source_target_pairs={{0,194},{64,0},{128,64},{192,128},{2,192},{66,2},{130,66},{194,130... | collective-permute-start | bytes 393224 | tf_op jit(solution)/shard_map/ppermute | solution.py:80
  96.1 8.9 %collective-permute-start.10 = (bf16[64,1024]{1,0:T(8,128)(2,1)S(1)}, bf16[64,1024]{1,0:T(8,128)(2,1)S(1)}, u32[]{:S(2)}, u32[]{:S(2)}) collective-permute-start(bf16[64,1024]{1,0:T(8,128)(2,1)S(1)} %collective-permute-done.8.refs_1_), channel_id=1, source_target_pairs={{0,64},{64,128},{128,192},{192,2},{2,66},{66,130},{130,194},{194,0... | collective-permute-start | bytes 393224 | tf_op jit(solution)/shard_map/ppermute | solution.py:80
  105.0 5.9 %collective-permute-start.12 = (bf16[64,1024]{1,0:T(8,128)(2,1)S(1)}, bf16[64,1024]{1,0:T(8,128)(2,1)S(1)}, u32[]{:S(2)}, u32[]{:S(2)}) collective-permute-start(bf16[64,1024]{1,0:T(8,128)(2,1)S(1)} %collective-permute-done.10.refs_3_), channel_id=1, source_target_pairs={{0,64},{64,128},{128,192},{192,2},{2,66},{66,130},{130,194},{194,0... | collective-permute-start | bytes 393224 | tf_op jit(solution)/shard_map/ppermute | solution.py:80
  110.9 5.5 %collective-permute-start.14 = (bf16[32,1024]{1,0:T(8,128)(2,1)S(1)}, bf16[32,1024]{1,0:T(8,128)(2,1)S(1)}, u32[]{:S(2)}, u32[]{:S(2)}) collective-permute-start(bf16[32,1024]{1,0:T(8,128)(2,1)S(1)} %slice.60), channel_id=1, source_target_pairs={{0,64},{64,128},{128,192},{192,2},{2,66},{66,130},{130,194},{194,0... | collective-permute-start | bytes 196616 | tf_op jit(solution)/shard_map/ppermute | solution.py:80
  111.4 5.2 %collective-permute-start.15 = (bf16[32,1024]{1,0:T(8,128)(2,1)S(1)}, bf16[32,1024]{1,0:T(8,128)(2,1)S(1)}, u32[]{:S(2)}, u32[]{:S(2)}) collective-permute-start(bf16[32,1024]{1,0:T(8,128)(2,1)S(1)} %slice.61), channel_id=1, source_target_pairs={{0,194},{64,0},{128,64},{192,128},{2,192},{66,2},{130,66},{194,130... | collective-permute-start | bytes 196616 | tf_op jit(solution)/shard_map/ppermute | solution.py:80
  133.8 7.1 %collective-permute-start.19 = (bf16[256,128]{1,0:T(8,128)(2,1)S(1)}, bf16[256,128]{1,0:T(8,128)(2,1)S(1)}, u32[]{:S(2)}, u32[]{:S(2)}) collective-permute-start(bf16[256,128]{1,0:T(8,128)(2,1)S(1)} %get-tuple-element.40), channel_id=1, source_target_pairs={{12,0},{0,4},{4,8},{8,12},{13,1},{1,5},{5,9},{9,13},{14,2},{2,6},{... | collective-permute-start | bytes 196616 | tf_op jit(solution)/shard_map/ppermute | solution.py:52
  133.9 7.0 %collective-permute-start.18 = (bf16[256,128]{1,0:T(8,128)(2,1)S(1)}, bf16[256,128]{1,0:T(8,128)(2,1)S(1)}, u32[]{:S(2)}, u32[]{:S(2)}) collective-permute-start(bf16[256,128]{1,0:T(8,128)(2,1)S(1)} %get-tuple-element.40), channel_id=1, source_target_pairs={{8,0},{12,4},{0,8},{4,12},{9,1},{13,5},{1,9},{5,13},{10,2},{14,6},... | collective-permute-start | bytes 196616 | tf_op jit(solution)/shard_map/ppermute | solution.py:52
  134.0 7.5 %collective-permute-start.17 = (bf16[256,128]{1,0:T(8,128)(2,1)S(1)}, bf16[256,128]{1,0:T(8,128)(2,1)S(1)}, u32[]{:S(2)}, u32[]{:S(2)}) collective-permute-start(bf16[256,128]{1,0:T(8,128)(2,1)S(1)} %get-tuple-element.40), channel_id=1, source_target_pairs={{4,0},{8,4},{12,8},{0,12},{5,1},{9,5},{13,9},{1,13},{6,2},{10,6},{... | collective-permute-start | bytes 196616 | tf_op jit(solution)/shard_map/ppermute | solution.py:52
  141.5 20.2 %collective-permute-start.20 = (bf16[4,256,128]{2,1,0:T(8,128)(2,1)S(1)}, bf16[4,256,128]{2,1,0:T(8,128)(2,1)S(1)}, u32[]{:S(2)}, u32[]{:S(2)}) collective-permute-start(bf16[4,256,128]{2,1,0:T(8,128)(2,1)S(1)} %pad_maximum_fusion.refs_3_), channel_id=1, source_target_pairs={{16,0},{32,16},{48,32},{0,48},{17,1},{33,17},{49,33},{1,49},{18,2}... | collective-permute-start | bytes 786440 | tf_op jit(solution)/shard_map/ppermute | solution.py:52
  144.9 6.2 %collective-permute-start.25 = (bf16[256,128]{1,0:T(8,128)(2,1)S(1)}, bf16[256,128]{1,0:T(8,128)(2,1)S(1)}, u32[]{:S(2)}, u32[]{:S(2)}) collective-permute-start(bf16[256,128]{1,0:T(8,128)(2,1)S(1)} %get-tuple-element.41), channel_id=1, source_target_pairs={{48,0},{0,16},{16,32},{32,48},{49,1},{1,17},{17,33},{33,49},{50,2}... | collective-permute-start | bytes 196616 | tf_op jit(solution)/shard_map/ppermute | solution.py:52
  144.9 8.2 %collective-permute-start.24 = (bf16[256,128]{1,0:T(8,128)(2,1)S(1)}, bf16[256,128]{1,0:T(8,128)(2,1)S(1)}, u32[]{:S(2)}, u32[]{:S(2)}) collective-permute-start(bf16[256,128]{1,0:T(8,128)(2,1)S(1)} %get-tuple-element.41), channel_id=1, source_target_pairs={{32,0},{48,16},{0,32},{16,48},{33,1},{49,17},{1,33},{17,49},{34,2}... | collective-permute-start | bytes 196616 | tf_op jit(solution)/shard_map/ppermute | solution.py:52
  147.1 11.7 %collective-permute-start.23 = (bf16[256,128]{1,0:T(8,128)(2,1)S(1)}, bf16[256,128]{1,0:T(8,128)(2,1)S(1)}, u32[]{:S(2)}, u32[]{:S(2)}) collective-permute-start(bf16[256,128]{1,0:T(8,128)(2,1)S(1)} %get-tuple-element.41), channel_id=1, source_target_pairs={{16,0},{32,16},{48,32},{0,48},{17,1},{33,17},{49,33},{1,49},{18,2}... | collective-permute-start | bytes 196616 | tf_op jit(solution)/shard_map/ppermute | solution.py:52
  147.1 16.2 %collective-permute-start.21 = (bf16[4,256,128]{2,1,0:T(8,128)(2,1)S(1)}, bf16[4,256,128]{2,1,0:T(8,128)(2,1)S(1)}, u32[]{:S(2)}, u32[]{:S(2)}) collective-permute-start(bf16[4,256,128]{2,1,0:T(8,128)(2,1)S(1)} %pad_maximum_fusion.refs_3_), channel_id=1, source_target_pairs={{32,0},{48,16},{0,32},{16,48},{33,1},{49,17},{1,33},{17,49},{34,2}... | collective-permute-start | bytes 786440 | tf_op jit(solution)/shard_map/ppermute | solution.py:52
  151.1 12.2 %collective-permute-start.22 = (bf16[4,256,128]{2,1,0:T(8,128)(2,1)S(1)}, bf16[4,256,128]{2,1,0:T(8,128)(2,1)S(1)}, u32[]{:S(2)}, u32[]{:S(2)}) collective-permute-start(bf16[4,256,128]{2,1,0:T(8,128)(2,1)S(1)} %pad_maximum_fusion.refs_3_), channel_id=1, source_target_pairs={{48,0},{0,16},{16,32},{32,48},{49,1},{1,17},{17,33},{33,49},{50,2}... | collective-permute-start | bytes 786440 | tf_op jit(solution)/shard_map/ppermute | solution.py:52
  158.8 13.1 %collective-permute-start.26 = (bf16[4,256,128]{2,1,0:T(8,128)(2,1)S(1)}, bf16[4,256,128]{2,1,0:T(8,128)(2,1)S(1)}, u32[]{:S(2)}, u32[]{:S(2)}) collective-permute-start(bf16[4,256,128]{2,1,0:T(8,128)(2,1)S(1)} %pad_maximum_fusion.1.refs_7_), channel_id=1, source_target_pairs={{4,0},{8,4},{12,8},{0,12},{5,1},{9,5},{13,9},{1,13},{6,2},{10,6},{... | collective-permute-start | bytes 786440 | tf_op jit(solution)/shard_map/ppermute | solution.py:52
  161.7 10.8 %collective-permute-start.27 = (bf16[4,256,128]{2,1,0:T(8,128)(2,1)S(1)}, bf16[4,256,128]{2,1,0:T(8,128)(2,1)S(1)}, u32[]{:S(2)}, u32[]{:S(2)}) collective-permute-start(bf16[4,256,128]{2,1,0:T(8,128)(2,1)S(1)} %pad_maximum_fusion.1.refs_7_), channel_id=1, source_target_pairs={{8,0},{12,4},{0,8},{4,12},{9,1},{13,5},{1,9},{5,13},{10,2},{14,6},... | collective-permute-start | bytes 786440 | tf_op jit(solution)/shard_map/ppermute | solution.py:52
  161.7 13.6 %collective-permute-start.28 = (bf16[4,256,128]{2,1,0:T(8,128)(2,1)S(1)}, bf16[4,256,128]{2,1,0:T(8,128)(2,1)S(1)}, u32[]{:S(2)}, u32[]{:S(2)}) collective-permute-start(bf16[4,256,128]{2,1,0:T(8,128)(2,1)S(1)} %pad_maximum_fusion.1.refs_7_), channel_id=1, source_target_pairs={{12,0},{0,4},{4,8},{8,12},{13,1},{1,5},{5,9},{9,13},{14,2},{2,6},{... | collective-permute-start | bytes 786440 | tf_op jit(solution)/shard_map/ppermute | solution.py:52
  192.6 10.9 %collective-permute-start.29 = (bf16[64,1024]{1,0:T(8,128)(2,1)S(1)}, bf16[64,1024]{1,0:T(8,128)(2,1)S(1)}, u32[]{:S(2)}, u32[]{:S(2)}) collective-permute-start(bf16[64,1024]{1,0:T(8,128)(2,1)S(1)} %get-tuple-element.42), channel_id=1, source_target_pairs={{0,0},{1,64},{2,128},{3,192},{64,1},{65,65},{66,129},{67,193},{128... | collective-permute-start | bytes 393224 | tf_op jit(solution)/shard_map/ppermute | solution.py:551
  194.6 9.0 %collective-permute-start.30 = (bf16[64,1024]{1,0:T(8,128)(2,1)S(1)}, bf16[64,1024]{1,0:T(8,128)(2,1)S(1)}, u32[]{:S(2)}, u32[]{:S(2)}) collective-permute-start(bf16[64,1024]{1,0:T(8,128)(2,1)S(1)} %get-tuple-element.43), channel_id=1, source_target_pairs={{0,64},{1,128},{2,192},{3,0},{64,65},{65,129},{66,193},{67,1},{128... | collective-permute-start | bytes 393224 | tf_op jit(solution)/shard_map/ppermute | solution.py:551
  194.7 17.2 %collective-permute-start.31 = (bf16[64,1024]{1,0:T(8,128)(2,1)S(1)}, bf16[64,1024]{1,0:T(8,128)(2,1)S(1)}, u32[]{:S(2)}, u32[]{:S(2)}) collective-permute-start(bf16[64,1024]{1,0:T(8,128)(2,1)S(1)} %get-tuple-element.44), channel_id=1, source_target_pairs={{0,128},{1,192},{2,0},{3,64},{64,129},{65,193},{66,1},{67,65},{128... | collective-permute-start | bytes 393224 | tf_op jit(solution)/shard_map/ppermute | solution.py:551
  198.7 16.5 %collective-permute-start.32 = (bf16[64,1024]{1,0:T(8,128)(2,1)S(1)}, bf16[64,1024]{1,0:T(8,128)(2,1)S(1)}, u32[]{:S(2)}, u32[]{:S(2)}) collective-permute-start(bf16[64,1024]{1,0:T(8,128)(2,1)S(1)} %get-tuple-element.45), channel_id=1, source_target_pairs={{0,192},{1,0},{2,64},{3,128},{64,193},{65,1},{66,65},{67,129},{128... | collective-permute-start | bytes 393224 | tf_op jit(solution)/shard_map/ppermute | solution.py:551
  (23 other events, 247.1 us)

commit v2 on v1

--- a/solution.py
+++ b/solution.py
@@ -89,7 +89,7 @@
     return pieces
 
 
-def on_chip(kernel, outs, scratch=(), limit=48, **extra):
+def on_chip(kernel, outs, scratch=(), limit=16, **extra):
     return pl.pallas_call(
         kernel,
         out_shape=outs,
@@ -190,24 +190,29 @@
 
 
 def patch_block(extended, bounds, lift, cross_kv):
-    spans = extended.shape[0]
+    spans, width = extended.shape
     slots = bounds.shape[0]
-    width = lift.shape[1]
-
-    def kernel(extended_ref, bounds_ref, lift_ref, cross_ref, out_ref):
+    wide = 2 * HD
+
+    def kernel(extended_ref, bounds_ref, lift_ref, cross_ref, out_ref, pooled_ref):
         column = lax.broadcasted_iota(i32, (slots, spans), 1)
         first, after, seen, used = (bounds_ref[:, k : k + 1] for k in range(4))
         rows = extended_ref[...]
-        inside = (column >= first) & (column < after)
+
+        @pl.when(pl.program_id(0) == 0)
+        def _():
+            inside = (column >= first) & (column < after)
+            member = jnp.where(inside, 1.0, 0.0).astype(bf16)
+            lengths = jnp.maximum(after - first, 1).astype(f32)
+            totals = jnp.dot(member, rows, preferred_element_type=f32)
+            pooled_ref[...] = (totals / lengths).astype(bf16)
+
         allowed = (column >= first) & (column < seen)
-        member = jnp.where(inside, 1.0, 0.0).astype(bf16)
-        lengths = jnp.maximum(after - first, 1).astype(f32)
-        pooled = (jnp.dot(member, rows, preferred_element_type=f32) / lengths).astype(bf16)
-        lifted = jnp.dot(pooled, lift_ref[...], preferred_element_type=f32)
+        lifted = jnp.dot(pooled_ref[...], lift_ref[...], preferred_element_type=f32)
         query = lifted.astype(bf16)
         keys = jnp.dot(rows, cross_ref[0], preferred_element_type=f32).astype(bf16)
         values = jnp.dot(rows, cross_ref[1], preferred_element_type=f32).astype(bf16)
-        for head in range(width // HD):
+        for head in range(wide // HD):
             span = slice(head * HD, (head + 1) * HD)
             scores = lax.dot_general(
                 query[:, span], keys[:, span], NT, preferred_element_type=f32
@@ -220,7 +225,19 @@
             total = jnp.where(used > 0, lifted[:, span] + crossed, 0.0)
             out_ref[:, span] = total.astype(bf16)
 
-    return on_chip(kernel, blank((slots, width)))(extended, bounds, lift, cross_kv)
+    return on_chip(
+        kernel,
+        blank((slots, lift.shape[1])),
+        [pltpu.VMEM((slots, width), bf16)],
+        grid=(lift.shape[1] // wide,),
+        in_specs=[
+            pl.BlockSpec((spans, width), lambda i: (0, 0)),
+            pl.BlockSpec(bounds.shape, lambda i: (0, 0)),
+            pl.BlockSpec((width, wide), lambda i: (0, i)),
+            pl.BlockSpec((2, width, wide), lambda i: (0, 0, i)),
+        ],
+        out_specs=pl.BlockSpec((slots, wide), lambda i: (0, i)),
+    )(extended, bounds, lift, cross_kv)
 
 
 def placed_rows(pieces):
@@ -383,34 +400,48 @@
     groups = weights.shape[0]
     slots = rows // columns
     cut = slots
-
-    def kernel(heads_ref, weights_ref, *out_refs):
-        here = lax.axis_index(TP)
+    pair = columns // 2
+
+    def kernel(heads_ref, weights_ref, kept_ref, sent_ref):
+        core, high = (lax.axis_index(CO), lax.axis_index(ZH))
         flat = [
             weights_ref[:, zl * cut : (zl + 1) * cut, :].reshape(groups * cut, HD)
             for zl in range(columns)
         ]
-        for k, out_ref in enumerate(out_refs):
-            start = lax.bitwise_and(here + k, columns - 1) * slots
-            span = pl.ds(pl.multiple_of(start, slots), slots)
-            total = jnp.zeros((slots, groups * cut), f32)
-            for zl in range(columns):
-                total += lax.dot_general(
-                    heads_ref[zl, span, :], flat[zl], NT, preferred_element_type=f32
-                )
-            out_ref[...] = total.astype(bf16)
+        for side, out_ref in enumerate((kept_ref, sent_ref)):
+            for i in range(pair):
+                block = pair * lax.bitwise_xor(core, side) + lax.bitwise_xor(high, i)
+                span = pl.ds(pl.multiple_of(block * slots, slots), slots)
+                total = jnp.zeros((slots, groups * cut), f32)
+                for zl in range(columns):
+                    total += lax.dot_general(
+                        heads_ref[zl, span, :], flat[zl], NT, preferred_element_type=f32
+                    )
+                out_ref[i] = total.astype(out_ref.dtype)
 
     block = (groups, columns * cut, HD)
+    shape = (pair, slots, groups * cut)
+    whole = pl.BlockSpec(shape, lambda i: (0, 0, 0))
     return on_chip(
         kernel,
-        [blank((slots, groups * cut))] * columns,
+        [blank(shape, f32), blank(shape)],
         grid=(1,),
         in_specs=[
             pl.BlockSpec(heads.shape, lambda i: (0, 0, 0)),
             pl.BlockSpec(block, lambda i: (0, 0, 0)),
         ],
-        out_specs=[pl.BlockSpec((slots, groups * cut), lambda i: (0, 0))] * columns,
+        out_specs=[whole, whole],
     )(heads, weights)
+
+
+def added_outputs(kept, received):
+    pair = kept.shape[0]
+
+    def kernel(kept_ref, received_ref, *out_refs):
+        for i, out_ref in enumerate(out_refs):
+            out_ref[...] = (kept_ref[i] + received_ref[i].astype(f32)).astype(bf16)
+
+    return on_chip(kernel, [blank(kept.shape[1:])] * pair)(kept, received)
 
 
 def summed_outputs(pieces, patches, counts):
@@ -457,8 +488,8 @@
     in_use = slot_ids < patch_count
 
     own_q, own_kv = encoder_heads(byte_states, enc_gain, enc_qkv)
+    far_kv = shifted(own_kv, SEQ, 2)
     near_kv = shifted(own_kv, SEQ, 1)
-    far_kv = shifted(near_kv, SEQ, 1)
 
     first_local = (local_starts[0] - anchor).astype(bf16)
     edge = jnp.concatenate(
@@ -480,15 +511,17 @@
     high_a, high_b = (swapped(enc_proj_out[at : at + half], ZH) for at in (0, half))
     out_side = swapped(enc_proj_out, CO)
 
-    near_kv, far_kv, by_head, edge, out_side, high_a = lax.optimization_barrier(
-        (near_kv, far_kv, by_head, edge, out_side, high_a)
-    )
-    by_head = exchanged(copied_weights(lat_proj_out.T, by_head, groups), ROWS)
+    near_kv, far_kv, edge, out_side, high_a = lax.optimization_barrier(
+        (near_kv, far_kv, edge, out_side, high_a)
+    )
     next_first = edge[SPILL, 0].astype(i32)
     more_q, more_kv = encoder_heads(edge, enc_gain, enc_qkv)
     attended = encoder_attention(own_q, more_q, far_kv, near_kv, own_kv, more_kv, anchor)
     both_a = swapped(high_a, CO)
-    attended, high_b, both_a = lax.optimization_barrier((attended, high_b, both_a))
+    attended, by_head, high_b, both_a = lax.optimization_barrier(
+        (attended, by_head, high_b, both_a)
+    )
+    by_head = exchanged(copied_weights(lat_proj_out.T, by_head, groups), ROWS)
     both_b = swapped(high_b, CO)
     attended = lax.all_gather(attended, TP)
     extended = encoder_output(
@@ -512,6 +545,11 @@
     used = in_use.astype(i32)
     bounds = jnp.stack([first, after, jnp.where(in_use, after, 1), used], axis=1)
     patches = patch_block(extended, bounds, lift, cross_kv)
+    own_rows = placed_rows(around_column(patches))
+    other_rows = swapped(own_rows, CO)
+    own_rows, by_head = lax.optimization_barrier((own_rows, by_head))
+    latent_in = placed_weights(by_head, columns * cut, columns, share, depth, step)
+
     grid = (*(lax.axis_size(name) for name in ROWS), columns)
     here = tuple(lax.axis_index(name) for name in ROWS)
     all_counts = jnp.stack(
@@ -536,28 +574,22 @@
     cosine, sine = (jnp.cos(angles), jnp.sin(angles))
     cosine = jnp.concatenate([cosine, cosine], axis=1)
     sine = jnp.concatenate([-sine, sine], axis=1)
-    latent_in = placed_weights(by_head, columns * cut, columns, share, depth, step)
-
-    own_rows = placed_rows(around_column(patches))
-    own_rows, latent_in = lax.optimization_barrier((own_rows, latent_in))
-    other_rows = swapped(own_rows, CO)
+
     queries, keys, values = latent_heads(own_rows, other_rows, latent_in, cosine, sine)
     keys = around_ring(jnp.stack(around_ring(keys, RY)), RX)
     values = around_ring(jnp.stack(around_ring(values, RX)), RY)
     heads = latent_attention(queries, keys, values, position[:, None], key_pos)
 
-    partial = partial_outputs(lax.all_gather(heads, ZL), by_head)
+    kept, sent = partial_outputs(lax.all_gather(heads, ZL), by_head)
+    partial = added_outputs(kept, swapped(sent, CO))
+    places = [(a, h, c) for a in range(columns) for h in range(2) for c in range(2)]
     partial = [
         lax.ppermute(
             piece,
             COLUMN,
-            [
-                (a * tensor + b, (b + k) % columns * tensor + a)
-                for a in range(columns)
-                for b in range(tensor)
-            ],
+            [(a * tensor + 2 * h + c, (2 * c + (h ^ i)) * tensor + a) for a, h, c in places],
         )
-        for k, piece in enumerate(partial)
+        for i, piece in enumerate(partial)
     ]
     latent = summed_outputs(partial, patches, counts)
     return (encoded, latent)

time: 217 us -> 213 us (0.982)
  the two profiles are of different devices: /device:TPU:38 before, /device:TPU:1 now
where the time goes in v2:
time: 213 us; the launch traced here: 211 us
  starting transfers between devices  88.5 us (42%)
  waiting for transfers between devices  40.3 us (19%)
  blocking collectives  37 us (17%)
  Pallas kernels  24.9 us (12%)
  local copies, waits for them, and re-layouts  15.5 us (7%)
  between operations  2.95 us (1%)
    ppermute x7, starting transfers between devices, swapped(): return lax.ppermute(value, axis, [(0, 1), (1, 0)])  39.3 us
    all_gather x1, blocking collectives, shards(): kept, sent = partial_outputs(lax.all_gather(heads, ZL), by_head)  22.6 us
    ppermute x12, waiting for transfers between devices, around_ring(): lax.ppermute(value, axis, [((i + k) % count, i) for i in range(count)])  15 us
    all_gather x1, blocking collectives, shards(): attended = lax.all_gather(attended, TP)  14.4 us
    ppermute x12, starting transfers between devices, around_ring(): lax.ppermute(value, axis, [((i + k) % count, i) for i in range(count)])  12.7 us
    all_to_all x2, starting transfers between devices, exchanged(): return lax.all_to_all(pieces, axis, split_axis=0, concat_axis=0, tiled=True)  11.6 us
    ppermute x8, starting transfers between devices, moved(): lax.ppermute(part, (ZL, ZH), [(named(z), named(z + step)) for z in range(...  10.8 us
    ppermute x8, waiting for transfers between devices, moved(): lax.ppermute(part, (ZL, ZH), [(named(z), named(z + step)) for z in range(...  10.3 us
  transfers between devices with their start and end apart: 34, of which 15 were waited for; matrix products, arithmetic and copies ran while one was open for 5% of the time, Pallas kernels for 8%

profile of v2, /device:TPU:1, one launch (start us, length us, event | category | flops | bytes accessed | tf_op | source)
XLA Modules:
  0.0 211.2 jit_solution(16291791733071876646)
XLA Ops:
  0.6 3.3 %collective-permute-start.3 = (bf16[256,1024]{1,0:T(8,128)(2,1)}, bf16[256,1024]{1,0:T(8,128)(2,1)S(1)}, u32[]{:S(2)}, u32[]{:S(2)}) collective-permute-start(bf16[256,1024]{1,0:T(8,128)(2,1)} %refs_0_.1), channel_id=1, source_target_pairs={{0,1},{1,0},{2,3},{3,2},{4,5},{5,4},{6,7},{7,6},{8,9},{9,8},{10,11... | collective-permute-start | bytes 1572872 | tf_op jit(solution)/shard_map/ppermute | solution.py:42
  8.5 2.2 %collective-permute-start = (bf16[256,512]{1,0:T(8,128)(2,1)}, bf16[256,512]{1,0:T(8,128)(2,1)}, u32[]{:S(2)}, u32[]{:S(2)}) collective-permute-start(bf16[256,512]{1,0:T(8,128)(2,1)} %get-tuple-element.24.own_ref), channel_id=1, source_target_pairs={{0,4},{4,8},{8,12},{12,16},{16,20},{20,24},{24,28},{28,32},{32,36}... | collective-permute-start | bytes 786440 | tf_op jit(solution)/shard_map/ppermute | solution.py:34
  10.6 4.5 %collective-permute-start.1 = (bf16[256,512]{1,0:T(8,128)(2,1)}, bf16[256,512]{1,0:T(8,128)(2,1)}, u32[]{:S(2)}, u32[]{:S(2)}) collective-permute-start(bf16[256,512]{1,0:T(8,128)(2,1)} %get-tuple-element.24.own_ref), channel_id=1, source_target_pairs={{0,8},{4,12},{8,16},{12,20},{16,24},{20,28},{24,32},{28,36},{32,40... | collective-permute-start | bytes 786440 | tf_op jit(solution)/shard_map/ppermute | solution.py:34
  17.1 6.9 %collective-permute-start.4 = (bf16[128,1024]{1,0:T(8,128)(2,1)}, bf16[128,1024]{1,0:T(8,128)(2,1)S(1)}, u32[]{:S(2)}, u32[]{:S(2)}) collective-permute-start(bf16[128,1024]{1,0:T(8,128)(2,1)} %get-tuple-element.53), channel_id=1, source_target_pairs={{0,2},{2,0},{1,3},{3,1},{4,6},{6,4},{5,7},{7,5},{8,10},{10,8},{9,1... | collective-permute-start | bytes 786440 | tf_op jit(solution)/shard_map/ppermute | solution.py:42
  27.1 3.4 %all-to-all-start = ((bf16[4,208,128]{2,1,0:T(8,128)(2,1)}), bf16[4,208,128]{2,1,0:T(8,128)(2,1)S(1)}, u32[]{:S(2)}, u32[]{:S(2)}) async-start(bf16[4,208,128]{2,1,0:T(8,128)(2,1)} %shard_map.125), calls=%async_computation | async-start | bytes 425984 | tf_op jit(solution)/shard_map/all_to_all | solution.py:38
  33.3 3.7 %collective-permute-done.2.states_ref.edge_ref = bf16[16,1024]{1,0:T(8,128)(2,1)S(1)} collective-permute-done((bf16[16,1024]{1,0:T(8,128)(2,1)S(1)}, bf16[16,1024]{1,0:T(8,128)(2,1)S(1)}, u32[]{:S(2)}, u32[]{:S(2)}) %collective-permute-start.2) | collective-permute-done | bytes 32800 | tf_op jit(solution)/shard_map/ppermute | solution.py:34
  37.0 2.4 %collective-permute-start.6 = (bf16[128,1024]{1,0:T(8,128)(2,1)S(1)}, bf16[128,1024]{1,0:T(8,128)(2,1)}, u32[]{:S(2)}, u32[]{:S(2)}) collective-permute-start(bf16[128,1024]{1,0:T(8,128)(2,1)S(1)} %collective-permute-done.4.refs_2_), channel_id=1, source_target_pairs={{0,1},{1,0},{2,3},{3,2},{4,5},{5,4},{6,7},{7,6},{8,9},{9,8},{10,11... | collective-permute-start | bytes 786440 | tf_op jit(solution)/shard_map/ppermute | solution.py:42
  39.7 3.1 %shard_map.124 = bf16[272,256]{1,0:T(8,128)(2,1)S(1)} custom-call(s32[1]{0:T(128)} %bitcast.1.anchor_ref, bf16[256,256]{1,0:T(8,128)(2,1)S(1)} %get-tuple-element.26.q_ref, bf16[16,256]{1,0:T(8,128)(2,1)S(1)} %get-tuple-element.27.mq_ref, bf16[256,512]{1,0:T(8,128)(2,1)} %collective-permute-done.1.far_ref, bf16[256,512]{1,0:T(8,128)(2,1)} %collective-permute-done.near_ref, ...), custom_call_target="tpu_custom_call" | custom-call | flops 1048576 | bytes 1048576 | tf_op jit(solution)/shard_map/pallas_call | solution.py:164
  42.9 4.3 %collective-permute-done.5.refs_4_ = bf16[128,1024]{1,0:T(8,128)(2,1)S(1)} collective-permute-done((bf16[128,1024]{1,0:T(8,128)(2,1)}, bf16[128,1024]{1,0:T(8,128)(2,1)S(1)}, u32[]{:S(2)}, u32[]{:S(2)}) %collective-permute-start.5) | collective-permute-done | bytes 262176 | tf_op jit(solution)/shard_map/ppermute | solution.py:42
  50.7 8.3 %all-to-all-start.1 = ((bf16[16,1088,128]{2,1,0:T(8,128)(2,1)}), bf16[16,1088,128]{2,1,0:T(8,128)(2,1)}, u32[]{:S(2)}, u32[]{:S(2)}) async-start(bf16[16,1088,128]{2,1,0:T(8,128)(2,1)} %copy-done), calls=%async_computation.1 | async-start | bytes 8912896 | tf_op jit(solution)/shard_map/all_to_all | solution.py:38
  60.4 9.1 %collective-permute-start.7 = (bf16[128,1024]{1,0:T(8,128)(2,1)S(1)}, bf16[128,1024]{1,0:T(8,128)(2,1)S(1)}, u32[]{:S(2)}, u32[]{:S(2)}) collective-permute-start(bf16[128,1024]{1,0:T(8,128)(2,1)S(1)} %collective-permute-done.5.refs_4_), channel_id=1, source_target_pairs={{0,1},{1,0},{2,3},{3,2},{4,5},{5,4},{6,7},{7,6},{8,9},{9,8},{10,11... | collective-permute-start | bytes 786440 | tf_op jit(solution)/shard_map/ppermute | solution.py:42
  69.6 14.4 %all-gather = bf16[1088,256]{1,0:T(8,128)(2,1)S(1)} all-gather(bf16[272,256]{1,0:T(8,128)(2,1)S(1)} %shard_map.124), channel_id=2, replica_groups=mesh['z_lo'=4,'ring_x'=4,'ring_y'=4,'z_hi'=2,'core'=2] {'z_hi','core'}, dimensions={0}, use_global_device_ids=true | all-gather | bytes 696320 | tf_op jit(solution)/shard_map/all_gather | solution.py:526
  87.6 6.6 %shard_map.127.refs_0_.patches_ref = bf16[64,1024]{1,0:T(8,128)(2,1)S(1)} custom-call(bf16[272,1024]{1,0:T(8,128)(2,1)S(1)} %shard_map.126.extended_ref, s32[64,4]{1,0:T(8,128)S(1)} %copy.26.bounds_ref, bf16[1024,1024]{1,0:T(8,128)(2,1)S(1)} %copy-done.7, bf16[2,1024,1024]{2,1,0:T(8,128)(2,1)S(1)} %copy-done.3), custom_call_target="tpu_custom_call" | custom-call | flops 1048576 | bytes 1048576 | tf_op jit(solution)/shard_map/pallas_call | solution.py:228
  94.3 2.7 %collective-permute-start.9 = (bf16[64,1024]{1,0:T(8,128)(2,1)S(1)}, bf16[64,1024]{1,0:T(8,128)(2,1)S(1)}, u32[]{:S(2)}, u32[]{:S(2)}) collective-permute-start(bf16[64,1024]{1,0:T(8,128)(2,1)S(1)} %shard_map.127.refs_0_.patches_ref), channel_id=1, source_target_pairs={{0,194},{64,0},{128,64},{192,128},{2,192},{66,2},{130,66},{194,130... | collective-permute-start | bytes 393224 | tf_op jit(solution)/shard_map/ppermute | solution.py:80
  96.9 3.5 %collective-permute-done.8.refs_1_ = bf16[64,1024]{1,0:T(8,128)(2,1)S(1)} collective-permute-done((bf16[64,1024]{1,0:T(8,128)(2,1)S(1)}, bf16[64,1024]{1,0:T(8,128)(2,1)S(1)}, u32[]{:S(2)}, u32[]{:S(2)}) %collective-permute-start.8) | collective-permute-done | bytes 131104 | tf_op jit(solution)/shard_map/ppermute | solution.py:80
  100.4 2.7 %collective-permute-start.11 = (bf16[64,1024]{1,0:T(8,128)(2,1)S(1)}, bf16[64,1024]{1,0:T(8,128)(2,1)S(1)}, u32[]{:S(2)}, u32[]{:S(2)}) collective-permute-start(bf16[64,1024]{1,0:T(8,128)(2,1)S(1)} %collective-permute-done.9.refs_2_), channel_id=1, source_target_pairs={{0,194},{64,0},{128,64},{192,128},{2,192},{66,2},{130,66},{194,130... | collective-permute-start | bytes 393224 | tf_op jit(solution)/shard_map/ppermute | solution.py:80
  103.1 2.7 %collective-permute-done.10.refs_3_ = bf16[64,1024]{1,0:T(8,128)(2,1)S(1)} collective-permute-done((bf16[64,1024]{1,0:T(8,128)(2,1)S(1)}, bf16[64,1024]{1,0:T(8,128)(2,1)S(1)}, u32[]{:S(2)}, u32[]{:S(2)}) %collective-permute-start.10) | collective-permute-done | bytes 131104 | tf_op jit(solution)/shard_map/ppermute | solution.py:80
  105.9 2.7 %collective-permute-start.13 = (bf16[64,1024]{1,0:T(8,128)(2,1)S(1)}, bf16[64,1024]{1,0:T(8,128)(2,1)S(1)}, u32[]{:S(2)}, u32[]{:S(2)}) collective-permute-start(bf16[64,1024]{1,0:T(8,128)(2,1)S(1)} %collective-permute-done.11.refs_4_), channel_id=1, source_target_pairs={{0,194},{64,0},{128,64},{192,128},{2,192},{66,2},{130,66},{194,130... | collective-permute-start | bytes 393224 | tf_op jit(solution)/shard_map/ppermute | solution.py:80
  108.8 2.5 %collective-permute-done.12.refs_5_ = bf16[64,1024]{1,0:T(8,128)(2,1)S(1)} collective-permute-done((bf16[64,1024]{1,0:T(8,128)(2,1)S(1)}, bf16[64,1024]{1,0:T(8,128)(2,1)S(1)}, u32[]{:S(2)}, u32[]{:S(2)}) %collective-permute-start.12) | collective-permute-done | bytes 131104 | tf_op jit(solution)/shard_map/ppermute | solution.py:80
  111.3 2.7 %collective-permute-start.15 = (bf16[32,1024]{1,0:T(8,128)(2,1)S(1)}, bf16[32,1024]{1,0:T(8,128)(2,1)S(1)}, u32[]{:S(2)}, u32[]{:S(2)}) collective-permute-start(bf16[32,1024]{1,0:T(8,128)(2,1)S(1)} %slice.61), channel_id=1, source_target_pairs={{0,194},{64,0},{128,64},{192,128},{2,192},{66,2},{130,66},{194,130... | collective-permute-start | bytes 196616 | tf_op jit(solution)/shard_map/ppermute | solution.py:80
  115.7 3.7 %collective-permute-start.16 = (bf16[256,2048]{1,0:T(8,128)(2,1)S(1)}, bf16[256,2048]{1,0:T(8,128)(2,1)S(1)}, u32[]{:S(2)}, u32[]{:S(2)}) collective-permute-start(bf16[256,2048]{1,0:T(8,128)(2,1)S(1)} %shard_map.128.own_ref), channel_id=1, source_target_pairs={{0,1},{1,0},{2,3},{3,2},{4,5},{5,4},{6,7},{7,6},{8,9},{9,8},{10,11... | collective-permute-start | bytes 3145736 | tf_op jit(solution)/shard_map/ppermute | solution.py:42
  121.5 2.8 %shard_map.130.weights_ref = bf16[2,2,1024,384]{3,2,1,0:T(8,128)(2,1)S(1)} custom-call(bf16[16,1088,128]{2,1,0:T(8,128)(2,1)} %all-to-all-done.1.weights_ref), custom_call_target="tpu_custom_call" | custom-call | flops 1048576 | bytes 1048576 | tf_op jit(solution)/shard_map/pallas_call | solution.py:330
  126.6 3.0 %collective-permute-start.23 = (bf16[256,128]{1,0:T(8,128)(2,1)S(1)}, bf16[256,128]{1,0:T(8,128)(2,1)S(1)}, u32[]{:S(2)}, u32[]{:S(2)}) collective-permute-start(bf16[256,128]{1,0:T(8,128)(2,1)S(1)} %get-tuple-element.41), channel_id=1, source_target_pairs={{16,0},{32,16},{48,32},{0,48},{17,1},{33,17},{49,33},{1,49},{18,2}... | collective-permute-start | bytes 196616 | tf_op jit(solution)/shard_map/ppermute | solution.py:52
  131.1 3.2 %collective-permute-done.24 = bf16[256,128]{1,0:T(8,128)(2,1)S(1)} collective-permute-done((bf16[256,128]{1,0:T(8,128)(2,1)S(1)}, bf16[256,128]{1,0:T(8,128)(2,1)S(1)}, u32[]{:S(2)}, u32[]{:S(2)}) %collective-permute-start.24) | collective-permute-done | bytes 65568 | tf_op jit(solution)/shard_map/ppermute | solution.py:52
  139.9 2.9 %collective-permute-start.27 = (bf16[4,256,128]{2,1,0:T(8,128)(2,1)S(1)}, bf16[4,256,128]{2,1,0:T(8,128)(2,1)S(1)}, u32[]{:S(2)}, u32[]{:S(2)}) collective-permute-start(bf16[4,256,128]{2,1,0:T(8,128)(2,1)S(1)} %pad_maximum_fusion.1.refs_7_), channel_id=1, source_target_pairs={{8,0},{12,4},{0,8},{4,12},{9,1},{13,5},{1,9},{5,13},{10,2},{14,6},... | collective-permute-start | bytes 786440 | tf_op jit(solution)/shard_map/ppermute | solution.py:52
  148.4 5.8 %collective-permute-done.28.refs_10_ = bf16[4,256,128]{2,1,0:T(8,128)(2,1)S(1)} collective-permute-done((bf16[4,256,128]{2,1,0:T(8,128)(2,1)S(1)}, bf16[4,256,128]{2,1,0:T(8,128)(2,1)S(1)}, u32[]{:S(2)}, u32[]{:S(2)}) %collective-permute-start.28) | collective-permute-done | bytes 262176 | tf_op jit(solution)/shard_map/ppermute | solution.py:52
  157.1 22.6 %all-gather.1 = bf16[1024,128]{1,0:T(8,128)(2,1)S(1)} all-gather(bf16[256,128]{1,0:T(8,128)(2,1)S(1)} %shard_map.132), channel_id=3, replica_groups=mesh['z_lo'=4,'ring_x'=4,'ring_y'=4,'z_hi'=2,'core'=2] {'z_lo'}, dimensions={0}, use_global_device_ids=true | all-gather | bytes 327680 | tf_op jit(solution)/shard_map/all_gather | solution.py:583
  179.7 2.8 %shard_map.133 = (f32[2,64,1024]{2,1,0:T(8,128)S(1)}, bf16[2,64,1024]{2,1,0:T(8,128)(2,1)S(1)}) custom-call(bf16[4,256,128]{2,1,0:T(8,128)(2,1)S(1)} %bitcast.28, bf16[16,1088,128]{2,1,0:T(8,128)(2,1)} %all-to-all-done.1.weights_ref), custom_call_target="tpu_custom_call" | custom-call | flops 1048576 | bytes 1048576 | tf_op jit(solution)/shard_map/pallas_call | solution.py:425
  182.5 13.9 %collective-permute-start.29 = (bf16[2,64,1024]{2,1,0:T(8,128)(2,1)S(1)}, bf16[2,64,1024]{2,1,0:T(8,128)(2,1)S(1)}, u32[]{:S(2)}, u32[]{:S(2)}) collective-permute-start(bf16[2,64,1024]{2,1,0:T(8,128)(2,1)S(1)} %get-tuple-element.43), channel_id=1, source_target_pairs={{0,1},{1,0},{2,3},{3,2},{4,5},{5,4},{6,7},{7,6},{8,9},{9,8},{10,11... | collective-permute-start | bytes 786440 | tf_op jit(solution)/shard_map/ppermute | solution.py:42
  197.6 2.5 %collective-permute-start.30 = (bf16[64,1024]{1,0:T(8,128)(2,1)S(1)}, bf16[64,1024]{1,0:T(8,128)(2,1)S(1)}, u32[]{:S(2)}, u32[]{:S(2)}) collective-permute-start(bf16[64,1024]{1,0:T(8,128)(2,1)S(1)} %get-tuple-element.44), channel_id=1, source_target_pairs={{0,0},{1,128},{2,64},{3,192},{64,1},{65,129},{66,65},{67,193},{128... | collective-permute-start | bytes 393224 | tf_op jit(solution)/shard_map/ppermute | solution.py:587
  200.1 3.6 %collective-permute-start.31 = (bf16[64,1024]{1,0:T(8,128)(2,1)S(1)}, bf16[64,1024]{1,0:T(8,128)(2,1)S(1)}, u32[]{:S(2)}, u32[]{:S(2)}) collective-permute-start(bf16[64,1024]{1,0:T(8,128)(2,1)S(1)} %get-tuple-element.45), channel_id=1, source_target_pairs={{0,64},{1,192},{2,0},{3,128},{64,65},{65,193},{66,1},{67,129},{128... | collective-permute-start | bytes 393224 | tf_op jit(solution)/shard_map/ppermute | solution.py:587
  204.6 5.9 %collective-permute-done.31.refs_1_ = bf16[64,1024]{1,0:T(8,128)(2,1)S(1)} collective-permute-done((bf16[64,1024]{1,0:T(8,128)(2,1)S(1)}, bf16[64,1024]{1,0:T(8,128)(2,1)S(1)}, u32[]{:S(2)}, u32[]{:S(2)}) %collective-permute-start.31) | collective-permute-done | bytes 131104 | tf_op jit(solution)/shard_map/ppermute | solution.py:587
  (122 shorter events, 44.0 us)
Async XLA Ops:
  0.6 36.4 %collective-permute-start.3 = (bf16[256,1024]{1,0:T(8,128)(2,1)}, bf16[256,1024]{1,0:T(8,128)(2,1)S(1)}, u32[]{:S(2)}, u32[]{:S(2)}) collective-permute-start(bf16[256,1024]{1,0:T(8,128)(2,1)} %refs_0_.1), channel_id=1, source_target_pairs={{0,1},{1,0},{2,3},{3,2},{4,5},{5,4},{6,7},{7,6},{8,9},{9,8},{10,11... | collective-permute-start | bytes 1572872 | tf_op jit(solution)/shard_map/ppermute | solution.py:42
  8.5 28.5 %collective-permute-start = (bf16[256,512]{1,0:T(8,128)(2,1)}, bf16[256,512]{1,0:T(8,128)(2,1)}, u32[]{:S(2)}, u32[]{:S(2)}) collective-permute-start(bf16[256,512]{1,0:T(8,128)(2,1)} %get-tuple-element.24.own_ref), channel_id=1, source_target_pairs={{0,4},{4,8},{8,12},{12,16},{16,20},{20,24},{24,28},{28,32},{32,36}... | collective-permute-start | bytes 786440 | tf_op jit(solution)/shard_map/ppermute | solution.py:34
  10.6 26.4 %collective-permute-start.1 = (bf16[256,512]{1,0:T(8,128)(2,1)}, bf16[256,512]{1,0:T(8,128)(2,1)}, u32[]{:S(2)}, u32[]{:S(2)}) collective-permute-start(bf16[256,512]{1,0:T(8,128)(2,1)} %get-tuple-element.24.own_ref), channel_id=1, source_target_pairs={{0,8},{4,12},{8,16},{12,20},{16,24},{20,28},{24,32},{28,36},{32,40... | collective-permute-start | bytes 786440 | tf_op jit(solution)/shard_map/ppermute | solution.py:34
  17.1 19.9 %collective-permute-start.4 = (bf16[128,1024]{1,0:T(8,128)(2,1)}, bf16[128,1024]{1,0:T(8,128)(2,1)S(1)}, u32[]{:S(2)}, u32[]{:S(2)}) collective-permute-start(bf16[128,1024]{1,0:T(8,128)(2,1)} %get-tuple-element.53), channel_id=1, source_target_pairs={{0,2},{2,0},{1,3},{3,1},{4,6},{6,4},{5,7},{7,5},{8,10},{10,8},{9,1... | collective-permute-start | bytes 786440 | tf_op jit(solution)/shard_map/ppermute | solution.py:42
  27.1 20.0 %all-to-all-start = ((bf16[4,208,128]{2,1,0:T(8,128)(2,1)}), bf16[4,208,128]{2,1,0:T(8,128)(2,1)S(1)}, u32[]{:S(2)}, u32[]{:S(2)}) async-start(bf16[4,208,128]{2,1,0:T(8,128)(2,1)} %shard_map.125), calls=%async_computation | async-start | bytes 425984 | tf_op jit(solution)/shard_map/all_to_all | solution.py:38
  32.0 4.9 %collective-permute-start.2 = (bf16[16,1024]{1,0:T(8,128)(2,1)S(1)}, bf16[16,1024]{1,0:T(8,128)(2,1)S(1)}, u32[]{:S(2)}, u32[]{:S(2)}) collective-permute-start(bf16[16,1024]{1,0:T(8,128)(2,1)S(1)} %slice_select_fusion), channel_id=1, source_target_pairs={{4,0},{8,4},{12,8},{16,12},{20,16},{24,20},{28,24},{32,28},{36,32}... | collective-permute-start | bytes 98312 | tf_op jit(solution)/shard_map/ppermute | solution.py:34
  37.0 10.2 %collective-permute-start.5 = (bf16[128,1024]{1,0:T(8,128)(2,1)}, bf16[128,1024]{1,0:T(8,128)(2,1)S(1)}, u32[]{:S(2)}, u32[]{:S(2)}) collective-permute-start(bf16[128,1024]{1,0:T(8,128)(2,1)} %get-tuple-element.52), channel_id=1, source_target_pairs={{0,2},{2,0},{1,3},{3,1},{4,6},{6,4},{5,7},{7,5},{8,10},{10,8},{9,1... | collective-permute-start | bytes 786440 | tf_op jit(solution)/shard_map/ppermute | solution.py:42
  37.0 10.2 %collective-permute-start.6 = (bf16[128,1024]{1,0:T(8,128)(2,1)S(1)}, bf16[128,1024]{1,0:T(8,128)(2,1)}, u32[]{:S(2)}, u32[]{:S(2)}) collective-permute-start(bf16[128,1024]{1,0:T(8,128)(2,1)S(1)} %collective-permute-done.4.refs_2_), channel_id=1, source_target_pairs={{0,1},{1,0},{2,3},{3,2},{4,5},{5,4},{6,7},{7,6},{8,9},{9,8},{10,11... | collective-permute-start | bytes 786440 | tf_op jit(solution)/shard_map/ppermute | solution.py:42
  50.7 68.7 %all-to-all-start.1 = ((bf16[16,1088,128]{2,1,0:T(8,128)(2,1)}), bf16[16,1088,128]{2,1,0:T(8,128)(2,1)}, u32[]{:S(2)}, u32[]{:S(2)}) async-start(bf16[16,1088,128]{2,1,0:T(8,128)(2,1)} %copy-done), calls=%async_computation.1 | async-start | bytes 8912896 | tf_op jit(solution)/shard_map/all_to_all | solution.py:38
  60.4 23.6 %collective-permute-start.7 = (bf16[128,1024]{1,0:T(8,128)(2,1)S(1)}, bf16[128,1024]{1,0:T(8,128)(2,1)S(1)}, u32[]{:S(2)}, u32[]{:S(2)}) collective-permute-start(bf16[128,1024]{1,0:T(8,128)(2,1)S(1)} %collective-permute-done.5.refs_4_), channel_id=1, source_target_pairs={{0,1},{1,0},{2,3},{3,2},{4,5},{5,4},{6,7},{7,6},{8,9},{9,8},{10,11... | collective-permute-start | bytes 786440 | tf_op jit(solution)/shard_map/ppermute | solution.py:42
  94.2 6.2 %collective-permute-start.8 = (bf16[64,1024]{1,0:T(8,128)(2,1)S(1)}, bf16[64,1024]{1,0:T(8,128)(2,1)S(1)}, u32[]{:S(2)}, u32[]{:S(2)}) collective-permute-start(bf16[64,1024]{1,0:T(8,128)(2,1)S(1)} %shard_map.127.refs_0_.patches_ref), channel_id=1, source_target_pairs={{0,64},{64,128},{128,192},{192,2},{2,66},{66,130},{130,194},{194,0... | collective-permute-start | bytes 393224 | tf_op jit(solution)/shard_map/ppermute | solution.py:80
  94.3 6.1 %collective-permute-start.9 = (bf16[64,1024]{1,0:T(8,128)(2,1)S(1)}, bf16[64,1024]{1,0:T(8,128)(2,1)S(1)}, u32[]{:S(2)}, u32[]{:S(2)}) collective-permute-start(bf16[64,1024]{1,0:T(8,128)(2,1)S(1)} %shard_map.127.refs_0_.patches_ref), channel_id=1, source_target_pairs={{0,194},{64,0},{128,64},{192,128},{2,192},{66,2},{130,66},{194,130... | collective-permute-start | bytes 393224 | tf_op jit(solution)/shard_map/ppermute | solution.py:80
  100.4 5.4 %collective-permute-start.10 = (bf16[64,1024]{1,0:T(8,128)(2,1)S(1)}, bf16[64,1024]{1,0:T(8,128)(2,1)S(1)}, u32[]{:S(2)}, u32[]{:S(2)}) collective-permute-start(bf16[64,1024]{1,0:T(8,128)(2,1)S(1)} %collective-permute-done.8.refs_1_), channel_id=1, source_target_pairs={{0,64},{64,128},{128,192},{192,2},{2,66},{66,130},{130,194},{194,0... | collective-permute-start | bytes 393224 | tf_op jit(solution)/shard_map/ppermute | solution.py:80
  100.4 5.4 %collective-permute-start.11 = (bf16[64,1024]{1,0:T(8,128)(2,1)S(1)}, bf16[64,1024]{1,0:T(8,128)(2,1)S(1)}, u32[]{:S(2)}, u32[]{:S(2)}) collective-permute-start(bf16[64,1024]{1,0:T(8,128)(2,1)S(1)} %collective-permute-done.9.refs_2_), channel_id=1, source_target_pairs={{0,194},{64,0},{128,64},{192,128},{2,192},{66,2},{130,66},{194,130... | collective-permute-start | bytes 393224 | tf_op jit(solution)/shard_map/ppermute | solution.py:80
  105.8 5.4 %collective-permute-start.12 = (bf16[64,1024]{1,0:T(8,128)(2,1)S(1)}, bf16[64,1024]{1,0:T(8,128)(2,1)S(1)}, u32[]{:S(2)}, u32[]{:S(2)}) collective-permute-start(bf16[64,1024]{1,0:T(8,128)(2,1)S(1)} %collective-permute-done.10.refs_3_), channel_id=1, source_target_pairs={{0,64},{64,128},{128,192},{192,2},{2,66},{66,130},{130,194},{194,0... | collective-permute-start | bytes 393224 | tf_op jit(solution)/shard_map/ppermute | solution.py:80
  105.9 5.4 %collective-permute-start.13 = (bf16[64,1024]{1,0:T(8,128)(2,1)S(1)}, bf16[64,1024]{1,0:T(8,128)(2,1)S(1)}, u32[]{:S(2)}, u32[]{:S(2)}) collective-permute-start(bf16[64,1024]{1,0:T(8,128)(2,1)S(1)} %collective-permute-done.11.refs_4_), channel_id=1, source_target_pairs={{0,194},{64,0},{128,64},{192,128},{2,192},{66,2},{130,66},{194,130... | collective-permute-start | bytes 393224 | tf_op jit(solution)/shard_map/ppermute | solution.py:80
  115.7 9.4 %collective-permute-start.16 = (bf16[256,2048]{1,0:T(8,128)(2,1)S(1)}, bf16[256,2048]{1,0:T(8,128)(2,1)S(1)}, u32[]{:S(2)}, u32[]{:S(2)}) collective-permute-start(bf16[256,2048]{1,0:T(8,128)(2,1)S(1)} %shard_map.128.own_ref), channel_id=1, source_target_pairs={{0,1},{1,0},{2,3},{3,2},{4,5},{5,4},{6,7},{7,6},{8,9},{9,8},{10,11... | collective-permute-start | bytes 3145736 | tf_op jit(solution)/shard_map/ppermute | solution.py:42
  126.6 4.5 %collective-permute-start.23 = (bf16[256,128]{1,0:T(8,128)(2,1)S(1)}, bf16[256,128]{1,0:T(8,128)(2,1)S(1)}, u32[]{:S(2)}, u32[]{:S(2)}) collective-permute-start(bf16[256,128]{1,0:T(8,128)(2,1)S(1)} %get-tuple-element.41), channel_id=1, source_target_pairs={{16,0},{32,16},{48,32},{0,48},{17,1},{33,17},{49,33},{1,49},{18,2}... | collective-permute-start | bytes 196616 | tf_op jit(solution)/shard_map/ppermute | solution.py:52
  129.6 4.7 %collective-permute-start.24 = (bf16[256,128]{1,0:T(8,128)(2,1)S(1)}, bf16[256,128]{1,0:T(8,128)(2,1)S(1)}, u32[]{:S(2)}, u32[]{:S(2)}) collective-permute-start(bf16[256,128]{1,0:T(8,128)(2,1)S(1)} %get-tuple-element.41), channel_id=1, source_target_pairs={{32,0},{48,16},{0,32},{16,48},{33,1},{49,17},{1,33},{17,49},{34,2}... | collective-permute-start | bytes 196616 | tf_op jit(solution)/shard_map/ppermute | solution.py:52
  130.2 6.1 %collective-permute-start.25 = (bf16[256,128]{1,0:T(8,128)(2,1)S(1)}, bf16[256,128]{1,0:T(8,128)(2,1)S(1)}, u32[]{:S(2)}, u32[]{:S(2)}) collective-permute-start(bf16[256,128]{1,0:T(8,128)(2,1)S(1)} %get-tuple-element.41), channel_id=1, source_target_pairs={{48,0},{0,16},{16,32},{32,48},{49,1},{1,17},{17,33},{33,49},{50,2}... | collective-permute-start | bytes 196616 | tf_op jit(solution)/shard_map/ppermute | solution.py:52
  136.3 10.0 %collective-permute-start.26 = (bf16[4,256,128]{2,1,0:T(8,128)(2,1)S(1)}, bf16[4,256,128]{2,1,0:T(8,128)(2,1)S(1)}, u32[]{:S(2)}, u32[]{:S(2)}) collective-permute-start(bf16[4,256,128]{2,1,0:T(8,128)(2,1)S(1)} %pad_maximum_fusion.1.refs_7_), channel_id=1, source_target_pairs={{4,0},{8,4},{12,8},{0,12},{5,1},{9,5},{13,9},{1,13},{6,2},{10,6},{... | collective-permute-start | bytes 786440 | tf_op jit(solution)/shard_map/ppermute | solution.py:52
  137.8 7.1 %collective-permute-start.17 = (bf16[256,128]{1,0:T(8,128)(2,1)S(1)}, bf16[256,128]{1,0:T(8,128)(2,1)S(1)}, u32[]{:S(2)}, u32[]{:S(2)}) collective-permute-start(bf16[256,128]{1,0:T(8,128)(2,1)S(1)} %get-tuple-element.40), channel_id=1, source_target_pairs={{4,0},{8,4},{12,8},{0,12},{5,1},{9,5},{13,9},{1,13},{6,2},{10,6},{... | collective-permute-start | bytes 196616 | tf_op jit(solution)/shard_map/ppermute | solution.py:52
  138.7 6.6 %collective-permute-start.18 = (bf16[256,128]{1,0:T(8,128)(2,1)S(1)}, bf16[256,128]{1,0:T(8,128)(2,1)S(1)}, u32[]{:S(2)}, u32[]{:S(2)}) collective-permute-start(bf16[256,128]{1,0:T(8,128)(2,1)S(1)} %get-tuple-element.40), channel_id=1, source_target_pairs={{8,0},{12,4},{0,8},{4,12},{9,1},{13,5},{1,9},{5,13},{10,2},{14,6},... | collective-permute-start | bytes 196616 | tf_op jit(solution)/shard_map/ppermute | solution.py:52
  139.6 5.7 %collective-permute-start.19 = (bf16[256,128]{1,0:T(8,128)(2,1)S(1)}, bf16[256,128]{1,0:T(8,128)(2,1)S(1)}, u32[]{:S(2)}, u32[]{:S(2)}) collective-permute-start(bf16[256,128]{1,0:T(8,128)(2,1)S(1)} %get-tuple-element.40), channel_id=1, source_target_pairs={{12,0},{0,4},{4,8},{8,12},{13,1},{1,5},{5,9},{9,13},{14,2},{2,6},{... | collective-permute-start | bytes 196616 | tf_op jit(solution)/shard_map/ppermute | solution.py:52
  139.9 8.5 %collective-permute-start.27 = (bf16[4,256,128]{2,1,0:T(8,128)(2,1)S(1)}, bf16[4,256,128]{2,1,0:T(8,128)(2,1)S(1)}, u32[]{:S(2)}, u32[]{:S(2)}) collective-permute-start(bf16[4,256,128]{2,1,0:T(8,128)(2,1)S(1)} %pad_maximum_fusion.1.refs_7_), channel_id=1, source_target_pairs={{8,0},{12,4},{0,8},{4,12},{9,1},{13,5},{1,9},{5,13},{10,2},{14,6},... | collective-permute-start | bytes 786440 | tf_op jit(solution)/shard_map/ppermute | solution.py:52
  144.9 9.4 %collective-permute-start.28 = (bf16[4,256,128]{2,1,0:T(8,128)(2,1)S(1)}, bf16[4,256,128]{2,1,0:T(8,128)(2,1)S(1)}, u32[]{:S(2)}, u32[]{:S(2)}) collective-permute-start(bf16[4,256,128]{2,1,0:T(8,128)(2,1)S(1)} %pad_maximum_fusion.1.refs_7_), channel_id=1, source_target_pairs={{12,0},{0,4},{4,8},{8,12},{13,1},{1,5},{5,9},{9,13},{14,2},{2,6},{... | collective-permute-start | bytes 786440 | tf_op jit(solution)/shard_map/ppermute | solution.py:52
  145.3 8.9 %collective-permute-start.20 = (bf16[4,256,128]{2,1,0:T(8,128)(2,1)S(1)}, bf16[4,256,128]{2,1,0:T(8,128)(2,1)S(1)}, u32[]{:S(2)}, u32[]{:S(2)}) collective-permute-start(bf16[4,256,128]{2,1,0:T(8,128)(2,1)S(1)} %pad_maximum_fusion.refs_3_), channel_id=1, source_target_pairs={{16,0},{32,16},{48,32},{0,48},{17,1},{33,17},{49,33},{1,49},{18,2}... | collective-permute-start | bytes 786440 | tf_op jit(solution)/shard_map/ppermute | solution.py:52
  145.4 8.8 %collective-permute-start.21 = (bf16[4,256,128]{2,1,0:T(8,128)(2,1)S(1)}, bf16[4,256,128]{2,1,0:T(8,128)(2,1)S(1)}, u32[]{:S(2)}, u32[]{:S(2)}) collective-permute-start(bf16[4,256,128]{2,1,0:T(8,128)(2,1)S(1)} %pad_maximum_fusion.refs_3_), channel_id=1, source_target_pairs={{32,0},{48,16},{0,32},{16,48},{33,1},{49,17},{1,33},{17,49},{34,2}... | collective-permute-start | bytes 786440 | tf_op jit(solution)/shard_map/ppermute | solution.py:52
  146.3 8.8 %collective-permute-start.22 = (bf16[4,256,128]{2,1,0:T(8,128)(2,1)S(1)}, bf16[4,256,128]{2,1,0:T(8,128)(2,1)S(1)}, u32[]{:S(2)}, u32[]{:S(2)}) collective-permute-start(bf16[4,256,128]{2,1,0:T(8,128)(2,1)S(1)} %pad_maximum_fusion.refs_3_), channel_id=1, source_target_pairs={{48,0},{0,16},{16,32},{32,48},{49,1},{1,17},{17,33},{33,49},{50,2}... | collective-permute-start | bytes 786440 | tf_op jit(solution)/shard_map/ppermute | solution.py:52
  182.5 15.0 %collective-permute-start.29 = (bf16[2,64,1024]{2,1,0:T(8,128)(2,1)S(1)}, bf16[2,64,1024]{2,1,0:T(8,128)(2,1)S(1)}, u32[]{:S(2)}, u32[]{:S(2)}) collective-permute-start(bf16[2,64,1024]{2,1,0:T(8,128)(2,1)S(1)} %get-tuple-element.43), channel_id=1, source_target_pairs={{0,1},{1,0},{2,3},{3,2},{4,5},{5,4},{6,7},{7,6},{8,9},{9,8},{10,11... | collective-permute-start | bytes 786440 | tf_op jit(solution)/shard_map/ppermute | solution.py:42
  197.6 7.0 %collective-permute-start.30 = (bf16[64,1024]{1,0:T(8,128)(2,1)S(1)}, bf16[64,1024]{1,0:T(8,128)(2,1)S(1)}, u32[]{:S(2)}, u32[]{:S(2)}) collective-permute-start(bf16[64,1024]{1,0:T(8,128)(2,1)S(1)} %get-tuple-element.44), channel_id=1, source_target_pairs={{0,0},{1,128},{2,64},{3,192},{64,1},{65,129},{66,65},{67,193},{128... | collective-permute-start | bytes 393224 | tf_op jit(solution)/shard_map/ppermute | solution.py:587
  200.1 10.3 %collective-permute-start.31 = (bf16[64,1024]{1,0:T(8,128)(2,1)S(1)}, bf16[64,1024]{1,0:T(8,128)(2,1)S(1)}, u32[]{:S(2)}, u32[]{:S(2)}) collective-permute-start(bf16[64,1024]{1,0:T(8,128)(2,1)S(1)} %get-tuple-element.45), channel_id=1, source_target_pairs={{0,64},{1,192},{2,0},{3,128},{64,65},{65,193},{66,1},{67,129},{128... | collective-permute-start | bytes 393224 | tf_op jit(solution)/shard_map/ppermute | solution.py:587
  (13 other events, 140.0 us)

commit v3 on v2

--- a/solution.py
+++ b/solution.py
@@ -302,7 +302,7 @@
 
     return on_chip(
         kernel,
-        blank((copies, total, HD)),
+        pltpu.HBM((copies, total, HD), bf16),
         grid=(copies,),
         in_specs=[
             pl.BlockSpec(out_part.shape, lambda i: (0, 0)),
@@ -507,8 +507,8 @@
     by_head = exchanged(by_head, ZL)
     cut = lat_proj_out.shape[1]
 
-    half = enc_proj_out.shape[0] // 2
-    high_a, high_b = (swapped(enc_proj_out[at : at + half], ZH) for at in (0, half))
+    most = enc_proj_out.shape[0] // 2
+    high_a, high_b = (swapped(part, ZH) for part in (enc_proj_out[:most], enc_proj_out[most:]))
     out_side = swapped(enc_proj_out, CO)
 
     near_kv, far_kv, edge, out_side, high_a = lax.optimization_barrier(
@@ -518,12 +518,11 @@
     more_q, more_kv = encoder_heads(edge, enc_gain, enc_qkv)
     attended = encoder_attention(own_q, more_q, far_kv, near_kv, own_kv, more_kv, anchor)
     both_a = swapped(high_a, CO)
-    attended, by_head, high_b, both_a = lax.optimization_barrier(
-        (attended, by_head, high_b, both_a)
-    )
+    attended, by_head, both_a = lax.optimization_barrier((attended, by_head, both_a))
     by_head = exchanged(copied_weights(lat_proj_out.T, by_head, groups), ROWS)
+    attended = lax.all_gather(attended, TP)
+    attended, high_b = lax.optimization_barrier((attended, high_b))
     both_b = swapped(high_b, CO)
-    attended = lax.all_gather(attended, TP)
     extended = encoder_output(
         byte_states,
         edge,
@@ -533,8 +532,8 @@
             (out_side, 1, 0),
             (high_a, 2, 0),
             (both_a, 3, 0),
-            (high_b, 2, half),
-            (both_b, 3, half),
+            (high_b, 2, most),
+            (both_b, 3, most),
         ),
     )
     encoded = extended[:byte_rows]

time: 213 us -> 206 us (0.967)
  starting transfers between devices: 88.5 us -> 77.7 us
  local copies, waits for them, and re-layouts: 15.5 us -> 21.9 us
  Pallas kernels: 24.9 us -> 28.5 us
  waiting for transfers between devices: 40.3 us -> 36.9 us
  blocking collectives: 37 us -> 33.9 us
    all_gather x1, blocking collectives: 22.6 us -> 10.9 us  [shards(): kept, sent = partial_outputs(lax.all_gather(heads, ZL), by_head)]
    ppermute x7, starting transfers between devices: 39.3 us -> 27.7 us  [swapped(): return lax.ppermute(value, axis, [(0, 1), (1, 0)])]
    all_gather x1, blocking collectives: 14.4 us -> 23 us  [shards(): attended = lax.all_gather(attended, TP)]
    pallas_call x1, Pallas kernels: 0.59 us -> 6.01 us  [copied_weights(): on_chip(kernel, pltpu.HBM((copies, total, HD), bf16), grid=(copies,), in_...]
    unnamed x22 -> x44, local copies, waits for them, and re-layouts: 7.92 us -> 13.1 us
    ppermute x7, waiting for transfers between devices: 5.47 us -> 1.18 us  [swapped(): return lax.ppermute(value, axis, [(0, 1), (1, 0)])]
where the time goes in v3:
time: 206 us; the launch traced here: 204 us
  starting transfers between devices  77.7 us (38%)
  waiting for transfers between devices  36.9 us (18%)
  blocking collectives  33.9 us (16%)
  Pallas kernels  28.5 us (14%)
  local copies, waits for them, and re-layouts  21.9 us (11%)
  between operations  2.98 us (1%)
  other arithmetic  2.1 us (1%)
    ppermute x7, starting transfers between devices, swapped(): return lax.ppermute(value, axis, [(0, 1), (1, 0)])  27.7 us
    all_gather x1, blocking collectives, shards(): attended = lax.all_gather(attended, TP)  23 us
    ppermute x12, waiting for transfers between devices, around_ring(): lax.ppermute(value, axis, [((i + k) % count, i) for i in range(count)])  14.9 us
    ppermute x12, starting transfers between devices, around_ring(): lax.ppermute(value, axis, [((i + k) % count, i) for i in range(count)])  13.5 us
    unnamed x44, local copies, waits for them, and re-layouts  13.1 us
    all_to_all x2, starting transfers between devices, exchanged(): return lax.all_to_all(pieces, axis, split_axis=0, concat_axis=0, tiled=True)  12.6 us
    all_gather x1, blocking collectives, shards(): kept, sent = partial_outputs(lax.all_gather(heads, ZL), by_head)  10.9 us
    ppermute x8, starting transfers between devices, moved(): lax.ppermute(part, (ZL, ZH), [(named(z), named(z + step)) for z in range(...  10.8 us
  transfers between devices with their start and end apart: 34, of which 15 were waited for; matrix products, arithmetic and copies ran while one was open for 5% of the time, Pallas kernels for 8%

profile of v3, /device:TPU:1, one launch (start us, length us, event | category | flops | bytes accessed | tf_op | source)
XLA Modules:
  0.0 204.1 jit_solution(13952871551952908193)
XLA Ops:
  0.6 3.3 %collective-permute-start.3 = (bf16[256,1024]{1,0:T(8,128)(2,1)}, bf16[256,1024]{1,0:T(8,128)(2,1)S(1)}, u32[]{:S(2)}, u32[]{:S(2)}) collective-permute-start(bf16[256,1024]{1,0:T(8,128)(2,1)} %refs_0_.1), channel_id=1, source_target_pairs={{0,1},{1,0},{2,3},{3,2},{4,5},{5,4},{6,7},{7,6},{8,9},{9,8},{10,11... | collective-permute-start | bytes 1572872 | tf_op jit(solution)/shard_map/ppermute | solution.py:42
  7.8 2.2 %collective-permute-start = (bf16[256,512]{1,0:T(8,128)(2,1)S(1)}, bf16[256,512]{1,0:T(8,128)(2,1)}, u32[]{:S(2)}, u32[]{:S(2)}) collective-permute-start(bf16[256,512]{1,0:T(8,128)(2,1)S(1)} %get-tuple-element.25.own_ref), channel_id=1, source_target_pairs={{0,4},{4,8},{8,12},{12,16},{16,20},{20,24},{24,28},{28,32},{32,36}... | collective-permute-start | bytes 786440 | tf_op jit(solution)/shard_map/ppermute | solution.py:34
  10.0 4.6 %collective-permute-start.1 = (bf16[256,512]{1,0:T(8,128)(2,1)S(1)}, bf16[256,512]{1,0:T(8,128)(2,1)}, u32[]{:S(2)}, u32[]{:S(2)}) collective-permute-start(bf16[256,512]{1,0:T(8,128)(2,1)S(1)} %get-tuple-element.25.own_ref), channel_id=1, source_target_pairs={{0,8},{4,12},{8,16},{12,20},{16,24},{20,28},{24,32},{28,36},{32,40... | collective-permute-start | bytes 786440 | tf_op jit(solution)/shard_map/ppermute | solution.py:34
  16.4 6.9 %collective-permute-start.4 = (bf16[128,1024]{1,0:T(8,128)(2,1)}, bf16[128,1024]{1,0:T(8,128)(2,1)S(1)}, u32[]{:S(2)}, u32[]{:S(2)}) collective-permute-start(bf16[128,1024]{1,0:T(8,128)(2,1)} %get-tuple-element.55), channel_id=1, source_target_pairs={{0,2},{2,0},{1,3},{3,1},{4,6},{6,4},{5,7},{7,5},{8,10},{10,8},{9,1... | collective-permute-start | bytes 786440 | tf_op jit(solution)/shard_map/ppermute | solution.py:42
  26.4 3.4 %all-to-all-start = ((bf16[4,208,128]{2,1,0:T(8,128)(2,1)}), bf16[4,208,128]{2,1,0:T(8,128)(2,1)S(1)}, u32[]{:S(2)}, u32[]{:S(2)}) async-start(bf16[4,208,128]{2,1,0:T(8,128)(2,1)} %shard_map.125), calls=%async_computation | async-start | bytes 425984 | tf_op jit(solution)/shard_map/all_to_all | solution.py:38
  32.6 3.7 %collective-permute-done.2.states_ref.edge_ref = bf16[16,1024]{1,0:T(8,128)(2,1)S(1)} collective-permute-done((bf16[16,1024]{1,0:T(8,128)(2,1)S(1)}, bf16[16,1024]{1,0:T(8,128)(2,1)S(1)}, u32[]{:S(2)}, u32[]{:S(2)}) %collective-permute-start.2) | collective-permute-done | bytes 32800 | tf_op jit(solution)/shard_map/ppermute | solution.py:34
  40.4 3.0 %shard_map.124 = bf16[272,256]{1,0:T(8,128)(2,1)S(1)} custom-call(s32[1]{0:T(128)} %bitcast.1.anchor_ref, bf16[256,256]{1,0:T(8,128)(2,1)S(1)} %copy-done.18, bf16[16,256]{1,0:T(8,128)(2,1)S(1)} %get-tuple-element.28.mq_ref, bf16[256,512]{1,0:T(8,128)(2,1)} %collective-permute-done.1.far_ref, bf16[256,512]{1,0:T(8,128)(2,1)} %collective-permute-done.near_ref, ...), custom_call_target="tpu_custom_call" | custom-call | flops 1048576 | bytes 1048576 | tf_op jit(solution)/shard_map/pallas_call | solution.py:164
  44.3 6.0 %shard_map.129 = bf16[16,1088,128]{2,1,0:T(8,128)(2,1)} custom-call(bf16[64,512]{1,0:T(8,128)(2,1)S(1)} %bitcast.29, bf16[4,208,128]{2,1,0:T(8,128)(2,1)S(1)} %all-to-all-done.by_head_ref), custom_call_target="tpu_custom_call" | custom-call | flops 1048576 | bytes 1048576 | tf_op jit(solution)/shard_map/pallas_call | solution.py:303
  50.3 9.2 %all-to-all-start.1 = ((bf16[16,1088,128]{2,1,0:T(8,128)(2,1)}), bf16[16,1088,128]{2,1,0:T(8,128)(2,1)}, u32[]{:S(2)}, u32[]{:S(2)}) async-start(bf16[16,1088,128]{2,1,0:T(8,128)(2,1)} %shard_map.129), calls=%async_computation.1 | async-start | bytes 8912896 | tf_op jit(solution)/shard_map/all_to_all | solution.py:38
  61.6 23.0 %all-gather = bf16[1088,256]{1,0:T(8,128)(2,1)S(1)} all-gather(bf16[272,256]{1,0:T(8,128)(2,1)S(1)} %shard_map.124), channel_id=2, replica_groups=mesh['z_lo'=4,'ring_x'=4,'ring_y'=4,'z_hi'=2,'core'=2] {'z_hi','core'}, dimensions={0}, use_global_device_ids=true | all-gather | bytes 696320 | tf_op jit(solution)/shard_map/all_gather | solution.py:523
  90.7 2.2 %copy-done.2 = bf16[2,1024,1024]{2,1,0:T(8,128)(2,1)S(1)} copy-done((bf16[2,1024,1024]{2,1,0:T(8,128)(2,1)S(1)}, bf16[2,1024,1024]{2,1,0:T(8,128)(2,1)}, u32[]{:S(2)}) %copy-start.2) | copy-done | bytes 4194328
  93.7 6.6 %shard_map.127.refs_0_.patches_ref = bf16[64,1024]{1,0:T(8,128)(2,1)S(1)} custom-call(bf16[272,1024]{1,0:T(8,128)(2,1)S(1)} %shard_map.126.extended_ref, s32[64,4]{1,0:T(8,128)S(1)} %copy-done.16, bf16[1024,1024]{1,0:T(8,128)(2,1)S(1)} %copy-done.6, bf16[2,1024,1024]{2,1,0:T(8,128)(2,1)S(1)} %copy-done.2), custom_call_target="tpu_custom_call" | custom-call | flops 1048576 | bytes 1048576 | tf_op jit(solution)/shard_map/pallas_call | solution.py:228
  103.0 3.4 %collective-permute-done.8.refs_1_ = bf16[64,1024]{1,0:T(8,128)(2,1)S(1)} collective-permute-done((bf16[64,1024]{1,0:T(8,128)(2,1)S(1)}, bf16[64,1024]{1,0:T(8,128)(2,1)S(1)}, u32[]{:S(2)}, u32[]{:S(2)}) %collective-permute-start.8) | collective-permute-done | bytes 131104 | tf_op jit(solution)/shard_map/ppermute | solution.py:80
  106.4 2.7 %collective-permute-start.11 = (bf16[64,1024]{1,0:T(8,128)(2,1)S(1)}, bf16[64,1024]{1,0:T(8,128)(2,1)S(1)}, u32[]{:S(2)}, u32[]{:S(2)}) collective-permute-start(bf16[64,1024]{1,0:T(8,128)(2,1)S(1)} %collective-permute-done.9.refs_2_), channel_id=1, source_target_pairs={{0,194},{64,0},{128,64},{192,128},{2,192},{66,2},{130,66},{194,130... | collective-permute-start | bytes 393224 | tf_op jit(solution)/shard_map/ppermute | solution.py:80
  109.1 2.7 %collective-permute-done.10.refs_3_ = bf16[64,1024]{1,0:T(8,128)(2,1)S(1)} collective-permute-done((bf16[64,1024]{1,0:T(8,128)(2,1)S(1)}, bf16[64,1024]{1,0:T(8,128)(2,1)S(1)}, u32[]{:S(2)}, u32[]{:S(2)}) %collective-permute-start.10) | collective-permute-done | bytes 131104 | tf_op jit(solution)/shard_map/ppermute | solution.py:80
  111.9 2.7 %collective-permute-start.13 = (bf16[64,1024]{1,0:T(8,128)(2,1)S(1)}, bf16[64,1024]{1,0:T(8,128)(2,1)S(1)}, u32[]{:S(2)}, u32[]{:S(2)}) collective-permute-start(bf16[64,1024]{1,0:T(8,128)(2,1)S(1)} %collective-permute-done.11.refs_4_), channel_id=1, source_target_pairs={{0,194},{64,0},{128,64},{192,128},{2,192},{66,2},{130,66},{194,130... | collective-permute-start | bytes 393224 | tf_op jit(solution)/shard_map/ppermute | solution.py:80
  114.8 2.5 %collective-permute-done.12.refs_5_ = bf16[64,1024]{1,0:T(8,128)(2,1)S(1)} collective-permute-done((bf16[64,1024]{1,0:T(8,128)(2,1)S(1)}, bf16[64,1024]{1,0:T(8,128)(2,1)S(1)}, u32[]{:S(2)}, u32[]{:S(2)}) %collective-permute-start.12) | collective-permute-done | bytes 131104 | tf_op jit(solution)/shard_map/ppermute | solution.py:80
  117.3 2.7 %collective-permute-start.15 = (bf16[32,1024]{1,0:T(8,128)(2,1)S(1)}, bf16[32,1024]{1,0:T(8,128)(2,1)S(1)}, u32[]{:S(2)}, u32[]{:S(2)}) collective-permute-start(bf16[32,1024]{1,0:T(8,128)(2,1)S(1)} %slice.61), channel_id=1, source_target_pairs={{0,194},{64,0},{128,64},{192,128},{2,192},{66,2},{130,66},{194,130... | collective-permute-start | bytes 196616 | tf_op jit(solution)/shard_map/ppermute | solution.py:80
  121.7 3.8 %collective-permute-start.16 = (bf16[256,2048]{1,0:T(8,128)(2,1)S(1)}, bf16[256,2048]{1,0:T(8,128)(2,1)S(1)}, u32[]{:S(2)}, u32[]{:S(2)}) collective-permute-start(bf16[256,2048]{1,0:T(8,128)(2,1)S(1)} %shard_map.128.own_ref), channel_id=1, source_target_pairs={{0,1},{1,0},{2,3},{3,2},{4,5},{5,4},{6,7},{7,6},{8,9},{9,8},{10,11... | collective-permute-start | bytes 3145736 | tf_op jit(solution)/shard_map/ppermute | solution.py:42
  127.6 2.8 %shard_map.130.weights_ref = bf16[2,2,1024,384]{3,2,1,0:T(8,128)(2,1)S(1)} custom-call(bf16[16,1088,128]{2,1,0:T(8,128)(2,1)} %all-to-all-done.1.weights_ref), custom_call_target="tpu_custom_call" | custom-call | flops 1048576 | bytes 1048576 | tf_op jit(solution)/shard_map/pallas_call | solution.py:330
  132.7 2.6 %collective-permute-start.23 = (bf16[256,128]{1,0:T(8,128)(2,1)S(1)}, bf16[256,128]{1,0:T(8,128)(2,1)S(1)}, u32[]{:S(2)}, u32[]{:S(2)}) collective-permute-start(bf16[256,128]{1,0:T(8,128)(2,1)S(1)} %get-tuple-element.43), channel_id=1, source_target_pairs={{16,0},{32,16},{48,32},{0,48},{17,1},{33,17},{49,33},{1,49},{18,2}... | collective-permute-start | bytes 196616 | tf_op jit(solution)/shard_map/ppermute | solution.py:52
  136.8 3.2 %collective-permute-done.24 = bf16[256,128]{1,0:T(8,128)(2,1)S(1)} collective-permute-done((bf16[256,128]{1,0:T(8,128)(2,1)S(1)}, bf16[256,128]{1,0:T(8,128)(2,1)S(1)}, u32[]{:S(2)}, u32[]{:S(2)}) %collective-permute-start.24) | collective-permute-done | bytes 65568 | tf_op jit(solution)/shard_map/ppermute | solution.py:52
  142.0 2.5 %collective-permute-start.26 = (bf16[4,256,128]{2,1,0:T(8,128)(2,1)S(1)}, bf16[4,256,128]{2,1,0:T(8,128)(2,1)S(1)}, u32[]{:S(2)}, u32[]{:S(2)}) collective-permute-start(bf16[4,256,128]{2,1,0:T(8,128)(2,1)S(1)} %pad_maximum_fusion.1.refs_7_), channel_id=1, source_target_pairs={{4,0},{8,4},{12,8},{0,12},{5,1},{9,5},{13,9},{1,13},{6,2},{10,6},{... | collective-permute-start | bytes 786440 | tf_op jit(solution)/shard_map/ppermute | solution.py:52
  146.0 3.5 %collective-permute-start.27 = (bf16[4,256,128]{2,1,0:T(8,128)(2,1)S(1)}, bf16[4,256,128]{2,1,0:T(8,128)(2,1)S(1)}, u32[]{:S(2)}, u32[]{:S(2)}) collective-permute-start(bf16[4,256,128]{2,1,0:T(8,128)(2,1)S(1)} %pad_maximum_fusion.1.refs_7_), channel_id=1, source_target_pairs={{8,0},{12,4},{0,8},{4,12},{9,1},{13,5},{1,9},{5,13},{10,2},{14,6},... | collective-permute-start | bytes 786440 | tf_op jit(solution)/shard_map/ppermute | solution.py:52
  154.4 2.7 %collective-permute-done.27.refs_9_ = bf16[4,256,128]{2,1,0:T(8,128)(2,1)S(1)} collective-permute-done((bf16[4,256,128]{2,1,0:T(8,128)(2,1)S(1)}, bf16[4,256,128]{2,1,0:T(8,128)(2,1)S(1)}, u32[]{:S(2)}, u32[]{:S(2)}) %collective-permute-start.27) | collective-permute-done | bytes 262176 | tf_op jit(solution)/shard_map/ppermute | solution.py:52
  157.0 3.9 %collective-permute-done.28.refs_10_ = bf16[4,256,128]{2,1,0:T(8,128)(2,1)S(1)} collective-permute-done((bf16[4,256,128]{2,1,0:T(8,128)(2,1)S(1)}, bf16[4,256,128]{2,1,0:T(8,128)(2,1)S(1)}, u32[]{:S(2)}, u32[]{:S(2)}) %collective-permute-start.28) | collective-permute-done | bytes 262176 | tf_op jit(solution)/shard_map/ppermute | solution.py:52
  164.0 10.9 %all-gather.1 = bf16[1024,128]{1,0:T(8,128)(2,1)S(1)} all-gather(bf16[256,128]{1,0:T(8,128)(2,1)S(1)} %shard_map.132), channel_id=3, replica_groups=mesh['z_lo'=4,'ring_x'=4,'ring_y'=4,'z_hi'=2,'core'=2] {'z_lo'}, dimensions={0}, use_global_device_ids=true | all-gather | bytes 327680 | tf_op jit(solution)/shard_map/all_gather | solution.py:582
  174.9 2.8 %shard_map.133 = (f32[2,64,1024]{2,1,0:T(8,128)S(1)}, bf16[2,64,1024]{2,1,0:T(8,128)(2,1)S(1)}) custom-call(bf16[4,256,128]{2,1,0:T(8,128)(2,1)S(1)} %bitcast.28, bf16[16,1088,128]{2,1,0:T(8,128)(2,1)} %all-to-all-done.1.weights_ref), custom_call_target="tpu_custom_call" | custom-call | flops 1048576 | bytes 1048576 | tf_op jit(solution)/shard_map/pallas_call | solution.py:425
  177.6 11.6 %collective-permute-start.29 = (bf16[2,64,1024]{2,1,0:T(8,128)(2,1)S(1)}, bf16[2,64,1024]{2,1,0:T(8,128)(2,1)S(1)}, u32[]{:S(2)}, u32[]{:S(2)}) collective-permute-start(bf16[2,64,1024]{2,1,0:T(8,128)(2,1)S(1)} %get-tuple-element.45), channel_id=1, source_target_pairs={{0,1},{1,0},{2,3},{3,2},{4,5},{5,4},{6,7},{7,6},{8,9},{9,8},{10,11... | collective-permute-start | bytes 786440 | tf_op jit(solution)/shard_map/ppermute | solution.py:42
  190.4 2.5 %collective-permute-start.30 = (bf16[64,1024]{1,0:T(8,128)(2,1)S(1)}, bf16[64,1024]{1,0:T(8,128)(2,1)S(1)}, u32[]{:S(2)}, u32[]{:S(2)}) collective-permute-start(bf16[64,1024]{1,0:T(8,128)(2,1)S(1)} %get-tuple-element.46), channel_id=1, source_target_pairs={{0,0},{1,128},{2,64},{3,192},{64,1},{65,129},{66,65},{67,193},{128... | collective-permute-start | bytes 393224 | tf_op jit(solution)/shard_map/ppermute | solution.py:586
  193.0 2.5 %collective-permute-start.31 = (bf16[64,1024]{1,0:T(8,128)(2,1)S(1)}, bf16[64,1024]{1,0:T(8,128)(2,1)S(1)}, u32[]{:S(2)}, u32[]{:S(2)}) collective-permute-start(bf16[64,1024]{1,0:T(8,128)(2,1)S(1)} %get-tuple-element.47), channel_id=1, source_target_pairs={{0,64},{1,192},{2,0},{3,128},{64,65},{65,193},{66,1},{67,129},{128... | collective-permute-start | bytes 393224 | tf_op jit(solution)/shard_map/ppermute | solution.py:586
  196.7 6.6 %collective-permute-done.31.refs_1_ = bf16[64,1024]{1,0:T(8,128)(2,1)S(1)} collective-permute-done((bf16[64,1024]{1,0:T(8,128)(2,1)S(1)}, bf16[64,1024]{1,0:T(8,128)(2,1)S(1)}, u32[]{:S(2)}, u32[]{:S(2)}) %collective-permute-start.31) | collective-permute-done | bytes 131104 | tf_op jit(solution)/shard_map/ppermute | solution.py:586
  (144 shorter events, 48.4 us)
Async XLA Ops:
  0.6 35.7 %collective-permute-start.3 = (bf16[256,1024]{1,0:T(8,128)(2,1)}, bf16[256,1024]{1,0:T(8,128)(2,1)S(1)}, u32[]{:S(2)}, u32[]{:S(2)}) collective-permute-start(bf16[256,1024]{1,0:T(8,128)(2,1)} %refs_0_.1), channel_id=1, source_target_pairs={{0,1},{1,0},{2,3},{3,2},{4,5},{5,4},{6,7},{7,6},{8,9},{9,8},{10,11... | collective-permute-start | bytes 1572872 | tf_op jit(solution)/shard_map/ppermute | solution.py:42
  7.8 28.5 %collective-permute-start = (bf16[256,512]{1,0:T(8,128)(2,1)S(1)}, bf16[256,512]{1,0:T(8,128)(2,1)}, u32[]{:S(2)}, u32[]{:S(2)}) collective-permute-start(bf16[256,512]{1,0:T(8,128)(2,1)S(1)} %get-tuple-element.25.own_ref), channel_id=1, source_target_pairs={{0,4},{4,8},{8,12},{12,16},{16,20},{20,24},{24,28},{28,32},{32,36}... | collective-permute-start | bytes 786440 | tf_op jit(solution)/shard_map/ppermute | solution.py:34
  10.0 26.3 %collective-permute-start.1 = (bf16[256,512]{1,0:T(8,128)(2,1)S(1)}, bf16[256,512]{1,0:T(8,128)(2,1)}, u32[]{:S(2)}, u32[]{:S(2)}) collective-permute-start(bf16[256,512]{1,0:T(8,128)(2,1)S(1)} %get-tuple-element.25.own_ref), channel_id=1, source_target_pairs={{0,8},{4,12},{8,16},{12,20},{16,24},{20,28},{24,32},{28,36},{32,40... | collective-permute-start | bytes 786440 | tf_op jit(solution)/shard_map/ppermute | solution.py:34
  16.4 19.9 %collective-permute-start.4 = (bf16[128,1024]{1,0:T(8,128)(2,1)}, bf16[128,1024]{1,0:T(8,128)(2,1)S(1)}, u32[]{:S(2)}, u32[]{:S(2)}) collective-permute-start(bf16[128,1024]{1,0:T(8,128)(2,1)} %get-tuple-element.55), channel_id=1, source_target_pairs={{0,2},{2,0},{1,3},{3,1},{4,6},{6,4},{5,7},{7,5},{8,10},{10,8},{9,1... | collective-permute-start | bytes 786440 | tf_op jit(solution)/shard_map/ppermute | solution.py:42
  26.4 17.0 %all-to-all-start = ((bf16[4,208,128]{2,1,0:T(8,128)(2,1)}), bf16[4,208,128]{2,1,0:T(8,128)(2,1)S(1)}, u32[]{:S(2)}, u32[]{:S(2)}) async-start(bf16[4,208,128]{2,1,0:T(8,128)(2,1)} %shard_map.125), calls=%async_computation | async-start | bytes 425984 | tf_op jit(solution)/shard_map/all_to_all | solution.py:38
  31.3 4.9 %collective-permute-start.2 = (bf16[16,1024]{1,0:T(8,128)(2,1)S(1)}, bf16[16,1024]{1,0:T(8,128)(2,1)S(1)}, u32[]{:S(2)}, u32[]{:S(2)}) collective-permute-start(bf16[16,1024]{1,0:T(8,128)(2,1)S(1)} %slice_select_fusion), channel_id=1, source_target_pairs={{4,0},{8,4},{12,8},{16,12},{20,16},{24,20},{28,24},{32,28},{36,32}... | collective-permute-start | bytes 98312 | tf_op jit(solution)/shard_map/ppermute | solution.py:34
  36.3 7.1 %collective-permute-start.5 = (bf16[128,1024]{1,0:T(8,128)(2,1)S(1)}, bf16[128,1024]{1,0:T(8,128)(2,1)S(1)}, u32[]{:S(2)}, u32[]{:S(2)}) collective-permute-start(bf16[128,1024]{1,0:T(8,128)(2,1)S(1)} %collective-permute-done.4.refs_2_), channel_id=1, source_target_pairs={{0,1},{1,0},{2,3},{3,2},{4,5},{5,4},{6,7},{7,6},{8,9},{9,8},{10,11... | collective-permute-start | bytes 786440 | tf_op jit(solution)/shard_map/ppermute | solution.py:42
  50.3 75.2 %all-to-all-start.1 = ((bf16[16,1088,128]{2,1,0:T(8,128)(2,1)}), bf16[16,1088,128]{2,1,0:T(8,128)(2,1)}, u32[]{:S(2)}, u32[]{:S(2)}) async-start(bf16[16,1088,128]{2,1,0:T(8,128)(2,1)} %shard_map.129), calls=%async_computation.1 | async-start | bytes 8912896 | tf_op jit(solution)/shard_map/all_to_all | solution.py:38
  59.5 25.1 %collective-permute-start.6 = (bf16[128,1024]{1,0:T(8,128)(2,1)S(1)}, bf16[128,1024]{1,0:T(8,128)(2,1)S(1)}, u32[]{:S(2)}, u32[]{:S(2)}) collective-permute-start(bf16[128,1024]{1,0:T(8,128)(2,1)S(1)} %copy-done.20), channel_id=1, source_target_pairs={{0,2},{2,0},{1,3},{3,1},{4,6},{6,4},{5,7},{7,5},{8,10},{10,8},{9,1... | collective-permute-start | bytes 786440 | tf_op jit(solution)/shard_map/ppermute | solution.py:42
  100.3 6.1 %collective-permute-start.8 = (bf16[64,1024]{1,0:T(8,128)(2,1)S(1)}, bf16[64,1024]{1,0:T(8,128)(2,1)S(1)}, u32[]{:S(2)}, u32[]{:S(2)}) collective-permute-start(bf16[64,1024]{1,0:T(8,128)(2,1)S(1)} %shard_map.127.refs_0_.patches_ref), channel_id=1, source_target_pairs={{0,64},{64,128},{128,192},{192,2},{2,66},{66,130},{130,194},{194,0... | collective-permute-start | bytes 393224 | tf_op jit(solution)/shard_map/ppermute | solution.py:80
  101.5 4.9 %collective-permute-start.9 = (bf16[64,1024]{1,0:T(8,128)(2,1)S(1)}, bf16[64,1024]{1,0:T(8,128)(2,1)S(1)}, u32[]{:S(2)}, u32[]{:S(2)}) collective-permute-start(bf16[64,1024]{1,0:T(8,128)(2,1)S(1)} %shard_map.127.refs_0_.patches_ref), channel_id=1, source_target_pairs={{0,194},{64,0},{128,64},{192,128},{2,192},{66,2},{130,66},{194,130... | collective-permute-start | bytes 393224 | tf_op jit(solution)/shard_map/ppermute | solution.py:80
  106.4 5.4 %collective-permute-start.10 = (bf16[64,1024]{1,0:T(8,128)(2,1)S(1)}, bf16[64,1024]{1,0:T(8,128)(2,1)S(1)}, u32[]{:S(2)}, u32[]{:S(2)}) collective-permute-start(bf16[64,1024]{1,0:T(8,128)(2,1)S(1)} %collective-permute-done.8.refs_1_), channel_id=1, source_target_pairs={{0,64},{64,128},{128,192},{192,2},{2,66},{66,130},{130,194},{194,0... | collective-permute-start | bytes 393224 | tf_op jit(solution)/shard_map/ppermute | solution.py:80
  106.4 5.4 %collective-permute-start.11 = (bf16[64,1024]{1,0:T(8,128)(2,1)S(1)}, bf16[64,1024]{1,0:T(8,128)(2,1)S(1)}, u32[]{:S(2)}, u32[]{:S(2)}) collective-permute-start(bf16[64,1024]{1,0:T(8,128)(2,1)S(1)} %collective-permute-done.9.refs_2_), channel_id=1, source_target_pairs={{0,194},{64,0},{128,64},{192,128},{2,192},{66,2},{130,66},{194,130... | collective-permute-start | bytes 393224 | tf_op jit(solution)/shard_map/ppermute | solution.py:80
  111.9 5.4 %collective-permute-start.12 = (bf16[64,1024]{1,0:T(8,128)(2,1)S(1)}, bf16[64,1024]{1,0:T(8,128)(2,1)S(1)}, u32[]{:S(2)}, u32[]{:S(2)}) collective-permute-start(bf16[64,1024]{1,0:T(8,128)(2,1)S(1)} %collective-permute-done.10.refs_3_), channel_id=1, source_target_pairs={{0,64},{64,128},{128,192},{192,2},{2,66},{66,130},{130,194},{194,0... | collective-permute-start | bytes 393224 | tf_op jit(solution)/shard_map/ppermute | solution.py:80
  111.9 5.4 %collective-permute-start.13 = (bf16[64,1024]{1,0:T(8,128)(2,1)S(1)}, bf16[64,1024]{1,0:T(8,128)(2,1)S(1)}, u32[]{:S(2)}, u32[]{:S(2)}) collective-permute-start(bf16[64,1024]{1,0:T(8,128)(2,1)S(1)} %collective-permute-done.11.refs_4_), channel_id=1, source_target_pairs={{0,194},{64,0},{128,64},{192,128},{2,192},{66,2},{130,66},{194,130... | collective-permute-start | bytes 393224 | tf_op jit(solution)/shard_map/ppermute | solution.py:80
  117.3 4.3 %collective-permute-start.14 = (bf16[32,1024]{1,0:T(8,128)(2,1)S(1)}, bf16[32,1024]{1,0:T(8,128)(2,1)S(1)}, u32[]{:S(2)}, u32[]{:S(2)}) collective-permute-start(bf16[32,1024]{1,0:T(8,128)(2,1)S(1)} %slice.60), channel_id=1, source_target_pairs={{0,64},{64,128},{128,192},{192,2},{2,66},{66,130},{130,194},{194,0... | collective-permute-start | bytes 196616 | tf_op jit(solution)/shard_map/ppermute | solution.py:80
  117.3 4.3 %collective-permute-start.15 = (bf16[32,1024]{1,0:T(8,128)(2,1)S(1)}, bf16[32,1024]{1,0:T(8,128)(2,1)S(1)}, u32[]{:S(2)}, u32[]{:S(2)}) collective-permute-start(bf16[32,1024]{1,0:T(8,128)(2,1)S(1)} %slice.61), channel_id=1, source_target_pairs={{0,194},{64,0},{128,64},{192,128},{2,192},{66,2},{130,66},{194,130... | collective-permute-start | bytes 196616 | tf_op jit(solution)/shard_map/ppermute | solution.py:80
  121.7 9.5 %collective-permute-start.16 = (bf16[256,2048]{1,0:T(8,128)(2,1)S(1)}, bf16[256,2048]{1,0:T(8,128)(2,1)S(1)}, u32[]{:S(2)}, u32[]{:S(2)}) collective-permute-start(bf16[256,2048]{1,0:T(8,128)(2,1)S(1)} %shard_map.128.own_ref), channel_id=1, source_target_pairs={{0,1},{1,0},{2,3},{3,2},{4,5},{5,4},{6,7},{7,6},{8,9},{9,8},{10,11... | collective-permute-start | bytes 3145736 | tf_op jit(solution)/shard_map/ppermute | solution.py:42
  135.3 4.7 %collective-permute-start.24 = (bf16[256,128]{1,0:T(8,128)(2,1)S(1)}, bf16[256,128]{1,0:T(8,128)(2,1)S(1)}, u32[]{:S(2)}, u32[]{:S(2)}) collective-permute-start(bf16[256,128]{1,0:T(8,128)(2,1)S(1)} %get-tuple-element.43), channel_id=1, source_target_pairs={{32,0},{48,16},{0,32},{16,48},{33,1},{49,17},{1,33},{17,49},{34,2}... | collective-permute-start | bytes 196616 | tf_op jit(solution)/shard_map/ppermute | solution.py:52
  135.9 6.1 %collective-permute-start.25 = (bf16[256,128]{1,0:T(8,128)(2,1)S(1)}, bf16[256,128]{1,0:T(8,128)(2,1)S(1)}, u32[]{:S(2)}, u32[]{:S(2)}) collective-permute-start(bf16[256,128]{1,0:T(8,128)(2,1)S(1)} %get-tuple-element.43), channel_id=1, source_target_pairs={{48,0},{0,16},{16,32},{32,48},{49,1},{1,17},{17,33},{33,49},{50,2}... | collective-permute-start | bytes 196616 | tf_op jit(solution)/shard_map/ppermute | solution.py:52
  142.0 10.8 %collective-permute-start.26 = (bf16[4,256,128]{2,1,0:T(8,128)(2,1)S(1)}, bf16[4,256,128]{2,1,0:T(8,128)(2,1)S(1)}, u32[]{:S(2)}, u32[]{:S(2)}) collective-permute-start(bf16[4,256,128]{2,1,0:T(8,128)(2,1)S(1)} %pad_maximum_fusion.1.refs_7_), channel_id=1, source_target_pairs={{4,0},{8,4},{12,8},{0,12},{5,1},{9,5},{13,9},{1,13},{6,2},{10,6},{... | collective-permute-start | bytes 786440 | tf_op jit(solution)/shard_map/ppermute | solution.py:52
  144.5 6.9 %collective-permute-start.17 = (bf16[256,128]{1,0:T(8,128)(2,1)S(1)}, bf16[256,128]{1,0:T(8,128)(2,1)S(1)}, u32[]{:S(2)}, u32[]{:S(2)}) collective-permute-start(bf16[256,128]{1,0:T(8,128)(2,1)S(1)} %get-tuple-element.42), channel_id=1, source_target_pairs={{4,0},{8,4},{12,8},{0,12},{5,1},{9,5},{13,9},{1,13},{6,2},{10,6},{... | collective-permute-start | bytes 196616 | tf_op jit(solution)/shard_map/ppermute | solution.py:52
  144.7 7.4 %collective-permute-start.18 = (bf16[256,128]{1,0:T(8,128)(2,1)S(1)}, bf16[256,128]{1,0:T(8,128)(2,1)S(1)}, u32[]{:S(2)}, u32[]{:S(2)}) collective-permute-start(bf16[256,128]{1,0:T(8,128)(2,1)S(1)} %get-tuple-element.42), channel_id=1, source_target_pairs={{8,0},{12,4},{0,8},{4,12},{9,1},{13,5},{1,9},{5,13},{10,2},{14,6},... | collective-permute-start | bytes 196616 | tf_op jit(solution)/shard_map/ppermute | solution.py:52
  145.3 6.8 %collective-permute-start.19 = (bf16[256,128]{1,0:T(8,128)(2,1)S(1)}, bf16[256,128]{1,0:T(8,128)(2,1)S(1)}, u32[]{:S(2)}, u32[]{:S(2)}) collective-permute-start(bf16[256,128]{1,0:T(8,128)(2,1)S(1)} %get-tuple-element.42), channel_id=1, source_target_pairs={{12,0},{0,4},{4,8},{8,12},{13,1},{1,5},{5,9},{9,13},{14,2},{2,6},{... | collective-permute-start | bytes 196616 | tf_op jit(solution)/shard_map/ppermute | solution.py:52
  146.0 11.1 %collective-permute-start.27 = (bf16[4,256,128]{2,1,0:T(8,128)(2,1)S(1)}, bf16[4,256,128]{2,1,0:T(8,128)(2,1)S(1)}, u32[]{:S(2)}, u32[]{:S(2)}) collective-permute-start(bf16[4,256,128]{2,1,0:T(8,128)(2,1)S(1)} %pad_maximum_fusion.1.refs_7_), channel_id=1, source_target_pairs={{8,0},{12,4},{0,8},{4,12},{9,1},{13,5},{1,9},{5,13},{10,2},{14,6},... | collective-permute-start | bytes 786440 | tf_op jit(solution)/shard_map/ppermute | solution.py:52
  151.4 9.6 %collective-permute-start.28 = (bf16[4,256,128]{2,1,0:T(8,128)(2,1)S(1)}, bf16[4,256,128]{2,1,0:T(8,128)(2,1)S(1)}, u32[]{:S(2)}, u32[]{:S(2)}) collective-permute-start(bf16[4,256,128]{2,1,0:T(8,128)(2,1)S(1)} %pad_maximum_fusion.1.refs_7_), channel_id=1, source_target_pairs={{12,0},{0,4},{4,8},{8,12},{13,1},{1,5},{5,9},{9,13},{14,2},{2,6},{... | collective-permute-start | bytes 786440 | tf_op jit(solution)/shard_map/ppermute | solution.py:52
  152.2 8.8 %collective-permute-start.20 = (bf16[4,256,128]{2,1,0:T(8,128)(2,1)S(1)}, bf16[4,256,128]{2,1,0:T(8,128)(2,1)S(1)}, u32[]{:S(2)}, u32[]{:S(2)}) collective-permute-start(bf16[4,256,128]{2,1,0:T(8,128)(2,1)S(1)} %pad_maximum_fusion.refs_3_), channel_id=1, source_target_pairs={{16,0},{32,16},{48,32},{0,48},{17,1},{33,17},{49,33},{1,49},{18,2}... | collective-permute-start | bytes 786440 | tf_op jit(solution)/shard_map/ppermute | solution.py:52
  152.2 8.7 %collective-permute-start.21 = (bf16[4,256,128]{2,1,0:T(8,128)(2,1)S(1)}, bf16[4,256,128]{2,1,0:T(8,128)(2,1)S(1)}, u32[]{:S(2)}, u32[]{:S(2)}) collective-permute-start(bf16[4,256,128]{2,1,0:T(8,128)(2,1)S(1)} %pad_maximum_fusion.refs_3_), channel_id=1, source_target_pairs={{32,0},{48,16},{0,32},{16,48},{33,1},{49,17},{1,33},{17,49},{34,2}... | collective-permute-start | bytes 786440 | tf_op jit(solution)/shard_map/ppermute | solution.py:52
  152.8 9.1 %collective-permute-start.22 = (bf16[4,256,128]{2,1,0:T(8,128)(2,1)S(1)}, bf16[4,256,128]{2,1,0:T(8,128)(2,1)S(1)}, u32[]{:S(2)}, u32[]{:S(2)}) collective-permute-start(bf16[4,256,128]{2,1,0:T(8,128)(2,1)S(1)} %pad_maximum_fusion.refs_3_), channel_id=1, source_target_pairs={{48,0},{0,16},{16,32},{32,48},{49,1},{1,17},{17,33},{33,49},{50,2}... | collective-permute-start | bytes 786440 | tf_op jit(solution)/shard_map/ppermute | solution.py:52
  177.6 12.7 %collective-permute-start.29 = (bf16[2,64,1024]{2,1,0:T(8,128)(2,1)S(1)}, bf16[2,64,1024]{2,1,0:T(8,128)(2,1)S(1)}, u32[]{:S(2)}, u32[]{:S(2)}) collective-permute-start(bf16[2,64,1024]{2,1,0:T(8,128)(2,1)S(1)} %get-tuple-element.45), channel_id=1, source_target_pairs={{0,1},{1,0},{2,3},{3,2},{4,5},{5,4},{6,7},{7,6},{8,9},{9,8},{10,11... | collective-permute-start | bytes 786440 | tf_op jit(solution)/shard_map/ppermute | solution.py:42
  190.4 6.3 %collective-permute-start.30 = (bf16[64,1024]{1,0:T(8,128)(2,1)S(1)}, bf16[64,1024]{1,0:T(8,128)(2,1)S(1)}, u32[]{:S(2)}, u32[]{:S(2)}) collective-permute-start(bf16[64,1024]{1,0:T(8,128)(2,1)S(1)} %get-tuple-element.46), channel_id=1, source_target_pairs={{0,0},{1,128},{2,64},{3,192},{64,1},{65,129},{66,65},{67,193},{128... | collective-permute-start | bytes 393224 | tf_op jit(solution)/shard_map/ppermute | solution.py:586
  193.0 10.4 %collective-permute-start.31 = (bf16[64,1024]{1,0:T(8,128)(2,1)S(1)}, bf16[64,1024]{1,0:T(8,128)(2,1)S(1)}, u32[]{:S(2)}, u32[]{:S(2)}) collective-permute-start(bf16[64,1024]{1,0:T(8,128)(2,1)S(1)} %get-tuple-element.47), channel_id=1, source_target_pairs={{0,64},{1,192},{2,0},{3,128},{64,65},{65,193},{66,1},{67,129},{128... | collective-permute-start | bytes 393224 | tf_op jit(solution)/shard_map/ppermute | solution.py:586
  (24 other events, 185.7 us)

commit v4 on v3

--- a/solution.py
+++ b/solution.py
@@ -302,7 +302,7 @@
 
     return on_chip(
         kernel,
-        pltpu.HBM((copies, total, HD), bf16),
+        blank((copies, total, HD)),
         grid=(copies,),
         in_specs=[
             pl.BlockSpec(out_part.shape, lambda i: (0, 0)),
@@ -508,7 +508,8 @@
     cut = lat_proj_out.shape[1]
 
     most = enc_proj_out.shape[0] // 2
-    high_a, high_b = (swapped(part, ZH) for part in (enc_proj_out[:most], enc_proj_out[most:]))
+    own_q, late = lax.optimization_barrier((own_q, enc_proj_out))
+    high_a, high_b = (swapped(part, ZH) for part in (enc_proj_out[:most], late[most:]))
     out_side = swapped(enc_proj_out, CO)
 
     near_kv, far_kv, edge, out_side, high_a = lax.optimization_barrier(

time: 206 us -> 203 us (0.985)
  Pallas kernels: 28.5 us -> 23.1 us
  local copies, waits for them, and re-layouts: 21.9 us -> 24.5 us
    pallas_call x1, Pallas kernels: 6.01 us -> 0.58 us  [copied_weights(): on_chip(kernel, blank((copies, total, HD)), grid=(copies,), in_specs=[pl....]
    unnamed x44, local copies, waits for them, and re-layouts: 13.1 us -> 15.9 us
where the time goes in v4:
time: 203 us; the launch traced here: 201 us
  starting transfers between devices  77.5 us (38%)
  waiting for transfers between devices  37.1 us (18%)
  blocking collectives  33.9 us (17%)
  local copies, waits for them, and re-layouts  24.5 us (12%)
  Pallas kernels  23.1 us (11%)
  between operations  2.99 us (1%)
  other arithmetic  2.1 us (1%)
    ppermute x7, starting transfers between devices, swapped(): return lax.ppermute(value, axis, [(0, 1), (1, 0)])  27.6 us
    all_gather x1, blocking collectives, shards(): attended = lax.all_gather(attended, TP)  23 us
    unnamed x44, local copies, waits for them, and re-layouts  15.9 us
    ppermute x12, waiting for transfers between devices, around_ring(): lax.ppermute(value, axis, [((i + k) % count, i) for i in range(count)])  15.1 us
    ppermute x12, starting transfers between devices, around_ring(): lax.ppermute(value, axis, [((i + k) % count, i) for i in range(count)])  13.4 us
    all_to_all x2, starting transfers between devices, exchanged(): return lax.all_to_all(pieces, axis, split_axis=0, concat_axis=0, tiled=True)  12.6 us
    all_gather x1, blocking collectives, shards(): kept, sent = partial_outputs(lax.all_gather(heads, ZL), by_head)  10.9 us
    ppermute x8, starting transfers between devices, moved(): lax.ppermute(part, (ZL, ZH), [(named(z), named(z + step)) for z in range(...  10.8 us
  transfers between devices with their start and end apart: 34, of which 15 were waited for; matrix products, arithmetic and copies ran while one was open for 5% of the time, Pallas kernels for 8%

profile of v4, /device:TPU:1, one launch (start us, length us, event | category | flops | bytes accessed | tf_op | source)
XLA Modules:
  0.0 201.2 jit_solution(15679296506102261485)
XLA Ops:
  0.6 3.3 %collective-permute-start.3 = (bf16[256,1024]{1,0:T(8,128)(2,1)}, bf16[256,1024]{1,0:T(8,128)(2,1)S(1)}, u32[]{:S(2)}, u32[]{:S(2)}) collective-permute-start(bf16[256,1024]{1,0:T(8,128)(2,1)} %refs_0_.1), channel_id=1, source_target_pairs={{0,1},{1,0},{2,3},{3,2},{4,5},{5,4},{6,7},{7,6},{8,9},{9,8},{10,11... | collective-permute-start | bytes 1572872 | tf_op jit(solution)/shard_map/ppermute | solution.py:42
  8.4 2.2 %collective-permute-start = (bf16[256,512]{1,0:T(8,128)(2,1)S(1)}, bf16[256,512]{1,0:T(8,128)(2,1)}, u32[]{:S(2)}, u32[]{:S(2)}) collective-permute-start(bf16[256,512]{1,0:T(8,128)(2,1)S(1)} %get-tuple-element.27.own_ref), channel_id=1, source_target_pairs={{0,4},{4,8},{8,12},{12,16},{16,20},{20,24},{24,28},{28,32},{32,36}... | collective-permute-start | bytes 786440 | tf_op jit(solution)/shard_map/ppermute | solution.py:34
  10.6 4.5 %collective-permute-start.1 = (bf16[256,512]{1,0:T(8,128)(2,1)S(1)}, bf16[256,512]{1,0:T(8,128)(2,1)}, u32[]{:S(2)}, u32[]{:S(2)}) collective-permute-start(bf16[256,512]{1,0:T(8,128)(2,1)S(1)} %get-tuple-element.27.own_ref), channel_id=1, source_target_pairs={{0,8},{4,12},{8,16},{12,20},{16,24},{20,28},{24,32},{28,36},{32,40... | collective-permute-start | bytes 786440 | tf_op jit(solution)/shard_map/ppermute | solution.py:34
  16.8 6.9 %collective-permute-start.4 = (bf16[128,1024]{1,0:T(8,128)(2,1)}, bf16[128,1024]{1,0:T(8,128)(2,1)S(1)}, u32[]{:S(2)}, u32[]{:S(2)}) collective-permute-start(bf16[128,1024]{1,0:T(8,128)(2,1)} %slice.47), channel_id=1, source_target_pairs={{0,2},{2,0},{1,3},{3,1},{4,6},{6,4},{5,7},{7,5},{8,10},{10,8},{9,1... | collective-permute-start | bytes 786440 | tf_op jit(solution)/shard_map/ppermute | solution.py:42
  26.9 3.4 %all-to-all-start = ((bf16[4,208,128]{2,1,0:T(8,128)(2,1)}), bf16[4,208,128]{2,1,0:T(8,128)(2,1)S(1)}, u32[]{:S(2)}, u32[]{:S(2)}) async-start(bf16[4,208,128]{2,1,0:T(8,128)(2,1)} %shard_map.125), calls=%async_computation | async-start | bytes 425984 | tf_op jit(solution)/shard_map/all_to_all | solution.py:38
  33.1 3.7 %collective-permute-done.2.states_ref.edge_ref = bf16[16,1024]{1,0:T(8,128)(2,1)S(1)} collective-permute-done((bf16[16,1024]{1,0:T(8,128)(2,1)S(1)}, bf16[16,1024]{1,0:T(8,128)(2,1)S(1)}, u32[]{:S(2)}, u32[]{:S(2)}) %collective-permute-start.2) | collective-permute-done | bytes 32800 | tf_op jit(solution)/shard_map/ppermute | solution.py:34
  40.8 3.0 %shard_map.124 = bf16[272,256]{1,0:T(8,128)(2,1)S(1)} custom-call(s32[1]{0:T(128)} %bitcast.1.anchor_ref, bf16[256,256]{1,0:T(8,128)(2,1)S(1)} %copy-done.19, bf16[16,256]{1,0:T(8,128)(2,1)S(1)} %get-tuple-element.31.mq_ref, bf16[256,512]{1,0:T(8,128)(2,1)} %collective-permute-done.1.far_ref, bf16[256,512]{1,0:T(8,128)(2,1)} %collective-permute-done.near_ref, ...), custom_call_target="tpu_custom_call" | custom-call | flops 1048576 | bytes 1048576 | tf_op jit(solution)/shard_map/pallas_call | solution.py:164
  45.3 2.1 %copy-done = bf16[16,1088,128]{2,1,0:T(8,128)(2,1)} copy-done((bf16[16,1088,128]{2,1,0:T(8,128)(2,1)}, bf16[16,1088,128]{2,1,0:T(8,128)(2,1)S(1)}, u32[]{:S(2)}) %copy-start) | copy-done | bytes 4456472
  47.5 9.2 %all-to-all-start.1 = ((bf16[16,1088,128]{2,1,0:T(8,128)(2,1)}), bf16[16,1088,128]{2,1,0:T(8,128)(2,1)}, u32[]{:S(2)}, u32[]{:S(2)}) async-start(bf16[16,1088,128]{2,1,0:T(8,128)(2,1)} %copy-done), calls=%async_computation.1 | async-start | bytes 8912896 | tf_op jit(solution)/shard_map/all_to_all | solution.py:38
  58.8 23.0 %all-gather = bf16[1088,256]{1,0:T(8,128)(2,1)S(1)} all-gather(bf16[272,256]{1,0:T(8,128)(2,1)S(1)} %shard_map.124), channel_id=2, replica_groups=mesh['z_lo'=4,'ring_x'=4,'ring_y'=4,'z_hi'=2,'core'=2] {'z_hi','core'}, dimensions={0}, use_global_device_ids=true | all-gather | bytes 696320 | tf_op jit(solution)/shard_map/all_gather | solution.py:524
  87.9 2.2 %copy-done.3 = bf16[2,1024,1024]{2,1,0:T(8,128)(2,1)S(1)} copy-done((bf16[2,1024,1024]{2,1,0:T(8,128)(2,1)S(1)}, bf16[2,1024,1024]{2,1,0:T(8,128)(2,1)}, u32[]{:S(2)}) %copy-start.3) | copy-done | bytes 4194328
  90.8 6.6 %shard_map.127.refs_0_.patches_ref = bf16[64,1024]{1,0:T(8,128)(2,1)S(1)} custom-call(bf16[272,1024]{1,0:T(8,128)(2,1)S(1)} %shard_map.126.extended_ref, s32[64,4]{1,0:T(8,128)S(1)} %copy-done.17, bf16[1024,1024]{1,0:T(8,128)(2,1)S(1)} %copy-done.7, bf16[2,1024,1024]{2,1,0:T(8,128)(2,1)S(1)} %copy-done.3), custom_call_target="tpu_custom_call" | custom-call | flops 1048576 | bytes 1048576 | tf_op jit(solution)/shard_map/pallas_call | solution.py:228
  100.2 3.4 %collective-permute-done.8.refs_1_ = bf16[64,1024]{1,0:T(8,128)(2,1)S(1)} collective-permute-done((bf16[64,1024]{1,0:T(8,128)(2,1)S(1)}, bf16[64,1024]{1,0:T(8,128)(2,1)S(1)}, u32[]{:S(2)}, u32[]{:S(2)}) %collective-permute-start.8) | collective-permute-done | bytes 131104 | tf_op jit(solution)/shard_map/ppermute | solution.py:80
  103.6 2.7 %collective-permute-start.11 = (bf16[64,1024]{1,0:T(8,128)(2,1)S(1)}, bf16[64,1024]{1,0:T(8,128)(2,1)S(1)}, u32[]{:S(2)}, u32[]{:S(2)}) collective-permute-start(bf16[64,1024]{1,0:T(8,128)(2,1)S(1)} %collective-permute-done.9.refs_2_), channel_id=1, source_target_pairs={{0,194},{64,0},{128,64},{192,128},{2,192},{66,2},{130,66},{194,130... | collective-permute-start | bytes 393224 | tf_op jit(solution)/shard_map/ppermute | solution.py:80
  106.3 2.7 %collective-permute-done.10.refs_3_ = bf16[64,1024]{1,0:T(8,128)(2,1)S(1)} collective-permute-done((bf16[64,1024]{1,0:T(8,128)(2,1)S(1)}, bf16[64,1024]{1,0:T(8,128)(2,1)S(1)}, u32[]{:S(2)}, u32[]{:S(2)}) %collective-permute-start.10) | collective-permute-done | bytes 131104 | tf_op jit(solution)/shard_map/ppermute | solution.py:80
  109.0 2.7 %collective-permute-start.13 = (bf16[64,1024]{1,0:T(8,128)(2,1)S(1)}, bf16[64,1024]{1,0:T(8,128)(2,1)S(1)}, u32[]{:S(2)}, u32[]{:S(2)}) collective-permute-start(bf16[64,1024]{1,0:T(8,128)(2,1)S(1)} %collective-permute-done.11.refs_4_), channel_id=1, source_target_pairs={{0,194},{64,0},{128,64},{192,128},{2,192},{66,2},{130,66},{194,130... | collective-permute-start | bytes 393224 | tf_op jit(solution)/shard_map/ppermute | solution.py:80
  112.0 2.5 %collective-permute-done.12.refs_5_ = bf16[64,1024]{1,0:T(8,128)(2,1)S(1)} collective-permute-done((bf16[64,1024]{1,0:T(8,128)(2,1)S(1)}, bf16[64,1024]{1,0:T(8,128)(2,1)S(1)}, u32[]{:S(2)}, u32[]{:S(2)}) %collective-permute-start.12) | collective-permute-done | bytes 131104 | tf_op jit(solution)/shard_map/ppermute | solution.py:80
  114.5 2.7 %collective-permute-start.15 = (bf16[32,1024]{1,0:T(8,128)(2,1)S(1)}, bf16[32,1024]{1,0:T(8,128)(2,1)S(1)}, u32[]{:S(2)}, u32[]{:S(2)}) collective-permute-start(bf16[32,1024]{1,0:T(8,128)(2,1)S(1)} %slice.61), channel_id=1, source_target_pairs={{0,194},{64,0},{128,64},{192,128},{2,192},{66,2},{130,66},{194,130... | collective-permute-start | bytes 196616 | tf_op jit(solution)/shard_map/ppermute | solution.py:80
  118.9 3.8 %collective-permute-start.16 = (bf16[256,2048]{1,0:T(8,128)(2,1)S(1)}, bf16[256,2048]{1,0:T(8,128)(2,1)S(1)}, u32[]{:S(2)}, u32[]{:S(2)}) collective-permute-start(bf16[256,2048]{1,0:T(8,128)(2,1)S(1)} %shard_map.128.own_ref), channel_id=1, source_target_pairs={{0,1},{1,0},{2,3},{3,2},{4,5},{5,4},{6,7},{7,6},{8,9},{9,8},{10,11... | collective-permute-start | bytes 3145736 | tf_op jit(solution)/shard_map/ppermute | solution.py:42
  124.8 2.8 %shard_map.130.weights_ref = bf16[2,2,1024,384]{3,2,1,0:T(8,128)(2,1)S(1)} custom-call(bf16[16,1088,128]{2,1,0:T(8,128)(2,1)} %all-to-all-done.1.weights_ref), custom_call_target="tpu_custom_call" | custom-call | flops 1048576 | bytes 1048576 | tf_op jit(solution)/shard_map/pallas_call | solution.py:330
  129.9 2.6 %collective-permute-start.23 = (bf16[256,128]{1,0:T(8,128)(2,1)S(1)}, bf16[256,128]{1,0:T(8,128)(2,1)S(1)}, u32[]{:S(2)}, u32[]{:S(2)}) collective-permute-start(bf16[256,128]{1,0:T(8,128)(2,1)S(1)} %get-tuple-element.47), channel_id=1, source_target_pairs={{16,0},{32,16},{48,32},{0,48},{17,1},{33,17},{49,33},{1,49},{18,2}... | collective-permute-start | bytes 196616 | tf_op jit(solution)/shard_map/ppermute | solution.py:52
  133.9 3.2 %collective-permute-done.24 = bf16[256,128]{1,0:T(8,128)(2,1)S(1)} collective-permute-done((bf16[256,128]{1,0:T(8,128)(2,1)S(1)}, bf16[256,128]{1,0:T(8,128)(2,1)S(1)}, u32[]{:S(2)}, u32[]{:S(2)}) %collective-permute-start.24) | collective-permute-done | bytes 65568 | tf_op jit(solution)/shard_map/ppermute | solution.py:52
  139.2 2.5 %collective-permute-start.26 = (bf16[4,256,128]{2,1,0:T(8,128)(2,1)S(1)}, bf16[4,256,128]{2,1,0:T(8,128)(2,1)S(1)}, u32[]{:S(2)}, u32[]{:S(2)}) collective-permute-start(bf16[4,256,128]{2,1,0:T(8,128)(2,1)S(1)} %pad_maximum_fusion.1.refs_7_), channel_id=1, source_target_pairs={{4,0},{8,4},{12,8},{0,12},{5,1},{9,5},{13,9},{1,13},{6,2},{10,6},{... | collective-permute-start | bytes 786440 | tf_op jit(solution)/shard_map/ppermute | solution.py:52
  143.2 3.6 %collective-permute-start.27 = (bf16[4,256,128]{2,1,0:T(8,128)(2,1)S(1)}, bf16[4,256,128]{2,1,0:T(8,128)(2,1)S(1)}, u32[]{:S(2)}, u32[]{:S(2)}) collective-permute-start(bf16[4,256,128]{2,1,0:T(8,128)(2,1)S(1)} %pad_maximum_fusion.1.refs_7_), channel_id=1, source_target_pairs={{8,0},{12,4},{0,8},{4,12},{9,1},{13,5},{1,9},{5,13},{10,2},{14,6},... | collective-permute-start | bytes 786440 | tf_op jit(solution)/shard_map/ppermute | solution.py:52
  151.6 2.7 %collective-permute-done.27.refs_9_ = bf16[4,256,128]{2,1,0:T(8,128)(2,1)S(1)} collective-permute-done((bf16[4,256,128]{2,1,0:T(8,128)(2,1)S(1)}, bf16[4,256,128]{2,1,0:T(8,128)(2,1)S(1)}, u32[]{:S(2)}, u32[]{:S(2)}) %collective-permute-start.27) | collective-permute-done | bytes 262176 | tf_op jit(solution)/shard_map/ppermute | solution.py:52
  154.3 3.9 %collective-permute-done.28.refs_10_ = bf16[4,256,128]{2,1,0:T(8,128)(2,1)S(1)} collective-permute-done((bf16[4,256,128]{2,1,0:T(8,128)(2,1)S(1)}, bf16[4,256,128]{2,1,0:T(8,128)(2,1)S(1)}, u32[]{:S(2)}, u32[]{:S(2)}) %collective-permute-start.28) | collective-permute-done | bytes 262176 | tf_op jit(solution)/shard_map/ppermute | solution.py:52
  161.2 10.9 %all-gather.1 = bf16[1024,128]{1,0:T(8,128)(2,1)S(1)} all-gather(bf16[256,128]{1,0:T(8,128)(2,1)S(1)} %shard_map.132), channel_id=3, replica_groups=mesh['z_lo'=4,'ring_x'=4,'ring_y'=4,'z_hi'=2,'core'=2] {'z_lo'}, dimensions={0}, use_global_device_ids=true | all-gather | bytes 327680 | tf_op jit(solution)/shard_map/all_gather | solution.py:583
  172.1 2.8 %shard_map.133 = (f32[2,64,1024]{2,1,0:T(8,128)S(1)}, bf16[2,64,1024]{2,1,0:T(8,128)(2,1)S(1)}) custom-call(bf16[4,256,128]{2,1,0:T(8,128)(2,1)S(1)} %bitcast.28, bf16[16,1088,128]{2,1,0:T(8,128)(2,1)} %all-to-all-done.1.weights_ref), custom_call_target="tpu_custom_call" | custom-call | flops 1048576 | bytes 1048576 | tf_op jit(solution)/shard_map/pallas_call | solution.py:425
  174.9 11.5 %collective-permute-start.29 = (bf16[2,64,1024]{2,1,0:T(8,128)(2,1)S(1)}, bf16[2,64,1024]{2,1,0:T(8,128)(2,1)S(1)}, u32[]{:S(2)}, u32[]{:S(2)}) collective-permute-start(bf16[2,64,1024]{2,1,0:T(8,128)(2,1)S(1)} %get-tuple-element.49), channel_id=1, source_target_pairs={{0,1},{1,0},{2,3},{3,2},{4,5},{5,4},{6,7},{7,6},{8,9},{9,8},{10,11... | collective-permute-start | bytes 786440 | tf_op jit(solution)/shard_map/ppermute | solution.py:42
  187.6 2.5 %collective-permute-start.30 = (bf16[64,1024]{1,0:T(8,128)(2,1)S(1)}, bf16[64,1024]{1,0:T(8,128)(2,1)S(1)}, u32[]{:S(2)}, u32[]{:S(2)}) collective-permute-start(bf16[64,1024]{1,0:T(8,128)(2,1)S(1)} %get-tuple-element.50), channel_id=1, source_target_pairs={{0,0},{1,128},{2,64},{3,192},{64,1},{65,129},{66,65},{67,193},{128... | collective-permute-start | bytes 393224 | tf_op jit(solution)/shard_map/ppermute | solution.py:587
  190.1 2.5 %collective-permute-start.31 = (bf16[64,1024]{1,0:T(8,128)(2,1)S(1)}, bf16[64,1024]{1,0:T(8,128)(2,1)S(1)}, u32[]{:S(2)}, u32[]{:S(2)}) collective-permute-start(bf16[64,1024]{1,0:T(8,128)(2,1)S(1)} %get-tuple-element.51), channel_id=1, source_target_pairs={{0,64},{1,192},{2,0},{3,128},{64,65},{65,193},{66,1},{67,129},{128... | collective-permute-start | bytes 393224 | tf_op jit(solution)/shard_map/ppermute | solution.py:587
  193.9 6.6 %collective-permute-done.31.refs_1_ = bf16[64,1024]{1,0:T(8,128)(2,1)S(1)} collective-permute-done((bf16[64,1024]{1,0:T(8,128)(2,1)S(1)}, bf16[64,1024]{1,0:T(8,128)(2,1)S(1)}, u32[]{:S(2)}, u32[]{:S(2)}) %collective-permute-start.31) | collective-permute-done | bytes 131104 | tf_op jit(solution)/shard_map/ppermute | solution.py:587
  (145 shorter events, 49.6 us)
Async XLA Ops:
  0.6 36.1 %collective-permute-start.3 = (bf16[256,1024]{1,0:T(8,128)(2,1)}, bf16[256,1024]{1,0:T(8,128)(2,1)S(1)}, u32[]{:S(2)}, u32[]{:S(2)}) collective-permute-start(bf16[256,1024]{1,0:T(8,128)(2,1)} %refs_0_.1), channel_id=1, source_target_pairs={{0,1},{1,0},{2,3},{3,2},{4,5},{5,4},{6,7},{7,6},{8,9},{9,8},{10,11... | collective-permute-start | bytes 1572872 | tf_op jit(solution)/shard_map/ppermute | solution.py:42
  8.4 28.3 %collective-permute-start = (bf16[256,512]{1,0:T(8,128)(2,1)S(1)}, bf16[256,512]{1,0:T(8,128)(2,1)}, u32[]{:S(2)}, u32[]{:S(2)}) collective-permute-start(bf16[256,512]{1,0:T(8,128)(2,1)S(1)} %get-tuple-element.27.own_ref), channel_id=1, source_target_pairs={{0,4},{4,8},{8,12},{12,16},{16,20},{20,24},{24,28},{28,32},{32,36}... | collective-permute-start | bytes 786440 | tf_op jit(solution)/shard_map/ppermute | solution.py:34
  10.6 26.2 %collective-permute-start.1 = (bf16[256,512]{1,0:T(8,128)(2,1)S(1)}, bf16[256,512]{1,0:T(8,128)(2,1)}, u32[]{:S(2)}, u32[]{:S(2)}) collective-permute-start(bf16[256,512]{1,0:T(8,128)(2,1)S(1)} %get-tuple-element.27.own_ref), channel_id=1, source_target_pairs={{0,8},{4,12},{8,16},{12,20},{16,24},{20,28},{24,32},{28,36},{32,40... | collective-permute-start | bytes 786440 | tf_op jit(solution)/shard_map/ppermute | solution.py:34
  16.8 19.9 %collective-permute-start.4 = (bf16[128,1024]{1,0:T(8,128)(2,1)}, bf16[128,1024]{1,0:T(8,128)(2,1)S(1)}, u32[]{:S(2)}, u32[]{:S(2)}) collective-permute-start(bf16[128,1024]{1,0:T(8,128)(2,1)} %slice.47), channel_id=1, source_target_pairs={{0,2},{2,0},{1,3},{3,1},{4,6},{6,4},{5,7},{7,5},{8,10},{10,8},{9,1... | collective-permute-start | bytes 786440 | tf_op jit(solution)/shard_map/ppermute | solution.py:42
  26.9 17.0 %all-to-all-start = ((bf16[4,208,128]{2,1,0:T(8,128)(2,1)}), bf16[4,208,128]{2,1,0:T(8,128)(2,1)S(1)}, u32[]{:S(2)}, u32[]{:S(2)}) async-start(bf16[4,208,128]{2,1,0:T(8,128)(2,1)} %shard_map.125), calls=%async_computation | async-start | bytes 425984 | tf_op jit(solution)/shard_map/all_to_all | solution.py:38
  31.8 4.9 %collective-permute-start.2 = (bf16[16,1024]{1,0:T(8,128)(2,1)S(1)}, bf16[16,1024]{1,0:T(8,128)(2,1)S(1)}, u32[]{:S(2)}, u32[]{:S(2)}) collective-permute-start(bf16[16,1024]{1,0:T(8,128)(2,1)S(1)} %slice_select_fusion), channel_id=1, source_target_pairs={{4,0},{8,4},{12,8},{16,12},{20,16},{24,20},{28,24},{32,28},{36,32}... | collective-permute-start | bytes 98312 | tf_op jit(solution)/shard_map/ppermute | solution.py:34
  36.8 7.1 %collective-permute-start.5 = (bf16[128,1024]{1,0:T(8,128)(2,1)S(1)}, bf16[128,1024]{1,0:T(8,128)(2,1)S(1)}, u32[]{:S(2)}, u32[]{:S(2)}) collective-permute-start(bf16[128,1024]{1,0:T(8,128)(2,1)S(1)} %collective-permute-done.4.refs_2_), channel_id=1, source_target_pairs={{0,1},{1,0},{2,3},{3,2},{4,5},{5,4},{6,7},{7,6},{8,9},{9,8},{10,11... | collective-permute-start | bytes 786440 | tf_op jit(solution)/shard_map/ppermute | solution.py:42
  47.5 75.2 %all-to-all-start.1 = ((bf16[16,1088,128]{2,1,0:T(8,128)(2,1)}), bf16[16,1088,128]{2,1,0:T(8,128)(2,1)}, u32[]{:S(2)}, u32[]{:S(2)}) async-start(bf16[16,1088,128]{2,1,0:T(8,128)(2,1)} %copy-done), calls=%async_computation.1 | async-start | bytes 8912896 | tf_op jit(solution)/shard_map/all_to_all | solution.py:38
  56.7 25.1 %collective-permute-start.6 = (bf16[128,1024]{1,0:T(8,128)(2,1)S(1)}, bf16[128,1024]{1,0:T(8,128)(2,1)S(1)}, u32[]{:S(2)}, u32[]{:S(2)}) collective-permute-start(bf16[128,1024]{1,0:T(8,128)(2,1)S(1)} %slice.48), channel_id=1, source_target_pairs={{0,2},{2,0},{1,3},{3,1},{4,6},{6,4},{5,7},{7,5},{8,10},{10,8},{9,1... | collective-permute-start | bytes 786440 | tf_op jit(solution)/shard_map/ppermute | solution.py:42
  97.4 6.1 %collective-permute-start.8 = (bf16[64,1024]{1,0:T(8,128)(2,1)S(1)}, bf16[64,1024]{1,0:T(8,128)(2,1)S(1)}, u32[]{:S(2)}, u32[]{:S(2)}) collective-permute-start(bf16[64,1024]{1,0:T(8,128)(2,1)S(1)} %shard_map.127.refs_0_.patches_ref), channel_id=1, source_target_pairs={{0,64},{64,128},{128,192},{192,2},{2,66},{66,130},{130,194},{194,0... | collective-permute-start | bytes 393224 | tf_op jit(solution)/shard_map/ppermute | solution.py:80
  98.7 4.9 %collective-permute-start.9 = (bf16[64,1024]{1,0:T(8,128)(2,1)S(1)}, bf16[64,1024]{1,0:T(8,128)(2,1)S(1)}, u32[]{:S(2)}, u32[]{:S(2)}) collective-permute-start(bf16[64,1024]{1,0:T(8,128)(2,1)S(1)} %shard_map.127.refs_0_.patches_ref), channel_id=1, source_target_pairs={{0,194},{64,0},{128,64},{192,128},{2,192},{66,2},{130,66},{194,130... | collective-permute-start | bytes 393224 | tf_op jit(solution)/shard_map/ppermute | solution.py:80
  103.6 5.4 %collective-permute-start.10 = (bf16[64,1024]{1,0:T(8,128)(2,1)S(1)}, bf16[64,1024]{1,0:T(8,128)(2,1)S(1)}, u32[]{:S(2)}, u32[]{:S(2)}) collective-permute-start(bf16[64,1024]{1,0:T(8,128)(2,1)S(1)} %collective-permute-done.8.refs_1_), channel_id=1, source_target_pairs={{0,64},{64,128},{128,192},{192,2},{2,66},{66,130},{130,194},{194,0... | collective-permute-start | bytes 393224 | tf_op jit(solution)/shard_map/ppermute | solution.py:80
  103.6 5.4 %collective-permute-start.11 = (bf16[64,1024]{1,0:T(8,128)(2,1)S(1)}, bf16[64,1024]{1,0:T(8,128)(2,1)S(1)}, u32[]{:S(2)}, u32[]{:S(2)}) collective-permute-start(bf16[64,1024]{1,0:T(8,128)(2,1)S(1)} %collective-permute-done.9.refs_2_), channel_id=1, source_target_pairs={{0,194},{64,0},{128,64},{192,128},{2,192},{66,2},{130,66},{194,130... | collective-permute-start | bytes 393224 | tf_op jit(solution)/shard_map/ppermute | solution.py:80
  109.0 5.4 %collective-permute-start.12 = (bf16[64,1024]{1,0:T(8,128)(2,1)S(1)}, bf16[64,1024]{1,0:T(8,128)(2,1)S(1)}, u32[]{:S(2)}, u32[]{:S(2)}) collective-permute-start(bf16[64,1024]{1,0:T(8,128)(2,1)S(1)} %collective-permute-done.10.refs_3_), channel_id=1, source_target_pairs={{0,64},{64,128},{128,192},{192,2},{2,66},{66,130},{130,194},{194,0... | collective-permute-start | bytes 393224 | tf_op jit(solution)/shard_map/ppermute | solution.py:80
  109.0 5.4 %collective-permute-start.13 = (bf16[64,1024]{1,0:T(8,128)(2,1)S(1)}, bf16[64,1024]{1,0:T(8,128)(2,1)S(1)}, u32[]{:S(2)}, u32[]{:S(2)}) collective-permute-start(bf16[64,1024]{1,0:T(8,128)(2,1)S(1)} %collective-permute-done.11.refs_4_), channel_id=1, source_target_pairs={{0,194},{64,0},{128,64},{192,128},{2,192},{66,2},{130,66},{194,130... | collective-permute-start | bytes 393224 | tf_op jit(solution)/shard_map/ppermute | solution.py:80
  114.4 4.3 %collective-permute-start.14 = (bf16[32,1024]{1,0:T(8,128)(2,1)S(1)}, bf16[32,1024]{1,0:T(8,128)(2,1)S(1)}, u32[]{:S(2)}, u32[]{:S(2)}) collective-permute-start(bf16[32,1024]{1,0:T(8,128)(2,1)S(1)} %slice.60), channel_id=1, source_target_pairs={{0,64},{64,128},{128,192},{192,2},{2,66},{66,130},{130,194},{194,0... | collective-permute-start | bytes 196616 | tf_op jit(solution)/shard_map/ppermute | solution.py:80
  114.5 4.3 %collective-permute-start.15 = (bf16[32,1024]{1,0:T(8,128)(2,1)S(1)}, bf16[32,1024]{1,0:T(8,128)(2,1)S(1)}, u32[]{:S(2)}, u32[]{:S(2)}) collective-permute-start(bf16[32,1024]{1,0:T(8,128)(2,1)S(1)} %slice.61), channel_id=1, source_target_pairs={{0,194},{64,0},{128,64},{192,128},{2,192},{66,2},{130,66},{194,130... | collective-permute-start | bytes 196616 | tf_op jit(solution)/shard_map/ppermute | solution.py:80
  118.9 9.5 %collective-permute-start.16 = (bf16[256,2048]{1,0:T(8,128)(2,1)S(1)}, bf16[256,2048]{1,0:T(8,128)(2,1)S(1)}, u32[]{:S(2)}, u32[]{:S(2)}) collective-permute-start(bf16[256,2048]{1,0:T(8,128)(2,1)S(1)} %shard_map.128.own_ref), channel_id=1, source_target_pairs={{0,1},{1,0},{2,3},{3,2},{4,5},{5,4},{6,7},{7,6},{8,9},{9,8},{10,11... | collective-permute-start | bytes 3145736 | tf_op jit(solution)/shard_map/ppermute | solution.py:42
  132.4 4.7 %collective-permute-start.24 = (bf16[256,128]{1,0:T(8,128)(2,1)S(1)}, bf16[256,128]{1,0:T(8,128)(2,1)S(1)}, u32[]{:S(2)}, u32[]{:S(2)}) collective-permute-start(bf16[256,128]{1,0:T(8,128)(2,1)S(1)} %get-tuple-element.47), channel_id=1, source_target_pairs={{32,0},{48,16},{0,32},{16,48},{33,1},{49,17},{1,33},{17,49},{34,2}... | collective-permute-start | bytes 196616 | tf_op jit(solution)/shard_map/ppermute | solution.py:52
  133.0 6.1 %collective-permute-start.25 = (bf16[256,128]{1,0:T(8,128)(2,1)S(1)}, bf16[256,128]{1,0:T(8,128)(2,1)S(1)}, u32[]{:S(2)}, u32[]{:S(2)}) collective-permute-start(bf16[256,128]{1,0:T(8,128)(2,1)S(1)} %get-tuple-element.47), channel_id=1, source_target_pairs={{48,0},{0,16},{16,32},{32,48},{49,1},{1,17},{17,33},{33,49},{50,2}... | collective-permute-start | bytes 196616 | tf_op jit(solution)/shard_map/ppermute | solution.py:52
  139.2 11.0 %collective-permute-start.26 = (bf16[4,256,128]{2,1,0:T(8,128)(2,1)S(1)}, bf16[4,256,128]{2,1,0:T(8,128)(2,1)S(1)}, u32[]{:S(2)}, u32[]{:S(2)}) collective-permute-start(bf16[4,256,128]{2,1,0:T(8,128)(2,1)S(1)} %pad_maximum_fusion.1.refs_7_), channel_id=1, source_target_pairs={{4,0},{8,4},{12,8},{0,12},{5,1},{9,5},{13,9},{1,13},{6,2},{10,6},{... | collective-permute-start | bytes 786440 | tf_op jit(solution)/shard_map/ppermute | solution.py:52
  141.7 7.1 %collective-permute-start.17 = (bf16[256,128]{1,0:T(8,128)(2,1)S(1)}, bf16[256,128]{1,0:T(8,128)(2,1)S(1)}, u32[]{:S(2)}, u32[]{:S(2)}) collective-permute-start(bf16[256,128]{1,0:T(8,128)(2,1)S(1)} %get-tuple-element.46), channel_id=1, source_target_pairs={{4,0},{8,4},{12,8},{0,12},{5,1},{9,5},{13,9},{1,13},{6,2},{10,6},{... | collective-permute-start | bytes 196616 | tf_op jit(solution)/shard_map/ppermute | solution.py:52
  141.8 7.5 %collective-permute-start.18 = (bf16[256,128]{1,0:T(8,128)(2,1)S(1)}, bf16[256,128]{1,0:T(8,128)(2,1)S(1)}, u32[]{:S(2)}, u32[]{:S(2)}) collective-permute-start(bf16[256,128]{1,0:T(8,128)(2,1)S(1)} %get-tuple-element.46), channel_id=1, source_target_pairs={{8,0},{12,4},{0,8},{4,12},{9,1},{13,5},{1,9},{5,13},{10,2},{14,6},... | collective-permute-start | bytes 196616 | tf_op jit(solution)/shard_map/ppermute | solution.py:52
  142.5 6.9 %collective-permute-start.19 = (bf16[256,128]{1,0:T(8,128)(2,1)S(1)}, bf16[256,128]{1,0:T(8,128)(2,1)S(1)}, u32[]{:S(2)}, u32[]{:S(2)}) collective-permute-start(bf16[256,128]{1,0:T(8,128)(2,1)S(1)} %get-tuple-element.46), channel_id=1, source_target_pairs={{12,0},{0,4},{4,8},{8,12},{13,1},{1,5},{5,9},{9,13},{14,2},{2,6},{... | collective-permute-start | bytes 196616 | tf_op jit(solution)/shard_map/ppermute | solution.py:52
  143.2 11.2 %collective-permute-start.27 = (bf16[4,256,128]{2,1,0:T(8,128)(2,1)S(1)}, bf16[4,256,128]{2,1,0:T(8,128)(2,1)S(1)}, u32[]{:S(2)}, u32[]{:S(2)}) collective-permute-start(bf16[4,256,128]{2,1,0:T(8,128)(2,1)S(1)} %pad_maximum_fusion.1.refs_7_), channel_id=1, source_target_pairs={{8,0},{12,4},{0,8},{4,12},{9,1},{13,5},{1,9},{5,13},{10,2},{14,6},... | collective-permute-start | bytes 786440 | tf_op jit(solution)/shard_map/ppermute | solution.py:52
  148.8 9.4 %collective-permute-start.28 = (bf16[4,256,128]{2,1,0:T(8,128)(2,1)S(1)}, bf16[4,256,128]{2,1,0:T(8,128)(2,1)S(1)}, u32[]{:S(2)}, u32[]{:S(2)}) collective-permute-start(bf16[4,256,128]{2,1,0:T(8,128)(2,1)S(1)} %pad_maximum_fusion.1.refs_7_), channel_id=1, source_target_pairs={{12,0},{0,4},{4,8},{8,12},{13,1},{1,5},{5,9},{9,13},{14,2},{2,6},{... | collective-permute-start | bytes 786440 | tf_op jit(solution)/shard_map/ppermute | solution.py:52
  149.4 8.8 %collective-permute-start.20 = (bf16[4,256,128]{2,1,0:T(8,128)(2,1)S(1)}, bf16[4,256,128]{2,1,0:T(8,128)(2,1)S(1)}, u32[]{:S(2)}, u32[]{:S(2)}) collective-permute-start(bf16[4,256,128]{2,1,0:T(8,128)(2,1)S(1)} %pad_maximum_fusion.refs_3_), channel_id=1, source_target_pairs={{16,0},{32,16},{48,32},{0,48},{17,1},{33,17},{49,33},{1,49},{18,2}... | collective-permute-start | bytes 786440 | tf_op jit(solution)/shard_map/ppermute | solution.py:52
  149.5 8.7 %collective-permute-start.21 = (bf16[4,256,128]{2,1,0:T(8,128)(2,1)S(1)}, bf16[4,256,128]{2,1,0:T(8,128)(2,1)S(1)}, u32[]{:S(2)}, u32[]{:S(2)}) collective-permute-start(bf16[4,256,128]{2,1,0:T(8,128)(2,1)S(1)} %pad_maximum_fusion.refs_3_), channel_id=1, source_target_pairs={{32,0},{48,16},{0,32},{16,48},{33,1},{49,17},{1,33},{17,49},{34,2}... | collective-permute-start | bytes 786440 | tf_op jit(solution)/shard_map/ppermute | solution.py:52
  150.1 9.0 %collective-permute-start.22 = (bf16[4,256,128]{2,1,0:T(8,128)(2,1)S(1)}, bf16[4,256,128]{2,1,0:T(8,128)(2,1)S(1)}, u32[]{:S(2)}, u32[]{:S(2)}) collective-permute-start(bf16[4,256,128]{2,1,0:T(8,128)(2,1)S(1)} %pad_maximum_fusion.refs_3_), channel_id=1, source_target_pairs={{48,0},{0,16},{16,32},{32,48},{49,1},{1,17},{17,33},{33,49},{50,2}... | collective-permute-start | bytes 786440 | tf_op jit(solution)/shard_map/ppermute | solution.py:52
  174.9 12.6 %collective-permute-start.29 = (bf16[2,64,1024]{2,1,0:T(8,128)(2,1)S(1)}, bf16[2,64,1024]{2,1,0:T(8,128)(2,1)S(1)}, u32[]{:S(2)}, u32[]{:S(2)}) collective-permute-start(bf16[2,64,1024]{2,1,0:T(8,128)(2,1)S(1)} %get-tuple-element.49), channel_id=1, source_target_pairs={{0,1},{1,0},{2,3},{3,2},{4,5},{5,4},{6,7},{7,6},{8,9},{9,8},{10,11... | collective-permute-start | bytes 786440 | tf_op jit(solution)/shard_map/ppermute | solution.py:42
  187.6 6.3 %collective-permute-start.30 = (bf16[64,1024]{1,0:T(8,128)(2,1)S(1)}, bf16[64,1024]{1,0:T(8,128)(2,1)S(1)}, u32[]{:S(2)}, u32[]{:S(2)}) collective-permute-start(bf16[64,1024]{1,0:T(8,128)(2,1)S(1)} %get-tuple-element.50), channel_id=1, source_target_pairs={{0,0},{1,128},{2,64},{3,192},{64,1},{65,129},{66,65},{67,193},{128... | collective-permute-start | bytes 393224 | tf_op jit(solution)/shard_map/ppermute | solution.py:587
  190.1 10.4 %collective-permute-start.31 = (bf16[64,1024]{1,0:T(8,128)(2,1)S(1)}, bf16[64,1024]{1,0:T(8,128)(2,1)S(1)}, u32[]{:S(2)}, u32[]{:S(2)}) collective-permute-start(bf16[64,1024]{1,0:T(8,128)(2,1)S(1)} %get-tuple-element.51), channel_id=1, source_target_pairs={{0,64},{1,192},{2,0},{3,128},{64,65},{65,193},{66,1},{67,129},{128... | collective-permute-start | bytes 393224 | tf_op jit(solution)/shard_map/ppermute | solution.py:587
  (24 other events, 143.5 us)

commit v5 on v4

--- a/solution.py
+++ b/solution.py
@@ -237,7 +237,12 @@
             pl.BlockSpec((2, width, wide), lambda i: (0, 0, i)),
         ],
         out_specs=pl.BlockSpec((slots, wide), lambda i: (0, i)),
-    )(extended, bounds, lift, cross_kv)
+    )(
+        extended,
+        bounds,
+        pltpu.with_memory_space_constraint(lift, pltpu.HBM),
+        pltpu.with_memory_space_constraint(cross_kv, pltpu.HBM),
+    )
 
 
 def placed_rows(pieces):

time: 203 us -> 202 us (level)
  local copies, waits for them, and re-layouts: 24.5 us -> 22.2 us
    unnamed x44 -> x40, local copies, waits for them, and re-layouts: 15.9 us -> 13.6 us
where the time goes in v5:
time: 202 us; the launch traced here: 199 us
  starting transfers between devices  78.4 us (39%)
  waiting for transfers between devices  36 us (18%)
  blocking collectives  33.8 us (17%)
  Pallas kernels  23.7 us (12%)
  local copies, waits for them, and re-layouts  22.2 us (11%)
  between operations  2.98 us (1%)
  other arithmetic  2.1 us (1%)
    ppermute x7, starting transfers between devices, swapped(): return lax.ppermute(value, axis, [(0, 1), (1, 0)])  28.6 us
    all_gather x1, blocking collectives, shards(): attended = lax.all_gather(attended, TP)  23 us
    ppermute x12, waiting for transfers between devices, around_ring(): lax.ppermute(value, axis, [((i + k) % count, i) for i in range(count)])  14.4 us
    unnamed x40, local copies, waits for them, and re-layouts  13.6 us
    ppermute x12, starting transfers between devices, around_ring(): lax.ppermute(value, axis, [((i + k) % count, i) for i in range(count)])  13.1 us
    all_to_all x2, starting transfers between devices, exchanged(): return lax.all_to_all(pieces, axis, split_axis=0, concat_axis=0, tiled=True)  12.6 us
    all_gather x1, blocking collectives, shards(): kept, sent = partial_outputs(lax.all_gather(heads, ZL), by_head)  10.9 us
    ppermute x8, starting transfers between devices, moved(): lax.ppermute(part, (ZL, ZH), [(named(z), named(z + step)) for z in range(...  10.8 us
  transfers between devices with their start and end apart: 34, of which 15 were waited for; matrix products, arithmetic and copies ran while one was open for 5% of the time, Pallas kernels for 8%

profile of v5, /device:TPU:1, one launch (start us, length us, event | category | flops | bytes accessed | tf_op | source)
XLA Modules:
  0.0 199.4 jit_solution(1948729489735710768)
XLA Ops:
  0.6 3.3 %collective-permute-start.3 = (bf16[256,1024]{1,0:T(8,128)(2,1)}, bf16[256,1024]{1,0:T(8,128)(2,1)S(1)}, u32[]{:S(2)}, u32[]{:S(2)}) collective-permute-start(bf16[256,1024]{1,0:T(8,128)(2,1)} %refs_0_.1), channel_id=1, source_target_pairs={{0,1},{1,0},{2,3},{3,2},{4,5},{5,4},{6,7},{7,6},{8,9},{9,8},{10,11... | collective-permute-start | bytes 1572872 | tf_op jit(solution)/shard_map/ppermute | solution.py:42
  8.4 2.2 %collective-permute-start = (bf16[256,512]{1,0:T(8,128)(2,1)S(1)}, bf16[256,512]{1,0:T(8,128)(2,1)}, u32[]{:S(2)}, u32[]{:S(2)}) collective-permute-start(bf16[256,512]{1,0:T(8,128)(2,1)S(1)} %get-tuple-element.27.own_ref), channel_id=1, source_target_pairs={{0,4},{4,8},{8,12},{12,16},{16,20},{20,24},{24,28},{28,32},{32,36}... | collective-permute-start | bytes 786440 | tf_op jit(solution)/shard_map/ppermute | solution.py:34
  10.6 4.5 %collective-permute-start.1 = (bf16[256,512]{1,0:T(8,128)(2,1)S(1)}, bf16[256,512]{1,0:T(8,128)(2,1)}, u32[]{:S(2)}, u32[]{:S(2)}) collective-permute-start(bf16[256,512]{1,0:T(8,128)(2,1)S(1)} %get-tuple-element.27.own_ref), channel_id=1, source_target_pairs={{0,8},{4,12},{8,16},{12,20},{16,24},{20,28},{24,32},{28,36},{32,40... | collective-permute-start | bytes 786440 | tf_op jit(solution)/shard_map/ppermute | solution.py:34
  16.8 6.9 %collective-permute-start.4 = (bf16[128,1024]{1,0:T(8,128)(2,1)}, bf16[128,1024]{1,0:T(8,128)(2,1)S(1)}, u32[]{:S(2)}, u32[]{:S(2)}) collective-permute-start(bf16[128,1024]{1,0:T(8,128)(2,1)} %slice.47), channel_id=1, source_target_pairs={{0,2},{2,0},{1,3},{3,1},{4,6},{6,4},{5,7},{7,5},{8,10},{10,8},{9,1... | collective-permute-start | bytes 786440 | tf_op jit(solution)/shard_map/ppermute | solution.py:42
  26.9 3.4 %all-to-all-start = ((bf16[4,208,128]{2,1,0:T(8,128)(2,1)}), bf16[4,208,128]{2,1,0:T(8,128)(2,1)S(1)}, u32[]{:S(2)}, u32[]{:S(2)}) async-start(bf16[4,208,128]{2,1,0:T(8,128)(2,1)} %shard_map.125), calls=%async_computation | async-start | bytes 425984 | tf_op jit(solution)/shard_map/all_to_all | solution.py:38
  33.1 3.7 %collective-permute-done.2.states_ref.edge_ref = bf16[16,1024]{1,0:T(8,128)(2,1)S(1)} collective-permute-done((bf16[16,1024]{1,0:T(8,128)(2,1)S(1)}, bf16[16,1024]{1,0:T(8,128)(2,1)S(1)}, u32[]{:S(2)}, u32[]{:S(2)}) %collective-permute-start.2) | collective-permute-done | bytes 32800 | tf_op jit(solution)/shard_map/ppermute | solution.py:34
  36.8 1.8 collective-permute-start.5
  40.8 3.0 %shard_map.124 = bf16[272,256]{1,0:T(8,128)(2,1)S(1)} custom-call(s32[1]{0:T(128)} %bitcast.1.anchor_ref, bf16[256,256]{1,0:T(8,128)(2,1)S(1)} %copy-done.17, bf16[16,256]{1,0:T(8,128)(2,1)S(1)} %get-tuple-element.31.mq_ref, bf16[256,512]{1,0:T(8,128)(2,1)} %collective-permute-done.1.far_ref, bf16[256,512]{1,0:T(8,128)(2,1)} %collective-permute-done.near_ref, ...), custom_call_target="tpu_custom_call" | custom-call | flops 1048576 | bytes 1048576 | tf_op jit(solution)/shard_map/pallas_call | solution.py:164
  45.3 2.1 %copy-done = bf16[16,1088,128]{2,1,0:T(8,128)(2,1)} copy-done((bf16[16,1088,128]{2,1,0:T(8,128)(2,1)}, bf16[16,1088,128]{2,1,0:T(8,128)(2,1)S(1)}, u32[]{:S(2)}) %copy-start) | copy-done | bytes 4456472
  47.4 9.2 %all-to-all-start.1 = ((bf16[16,1088,128]{2,1,0:T(8,128)(2,1)}), bf16[16,1088,128]{2,1,0:T(8,128)(2,1)}, u32[]{:S(2)}, u32[]{:S(2)}) async-start(bf16[16,1088,128]{2,1,0:T(8,128)(2,1)} %copy-done), calls=%async_computation.1 | async-start | bytes 8912896 | tf_op jit(solution)/shard_map/all_to_all | solution.py:38
  58.8 23.0 %all-gather = bf16[1088,256]{1,0:T(8,128)(2,1)S(1)} all-gather(bf16[272,256]{1,0:T(8,128)(2,1)S(1)} %shard_map.124), channel_id=2, replica_groups=mesh['z_lo'=4,'ring_x'=4,'ring_y'=4,'z_hi'=2,'core'=2] {'z_hi','core'}, dimensions={0}, use_global_device_ids=true | all-gather | bytes 696320 | tf_op jit(solution)/shard_map/all_gather | solution.py:529
  88.5 7.2 %shard_map.127.refs_0_.patches_ref = bf16[64,1024]{1,0:T(8,128)(2,1)S(1)} custom-call(bf16[272,1024]{1,0:T(8,128)(2,1)S(1)} %shard_map.126.extended_ref, s32[64,4]{1,0:T(8,128)S(1)} %copy-done.15, bf16[1024,1024]{1,0:T(8,128)(2,1)} %lift_ref.1, bf16[2,1024,1024]{2,1,0:T(8,128)(2,1)} %cross_ref.1), custom_call_target="tpu_custom_call" | custom-call | flops 1048576 | bytes 1048576 | tf_op jit(solution)/shard_map/pallas_call | solution.py:228
  98.5 3.4 %collective-permute-done.8.refs_1_ = bf16[64,1024]{1,0:T(8,128)(2,1)S(1)} collective-permute-done((bf16[64,1024]{1,0:T(8,128)(2,1)S(1)}, bf16[64,1024]{1,0:T(8,128)(2,1)S(1)}, u32[]{:S(2)}, u32[]{:S(2)}) %collective-permute-start.8) | collective-permute-done | bytes 131104 | tf_op jit(solution)/shard_map/ppermute | solution.py:80
  101.9 2.7 %collective-permute-start.11 = (bf16[64,1024]{1,0:T(8,128)(2,1)S(1)}, bf16[64,1024]{1,0:T(8,128)(2,1)S(1)}, u32[]{:S(2)}, u32[]{:S(2)}) collective-permute-start(bf16[64,1024]{1,0:T(8,128)(2,1)S(1)} %collective-permute-done.9.refs_2_), channel_id=1, source_target_pairs={{0,194},{64,0},{128,64},{192,128},{2,192},{66,2},{130,66},{194,130... | collective-permute-start | bytes 393224 | tf_op jit(solution)/shard_map/ppermute | solution.py:80
  104.6 2.7 %collective-permute-done.10.refs_3_ = bf16[64,1024]{1,0:T(8,128)(2,1)S(1)} collective-permute-done((bf16[64,1024]{1,0:T(8,128)(2,1)S(1)}, bf16[64,1024]{1,0:T(8,128)(2,1)S(1)}, u32[]{:S(2)}, u32[]{:S(2)}) %collective-permute-start.10) | collective-permute-done | bytes 131104 | tf_op jit(solution)/shard_map/ppermute | solution.py:80
  107.3 2.7 %collective-permute-start.13 = (bf16[64,1024]{1,0:T(8,128)(2,1)S(1)}, bf16[64,1024]{1,0:T(8,128)(2,1)S(1)}, u32[]{:S(2)}, u32[]{:S(2)}) collective-permute-start(bf16[64,1024]{1,0:T(8,128)(2,1)S(1)} %collective-permute-done.11.refs_4_), channel_id=1, source_target_pairs={{0,194},{64,0},{128,64},{192,128},{2,192},{66,2},{130,66},{194,130... | collective-permute-start | bytes 393224 | tf_op jit(solution)/shard_map/ppermute | solution.py:80
  110.3 2.5 %collective-permute-done.12.refs_5_ = bf16[64,1024]{1,0:T(8,128)(2,1)S(1)} collective-permute-done((bf16[64,1024]{1,0:T(8,128)(2,1)S(1)}, bf16[64,1024]{1,0:T(8,128)(2,1)S(1)}, u32[]{:S(2)}, u32[]{:S(2)}) %collective-permute-start.12) | collective-permute-done | bytes 131104 | tf_op jit(solution)/shard_map/ppermute | solution.py:80
  112.8 2.7 %collective-permute-start.15 = (bf16[32,1024]{1,0:T(8,128)(2,1)S(1)}, bf16[32,1024]{1,0:T(8,128)(2,1)S(1)}, u32[]{:S(2)}, u32[]{:S(2)}) collective-permute-start(bf16[32,1024]{1,0:T(8,128)(2,1)S(1)} %slice.61), channel_id=1, source_target_pairs={{0,194},{64,0},{128,64},{192,128},{2,192},{66,2},{130,66},{194,130... | collective-permute-start | bytes 196616 | tf_op jit(solution)/shard_map/ppermute | solution.py:80
  117.2 3.8 %collective-permute-start.16 = (bf16[256,2048]{1,0:T(8,128)(2,1)S(1)}, bf16[256,2048]{1,0:T(8,128)(2,1)S(1)}, u32[]{:S(2)}, u32[]{:S(2)}) collective-permute-start(bf16[256,2048]{1,0:T(8,128)(2,1)S(1)} %shard_map.128.own_ref), channel_id=1, source_target_pairs={{0,1},{1,0},{2,3},{3,2},{4,5},{5,4},{6,7},{7,6},{8,9},{9,8},{10,11... | collective-permute-start | bytes 3145736 | tf_op jit(solution)/shard_map/ppermute | solution.py:42
  123.1 2.8 %shard_map.130.weights_ref = bf16[2,2,1024,384]{3,2,1,0:T(8,128)(2,1)S(1)} custom-call(bf16[16,1088,128]{2,1,0:T(8,128)(2,1)} %all-to-all-done.1.weights_ref), custom_call_target="tpu_custom_call" | custom-call | flops 1048576 | bytes 1048576 | tf_op jit(solution)/shard_map/pallas_call | solution.py:335
  128.2 2.6 %collective-permute-start.23 = (bf16[256,128]{1,0:T(8,128)(2,1)S(1)}, bf16[256,128]{1,0:T(8,128)(2,1)S(1)}, u32[]{:S(2)}, u32[]{:S(2)}) collective-permute-start(bf16[256,128]{1,0:T(8,128)(2,1)S(1)} %get-tuple-element.47), channel_id=1, source_target_pairs={{16,0},{32,16},{48,32},{0,48},{17,1},{33,17},{49,33},{1,49},{18,2}... | collective-permute-start | bytes 196616 | tf_op jit(solution)/shard_map/ppermute | solution.py:52
  132.1 3.3 %collective-permute-done.24 = bf16[256,128]{1,0:T(8,128)(2,1)S(1)} collective-permute-done((bf16[256,128]{1,0:T(8,128)(2,1)S(1)}, bf16[256,128]{1,0:T(8,128)(2,1)S(1)}, u32[]{:S(2)}, u32[]{:S(2)}) %collective-permute-start.24) | collective-permute-done | bytes 65568 | tf_op jit(solution)/shard_map/ppermute | solution.py:52
  137.2 2.4 %collective-permute-start.26 = (bf16[4,256,128]{2,1,0:T(8,128)(2,1)S(1)}, bf16[4,256,128]{2,1,0:T(8,128)(2,1)S(1)}, u32[]{:S(2)}, u32[]{:S(2)}) collective-permute-start(bf16[4,256,128]{2,1,0:T(8,128)(2,1)S(1)} %pad_maximum_fusion.1.refs_7_), channel_id=1, source_target_pairs={{4,0},{8,4},{12,8},{0,12},{5,1},{9,5},{13,9},{1,13},{6,2},{10,6},{... | collective-permute-start | bytes 786440 | tf_op jit(solution)/shard_map/ppermute | solution.py:52
  141.4 3.3 %collective-permute-start.27 = (bf16[4,256,128]{2,1,0:T(8,128)(2,1)S(1)}, bf16[4,256,128]{2,1,0:T(8,128)(2,1)S(1)}, u32[]{:S(2)}, u32[]{:S(2)}) collective-permute-start(bf16[4,256,128]{2,1,0:T(8,128)(2,1)S(1)} %pad_maximum_fusion.1.refs_7_), channel_id=1, source_target_pairs={{8,0},{12,4},{0,8},{4,12},{9,1},{13,5},{1,9},{5,13},{10,2},{14,6},... | collective-permute-start | bytes 786440 | tf_op jit(solution)/shard_map/ppermute | solution.py:52
  150.0 6.4 %collective-permute-done.28.refs_10_ = bf16[4,256,128]{2,1,0:T(8,128)(2,1)S(1)} collective-permute-done((bf16[4,256,128]{2,1,0:T(8,128)(2,1)S(1)}, bf16[4,256,128]{2,1,0:T(8,128)(2,1)S(1)}, u32[]{:S(2)}, u32[]{:S(2)}) %collective-permute-start.28) | collective-permute-done | bytes 262176 | tf_op jit(solution)/shard_map/ppermute | solution.py:52
  156.4 2.1 %shard_map.132 = bf16[256,128]{1,0:T(8,128)(2,1)S(1)} custom-call(bf16[256,128]{1,0:T(8,128)(2,1)S(1)} %get-tuple-element.45.refs_0_, s32[256,1]{1,0:T(8,128)S(1)} %add.161.refs_1_, s32[16,256]{1,0:T(8,128)S(1)} %add_select_fusion.refs_2_, bf16[4,256,128]{2,1,0:T(8,128)(2,1)S(1)} %pad_maximum_fusion.refs_3_, ...), custom_call_target="tpu_custom_call" | custom-call | flops 1048576 | bytes 1048576 | tf_op jit(solution)/shard_map/pallas_call | solution.py:398
  158.5 10.9 %all-gather.1 = bf16[1024,128]{1,0:T(8,128)(2,1)S(1)} all-gather(bf16[256,128]{1,0:T(8,128)(2,1)S(1)} %shard_map.132), channel_id=3, replica_groups=mesh['z_lo'=4,'ring_x'=4,'ring_y'=4,'z_hi'=2,'core'=2] {'z_lo'}, dimensions={0}, use_global_device_ids=true | all-gather | bytes 327680 | tf_op jit(solution)/shard_map/all_gather | solution.py:588
  169.4 2.8 %shard_map.133 = (f32[2,64,1024]{2,1,0:T(8,128)S(1)}, bf16[2,64,1024]{2,1,0:T(8,128)(2,1)S(1)}) custom-call(bf16[4,256,128]{2,1,0:T(8,128)(2,1)S(1)} %bitcast.28, bf16[16,1088,128]{2,1,0:T(8,128)(2,1)} %all-to-all-done.1.weights_ref), custom_call_target="tpu_custom_call" | custom-call | flops 1048576 | bytes 1048576 | tf_op jit(solution)/shard_map/pallas_call | solution.py:430
  172.2 12.4 %collective-permute-start.29 = (bf16[2,64,1024]{2,1,0:T(8,128)(2,1)S(1)}, bf16[2,64,1024]{2,1,0:T(8,128)(2,1)S(1)}, u32[]{:S(2)}, u32[]{:S(2)}) collective-permute-start(bf16[2,64,1024]{2,1,0:T(8,128)(2,1)S(1)} %get-tuple-element.49), channel_id=1, source_target_pairs={{0,1},{1,0},{2,3},{3,2},{4,5},{5,4},{6,7},{7,6},{8,9},{9,8},{10,11... | collective-permute-start | bytes 786440 | tf_op jit(solution)/shard_map/ppermute | solution.py:42
  185.8 2.5 %collective-permute-start.30 = (bf16[64,1024]{1,0:T(8,128)(2,1)S(1)}, bf16[64,1024]{1,0:T(8,128)(2,1)S(1)}, u32[]{:S(2)}, u32[]{:S(2)}) collective-permute-start(bf16[64,1024]{1,0:T(8,128)(2,1)S(1)} %get-tuple-element.50), channel_id=1, source_target_pairs={{0,0},{1,128},{2,64},{3,192},{64,1},{65,129},{66,65},{67,193},{128... | collective-permute-start | bytes 393224 | tf_op jit(solution)/shard_map/ppermute | solution.py:592
  188.3 2.8 %collective-permute-start.31 = (bf16[64,1024]{1,0:T(8,128)(2,1)S(1)}, bf16[64,1024]{1,0:T(8,128)(2,1)S(1)}, u32[]{:S(2)}, u32[]{:S(2)}) collective-permute-start(bf16[64,1024]{1,0:T(8,128)(2,1)S(1)} %get-tuple-element.51), channel_id=1, source_target_pairs={{0,64},{1,192},{2,0},{3,128},{64,65},{65,193},{66,1},{67,129},{128... | collective-permute-start | bytes 393224 | tf_op jit(solution)/shard_map/ppermute | solution.py:592
  192.1 6.6 %collective-permute-done.31.refs_1_ = bf16[64,1024]{1,0:T(8,128)(2,1)S(1)} collective-permute-done((bf16[64,1024]{1,0:T(8,128)(2,1)S(1)}, bf16[64,1024]{1,0:T(8,128)(2,1)S(1)}, u32[]{:S(2)}, u32[]{:S(2)}) %collective-permute-start.31) | collective-permute-done | bytes 131104 | tf_op jit(solution)/shard_map/ppermute | solution.py:592
  (141 shorter events, 44.8 us)
Async XLA Ops:
  0.6 36.1 %collective-permute-start.3 = (bf16[256,1024]{1,0:T(8,128)(2,1)}, bf16[256,1024]{1,0:T(8,128)(2,1)S(1)}, u32[]{:S(2)}, u32[]{:S(2)}) collective-permute-start(bf16[256,1024]{1,0:T(8,128)(2,1)} %refs_0_.1), channel_id=1, source_target_pairs={{0,1},{1,0},{2,3},{3,2},{4,5},{5,4},{6,7},{7,6},{8,9},{9,8},{10,11... | collective-permute-start | bytes 1572872 | tf_op jit(solution)/shard_map/ppermute | solution.py:42
  8.4 28.3 %collective-permute-start = (bf16[256,512]{1,0:T(8,128)(2,1)S(1)}, bf16[256,512]{1,0:T(8,128)(2,1)}, u32[]{:S(2)}, u32[]{:S(2)}) collective-permute-start(bf16[256,512]{1,0:T(8,128)(2,1)S(1)} %get-tuple-element.27.own_ref), channel_id=1, source_target_pairs={{0,4},{4,8},{8,12},{12,16},{16,20},{20,24},{24,28},{28,32},{32,36}... | collective-permute-start | bytes 786440 | tf_op jit(solution)/shard_map/ppermute | solution.py:34
  10.6 26.1 %collective-permute-start.1 = (bf16[256,512]{1,0:T(8,128)(2,1)S(1)}, bf16[256,512]{1,0:T(8,128)(2,1)}, u32[]{:S(2)}, u32[]{:S(2)}) collective-permute-start(bf16[256,512]{1,0:T(8,128)(2,1)S(1)} %get-tuple-element.27.own_ref), channel_id=1, source_target_pairs={{0,8},{4,12},{8,16},{12,20},{16,24},{20,28},{24,32},{28,36},{32,40... | collective-permute-start | bytes 786440 | tf_op jit(solution)/shard_map/ppermute | solution.py:34
  16.8 19.9 %collective-permute-start.4 = (bf16[128,1024]{1,0:T(8,128)(2,1)}, bf16[128,1024]{1,0:T(8,128)(2,1)S(1)}, u32[]{:S(2)}, u32[]{:S(2)}) collective-permute-start(bf16[128,1024]{1,0:T(8,128)(2,1)} %slice.47), channel_id=1, source_target_pairs={{0,2},{2,0},{1,3},{3,1},{4,6},{6,4},{5,7},{7,5},{8,10},{10,8},{9,1... | collective-permute-start | bytes 786440 | tf_op jit(solution)/shard_map/ppermute | solution.py:42
  26.9 17.0 %all-to-all-start = ((bf16[4,208,128]{2,1,0:T(8,128)(2,1)}), bf16[4,208,128]{2,1,0:T(8,128)(2,1)S(1)}, u32[]{:S(2)}, u32[]{:S(2)}) async-start(bf16[4,208,128]{2,1,0:T(8,128)(2,1)} %shard_map.125), calls=%async_computation | async-start | bytes 425984 | tf_op jit(solution)/shard_map/all_to_all | solution.py:38
  31.8 4.9 %collective-permute-start.2 = (bf16[16,1024]{1,0:T(8,128)(2,1)S(1)}, bf16[16,1024]{1,0:T(8,128)(2,1)S(1)}, u32[]{:S(2)}, u32[]{:S(2)}) collective-permute-start(bf16[16,1024]{1,0:T(8,128)(2,1)S(1)} %slice_select_fusion), channel_id=1, source_target_pairs={{4,0},{8,4},{12,8},{16,12},{20,16},{24,20},{28,24},{32,28},{36,32}... | collective-permute-start | bytes 98312 | tf_op jit(solution)/shard_map/ppermute | solution.py:34
  36.8 7.1 %collective-permute-start.5 = (bf16[128,1024]{1,0:T(8,128)(2,1)S(1)}, bf16[128,1024]{1,0:T(8,128)(2,1)S(1)}, u32[]{:S(2)}, u32[]{:S(2)}) collective-permute-start(bf16[128,1024]{1,0:T(8,128)(2,1)S(1)} %collective-permute-done.4.refs_2_), channel_id=1, source_target_pairs={{0,1},{1,0},{2,3},{3,2},{4,5},{5,4},{6,7},{7,6},{8,9},{9,8},{10,11... | collective-permute-start | bytes 786440 | tf_op jit(solution)/shard_map/ppermute | solution.py:42
  47.4 73.6 %all-to-all-start.1 = ((bf16[16,1088,128]{2,1,0:T(8,128)(2,1)}), bf16[16,1088,128]{2,1,0:T(8,128)(2,1)}, u32[]{:S(2)}, u32[]{:S(2)}) async-start(bf16[16,1088,128]{2,1,0:T(8,128)(2,1)} %copy-done), calls=%async_computation.1 | async-start | bytes 8912896 | tf_op jit(solution)/shard_map/all_to_all | solution.py:38
  56.7 25.1 %collective-permute-start.6 = (bf16[128,1024]{1,0:T(8,128)(2,1)S(1)}, bf16[128,1024]{1,0:T(8,128)(2,1)S(1)}, u32[]{:S(2)}, u32[]{:S(2)}) collective-permute-start(bf16[128,1024]{1,0:T(8,128)(2,1)S(1)} %slice.48), channel_id=1, source_target_pairs={{0,2},{2,0},{1,3},{3,1},{4,6},{6,4},{5,7},{7,5},{8,10},{10,8},{9,1... | collective-permute-start | bytes 786440 | tf_op jit(solution)/shard_map/ppermute | solution.py:42
  95.8 6.1 %collective-permute-start.8 = (bf16[64,1024]{1,0:T(8,128)(2,1)S(1)}, bf16[64,1024]{1,0:T(8,128)(2,1)S(1)}, u32[]{:S(2)}, u32[]{:S(2)}) collective-permute-start(bf16[64,1024]{1,0:T(8,128)(2,1)S(1)} %shard_map.127.refs_0_.patches_ref), channel_id=1, source_target_pairs={{0,64},{64,128},{128,192},{192,2},{2,66},{66,130},{130,194},{194,0... | collective-permute-start | bytes 393224 | tf_op jit(solution)/shard_map/ppermute | solution.py:80
  97.0 4.9 %collective-permute-start.9 = (bf16[64,1024]{1,0:T(8,128)(2,1)S(1)}, bf16[64,1024]{1,0:T(8,128)(2,1)S(1)}, u32[]{:S(2)}, u32[]{:S(2)}) collective-permute-start(bf16[64,1024]{1,0:T(8,128)(2,1)S(1)} %shard_map.127.refs_0_.patches_ref), channel_id=1, source_target_pairs={{0,194},{64,0},{128,64},{192,128},{2,192},{66,2},{130,66},{194,130... | collective-permute-start | bytes 393224 | tf_op jit(solution)/shard_map/ppermute | solution.py:80
  101.9 5.4 %collective-permute-start.10 = (bf16[64,1024]{1,0:T(8,128)(2,1)S(1)}, bf16[64,1024]{1,0:T(8,128)(2,1)S(1)}, u32[]{:S(2)}, u32[]{:S(2)}) collective-permute-start(bf16[64,1024]{1,0:T(8,128)(2,1)S(1)} %collective-permute-done.8.refs_1_), channel_id=1, source_target_pairs={{0,64},{64,128},{128,192},{192,2},{2,66},{66,130},{130,194},{194,0... | collective-permute-start | bytes 393224 | tf_op jit(solution)/shard_map/ppermute | solution.py:80
  101.9 5.4 %collective-permute-start.11 = (bf16[64,1024]{1,0:T(8,128)(2,1)S(1)}, bf16[64,1024]{1,0:T(8,128)(2,1)S(1)}, u32[]{:S(2)}, u32[]{:S(2)}) collective-permute-start(bf16[64,1024]{1,0:T(8,128)(2,1)S(1)} %collective-permute-done.9.refs_2_), channel_id=1, source_target_pairs={{0,194},{64,0},{128,64},{192,128},{2,192},{66,2},{130,66},{194,130... | collective-permute-start | bytes 393224 | tf_op jit(solution)/shard_map/ppermute | solution.py:80
  107.3 5.4 %collective-permute-start.12 = (bf16[64,1024]{1,0:T(8,128)(2,1)S(1)}, bf16[64,1024]{1,0:T(8,128)(2,1)S(1)}, u32[]{:S(2)}, u32[]{:S(2)}) collective-permute-start(bf16[64,1024]{1,0:T(8,128)(2,1)S(1)} %collective-permute-done.10.refs_3_), channel_id=1, source_target_pairs={{0,64},{64,128},{128,192},{192,2},{2,66},{66,130},{130,194},{194,0... | collective-permute-start | bytes 393224 | tf_op jit(solution)/shard_map/ppermute | solution.py:80
  107.3 5.4 %collective-permute-start.13 = (bf16[64,1024]{1,0:T(8,128)(2,1)S(1)}, bf16[64,1024]{1,0:T(8,128)(2,1)S(1)}, u32[]{:S(2)}, u32[]{:S(2)}) collective-permute-start(bf16[64,1024]{1,0:T(8,128)(2,1)S(1)} %collective-permute-done.11.refs_4_), channel_id=1, source_target_pairs={{0,194},{64,0},{128,64},{192,128},{2,192},{66,2},{130,66},{194,130... | collective-permute-start | bytes 393224 | tf_op jit(solution)/shard_map/ppermute | solution.py:80
  112.7 4.3 %collective-permute-start.14 = (bf16[32,1024]{1,0:T(8,128)(2,1)S(1)}, bf16[32,1024]{1,0:T(8,128)(2,1)S(1)}, u32[]{:S(2)}, u32[]{:S(2)}) collective-permute-start(bf16[32,1024]{1,0:T(8,128)(2,1)S(1)} %slice.60), channel_id=1, source_target_pairs={{0,64},{64,128},{128,192},{192,2},{2,66},{66,130},{130,194},{194,0... | collective-permute-start | bytes 196616 | tf_op jit(solution)/shard_map/ppermute | solution.py:80
  112.8 4.3 %collective-permute-start.15 = (bf16[32,1024]{1,0:T(8,128)(2,1)S(1)}, bf16[32,1024]{1,0:T(8,128)(2,1)S(1)}, u32[]{:S(2)}, u32[]{:S(2)}) collective-permute-start(bf16[32,1024]{1,0:T(8,128)(2,1)S(1)} %slice.61), channel_id=1, source_target_pairs={{0,194},{64,0},{128,64},{192,128},{2,192},{66,2},{130,66},{194,130... | collective-permute-start | bytes 196616 | tf_op jit(solution)/shard_map/ppermute | solution.py:80
  117.2 9.5 %collective-permute-start.16 = (bf16[256,2048]{1,0:T(8,128)(2,1)S(1)}, bf16[256,2048]{1,0:T(8,128)(2,1)S(1)}, u32[]{:S(2)}, u32[]{:S(2)}) collective-permute-start(bf16[256,2048]{1,0:T(8,128)(2,1)S(1)} %shard_map.128.own_ref), channel_id=1, source_target_pairs={{0,1},{1,0},{2,3},{3,2},{4,5},{5,4},{6,7},{7,6},{8,9},{9,8},{10,11... | collective-permute-start | bytes 3145736 | tf_op jit(solution)/shard_map/ppermute | solution.py:42
  130.8 4.7 %collective-permute-start.24 = (bf16[256,128]{1,0:T(8,128)(2,1)S(1)}, bf16[256,128]{1,0:T(8,128)(2,1)S(1)}, u32[]{:S(2)}, u32[]{:S(2)}) collective-permute-start(bf16[256,128]{1,0:T(8,128)(2,1)S(1)} %get-tuple-element.47), channel_id=1, source_target_pairs={{32,0},{48,16},{0,32},{16,48},{33,1},{49,17},{1,33},{17,49},{34,2}... | collective-permute-start | bytes 196616 | tf_op jit(solution)/shard_map/ppermute | solution.py:52
  131.4 5.8 %collective-permute-start.25 = (bf16[256,128]{1,0:T(8,128)(2,1)S(1)}, bf16[256,128]{1,0:T(8,128)(2,1)S(1)}, u32[]{:S(2)}, u32[]{:S(2)}) collective-permute-start(bf16[256,128]{1,0:T(8,128)(2,1)S(1)} %get-tuple-element.47), channel_id=1, source_target_pairs={{48,0},{0,16},{16,32},{32,48},{49,1},{1,17},{17,33},{33,49},{50,2}... | collective-permute-start | bytes 196616 | tf_op jit(solution)/shard_map/ppermute | solution.py:52
  137.2 10.1 %collective-permute-start.26 = (bf16[4,256,128]{2,1,0:T(8,128)(2,1)S(1)}, bf16[4,256,128]{2,1,0:T(8,128)(2,1)S(1)}, u32[]{:S(2)}, u32[]{:S(2)}) collective-permute-start(bf16[4,256,128]{2,1,0:T(8,128)(2,1)S(1)} %pad_maximum_fusion.1.refs_7_), channel_id=1, source_target_pairs={{4,0},{8,4},{12,8},{0,12},{5,1},{9,5},{13,9},{1,13},{6,2},{10,6},{... | collective-permute-start | bytes 786440 | tf_op jit(solution)/shard_map/ppermute | solution.py:52
  139.6 5.8 %collective-permute-start.17 = (bf16[256,128]{1,0:T(8,128)(2,1)S(1)}, bf16[256,128]{1,0:T(8,128)(2,1)S(1)}, u32[]{:S(2)}, u32[]{:S(2)}) collective-permute-start(bf16[256,128]{1,0:T(8,128)(2,1)S(1)} %get-tuple-element.46), channel_id=1, source_target_pairs={{4,0},{8,4},{12,8},{0,12},{5,1},{9,5},{13,9},{1,13},{6,2},{10,6},{... | collective-permute-start | bytes 196616 | tf_op jit(solution)/shard_map/ppermute | solution.py:52
  140.7 4.8 %collective-permute-start.18 = (bf16[256,128]{1,0:T(8,128)(2,1)S(1)}, bf16[256,128]{1,0:T(8,128)(2,1)S(1)}, u32[]{:S(2)}, u32[]{:S(2)}) collective-permute-start(bf16[256,128]{1,0:T(8,128)(2,1)S(1)} %get-tuple-element.46), channel_id=1, source_target_pairs={{8,0},{12,4},{0,8},{4,12},{9,1},{13,5},{1,9},{5,13},{10,2},{14,6},... | collective-permute-start | bytes 196616 | tf_op jit(solution)/shard_map/ppermute | solution.py:52
  140.7 5.1 %collective-permute-start.19 = (bf16[256,128]{1,0:T(8,128)(2,1)S(1)}, bf16[256,128]{1,0:T(8,128)(2,1)S(1)}, u32[]{:S(2)}, u32[]{:S(2)}) collective-permute-start(bf16[256,128]{1,0:T(8,128)(2,1)S(1)} %get-tuple-element.46), channel_id=1, source_target_pairs={{12,0},{0,4},{4,8},{8,12},{13,1},{1,5},{5,9},{9,13},{14,2},{2,6},{... | collective-permute-start | bytes 196616 | tf_op jit(solution)/shard_map/ppermute | solution.py:52
  141.4 8.6 %collective-permute-start.27 = (bf16[4,256,128]{2,1,0:T(8,128)(2,1)S(1)}, bf16[4,256,128]{2,1,0:T(8,128)(2,1)S(1)}, u32[]{:S(2)}, u32[]{:S(2)}) collective-permute-start(bf16[4,256,128]{2,1,0:T(8,128)(2,1)S(1)} %pad_maximum_fusion.1.refs_7_), channel_id=1, source_target_pairs={{8,0},{12,4},{0,8},{4,12},{9,1},{13,5},{1,9},{5,13},{10,2},{14,6},... | collective-permute-start | bytes 786440 | tf_op jit(solution)/shard_map/ppermute | solution.py:52
  145.4 11.0 %collective-permute-start.28 = (bf16[4,256,128]{2,1,0:T(8,128)(2,1)S(1)}, bf16[4,256,128]{2,1,0:T(8,128)(2,1)S(1)}, u32[]{:S(2)}, u32[]{:S(2)}) collective-permute-start(bf16[4,256,128]{2,1,0:T(8,128)(2,1)S(1)} %pad_maximum_fusion.1.refs_7_), channel_id=1, source_target_pairs={{12,0},{0,4},{4,8},{8,12},{13,1},{1,5},{5,9},{9,13},{14,2},{2,6},{... | collective-permute-start | bytes 786440 | tf_op jit(solution)/shard_map/ppermute | solution.py:52
  145.9 10.5 %collective-permute-start.20 = (bf16[4,256,128]{2,1,0:T(8,128)(2,1)S(1)}, bf16[4,256,128]{2,1,0:T(8,128)(2,1)S(1)}, u32[]{:S(2)}, u32[]{:S(2)}) collective-permute-start(bf16[4,256,128]{2,1,0:T(8,128)(2,1)S(1)} %pad_maximum_fusion.refs_3_), channel_id=1, source_target_pairs={{16,0},{32,16},{48,32},{0,48},{17,1},{33,17},{49,33},{1,49},{18,2}... | collective-permute-start | bytes 786440 | tf_op jit(solution)/shard_map/ppermute | solution.py:52
  146.5 9.9 %collective-permute-start.21 = (bf16[4,256,128]{2,1,0:T(8,128)(2,1)S(1)}, bf16[4,256,128]{2,1,0:T(8,128)(2,1)S(1)}, u32[]{:S(2)}, u32[]{:S(2)}) collective-permute-start(bf16[4,256,128]{2,1,0:T(8,128)(2,1)S(1)} %pad_maximum_fusion.refs_3_), channel_id=1, source_target_pairs={{32,0},{48,16},{0,32},{16,48},{33,1},{49,17},{1,33},{17,49},{34,2}... | collective-permute-start | bytes 786440 | tf_op jit(solution)/shard_map/ppermute | solution.py:52
  147.4 9.0 %collective-permute-start.22 = (bf16[4,256,128]{2,1,0:T(8,128)(2,1)S(1)}, bf16[4,256,128]{2,1,0:T(8,128)(2,1)S(1)}, u32[]{:S(2)}, u32[]{:S(2)}) collective-permute-start(bf16[4,256,128]{2,1,0:T(8,128)(2,1)S(1)} %pad_maximum_fusion.refs_3_), channel_id=1, source_target_pairs={{48,0},{0,16},{16,32},{32,48},{49,1},{1,17},{17,33},{33,49},{50,2}... | collective-permute-start | bytes 786440 | tf_op jit(solution)/shard_map/ppermute | solution.py:52
  172.2 13.6 %collective-permute-start.29 = (bf16[2,64,1024]{2,1,0:T(8,128)(2,1)S(1)}, bf16[2,64,1024]{2,1,0:T(8,128)(2,1)S(1)}, u32[]{:S(2)}, u32[]{:S(2)}) collective-permute-start(bf16[2,64,1024]{2,1,0:T(8,128)(2,1)S(1)} %get-tuple-element.49), channel_id=1, source_target_pairs={{0,1},{1,0},{2,3},{3,2},{4,5},{5,4},{6,7},{7,6},{8,9},{9,8},{10,11... | collective-permute-start | bytes 786440 | tf_op jit(solution)/shard_map/ppermute | solution.py:42
  185.8 6.3 %collective-permute-start.30 = (bf16[64,1024]{1,0:T(8,128)(2,1)S(1)}, bf16[64,1024]{1,0:T(8,128)(2,1)S(1)}, u32[]{:S(2)}, u32[]{:S(2)}) collective-permute-start(bf16[64,1024]{1,0:T(8,128)(2,1)S(1)} %get-tuple-element.50), channel_id=1, source_target_pairs={{0,0},{1,128},{2,64},{3,192},{64,1},{65,129},{66,65},{67,193},{128... | collective-permute-start | bytes 393224 | tf_op jit(solution)/shard_map/ppermute | solution.py:592
  188.3 10.3 %collective-permute-start.31 = (bf16[64,1024]{1,0:T(8,128)(2,1)S(1)}, bf16[64,1024]{1,0:T(8,128)(2,1)S(1)}, u32[]{:S(2)}, u32[]{:S(2)}) collective-permute-start(bf16[64,1024]{1,0:T(8,128)(2,1)S(1)} %get-tuple-element.51), channel_id=1, source_target_pairs={{0,64},{1,192},{2,0},{3,128},{64,65},{65,193},{66,1},{67,129},{128... | collective-permute-start | bytes 393224 | tf_op jit(solution)/shard_map/ppermute | solution.py:592
  (22 other events, 136.6 us)
